TPU v7x, 512 devices: a whole 4x4x16 slice. The times are simulated.
512 devices in a mesh: seq: 128 (over y, z, core), head: 4 (over x).
Axes of the slice: x: 4, y: 4, z: 16, core: 2. Of those that a mesh axis runs over, the one named last changes fastest.
Arguments:
- queries: bfloat16 [65536, 2048], P('seq', 'head'), may hold values from -6 to 6
- key_vectors: bfloat16 [65536, 2048], P('seq', 'head'), may hold values from -6 to 6
- values: bfloat16 [65536, 2048], P('seq', 'head'), may hold values from -6 to 6
- out_weight: bfloat16 [2048, 2048], P('head', 'seq'), may hold values from -4 to 4
Outputs:
- mixed: bfloat16 [65536, 2048], P('seq', 'head')
All inputs are finite; a program needn't handle non-finite values.
Results may differ from a plain program's by a relative error of at most 0.0095.
Values may be sent and summed in bfloat16 or wider, within the bound.
No kernel may reach another device: no remote copies, remote signals or barrier semaphores. Data moves between devices by JAX's collectives and lax.ppermute only.
A program may use at most 64 MiB of HBM per device.

v0:
```python
import math

import jax
import jax.numpy as jnp
from jax import lax
from jax.sharding import PartitionSpec as P

HEAD_DIM = 128
BLOCK = 128
LEVELS = 5


def partner(value, axis, stride):
    mask = 2**stride
    pairs = [(source, source ^ mask) for source in range(lax.axis_size(axis))]
    return lax.ppermute(value, axis, pairs)


def pool_mean(array_in):
    paired = array_in.astype(jnp.float32).reshape(array_in.shape[0] // 2, 2, array_in.shape[1])
    return ((paired[:, 0] + paired[:, 1]) * 0.5).astype(jnp.bfloat16)


def pool_sum(array_in):
    paired = array_in.astype(jnp.float32).reshape(array_in.shape[0] // 2, 2, array_in.shape[1])
    return (paired[:, 0] + paired[:, 1]).astype(jnp.bfloat16)


def to_blocks(array_in, head_count, block_rows):
    return array_in.reshape(-1, block_rows, head_count, array_in.shape[1] // head_count)


def swap_pairs(blocked):
    block_count = blocked.shape[0]
    return blocked.reshape((block_count // 2, 2) + blocked.shape[1:])[:, ::-1].reshape(
        blocked.shape
    )


def level_terms(
    blocked_query_rows, blocked_key_rows, blocked_value_rows, weight, logit_scale_factor
):
    attention_logits = (
        jnp.einsum(
            "bqhd,bkhd->bhqk",
            blocked_query_rows,
            blocked_key_rows,
            preferred_element_type=jnp.float32,
        )
        * logit_scale_factor
    )
    peak_score = jnp.max(attention_logits, axis=-1)
    expo = jnp.exp(attention_logits - peak_score[..., None])
    mass = weight * jnp.sum(expo, axis=-1)
    weighted_value_sum = jnp.einsum(
        "bhqk,bkhd->bqhd",
        expo.astype(jnp.bfloat16),
        blocked_value_rows,
        preferred_element_type=jnp.float32,
    )
    head_count = blocked_query_rows.shape[2]
    peak_rows = jnp.transpose(peak_score, (0, 2, 1)).reshape(-1, head_count)
    mass_rows = jnp.transpose(mass, (0, 2, 1)).reshape(-1, head_count)
    return (
        peak_rows,
        mass_rows,
        weighted_value_sum.reshape(-1, head_count, weighted_value_sum.shape[3]),
    )


def merge_level(running, terms, factor):
    running_max, running_sum, running_out = running
    peak_rows = jnp.repeat(terms[0], factor, axis=0)
    mass_rows = jnp.repeat(terms[1], factor, axis=0)
    weighted_value_sum = jnp.repeat(terms[2], factor, axis=0)
    newest = jnp.maximum(running_max, peak_rows)
    keep_old = jnp.exp(running_max - newest)
    keep_new = jnp.exp(peak_rows - newest)
    return (
        newest,
        running_sum * keep_old + mass_rows * keep_new,
        running_out * keep_old[..., None] + weighted_value_sum * keep_new[..., None],
    )


def body(queries, key_vectors, values, out_weight):
    row_count, col_count = queries.shape
    head_count = col_count // HEAD_DIM
    logit_scale_factor = 1.0 / math.sqrt(HEAD_DIM)
    seq_index = lax.axis_index("seq")
    blocked_key_rows = to_blocks(key_vectors, head_count, BLOCK)
    blocked_value_rows = to_blocks(values, head_count, BLOCK)
    near_keys = jnp.concatenate([blocked_key_rows, swap_pairs(blocked_key_rows)], axis=1)
    near_values = jnp.concatenate([blocked_value_rows, swap_pairs(blocked_value_rows)], axis=1)
    running = level_terms(
        to_blocks(queries, head_count, BLOCK), near_keys, near_values, 1.0, logit_scale_factor
    )
    level_queries, level_keys, level_values = (queries, key_vectors, values)
    far_keys, far_values = (key_vectors, values)
    is_local = True
    partner_bit = 0
    for coarse_level in range(1, LEVELS + 1):
        level_queries = pool_mean(level_queries)
        if is_local:
            level_keys = pool_mean(level_keys)
            level_values = pool_sum(level_values)
            is_local = level_keys.shape[0] >= 2 * BLOCK
        else:
            leading = seq_index >> partner_bit - 1 & 1 == 0
            level_keys = pool_mean(
                jnp.concatenate(
                    [
                        jnp.where(leading, level_keys, far_keys),
                        jnp.where(leading, far_keys, level_keys),
                    ],
                    axis=0,
                )
            )
            level_values = pool_sum(
                jnp.concatenate(
                    [
                        jnp.where(leading, level_values, far_values),
                        jnp.where(leading, far_values, level_values),
                    ],
                    axis=0,
                )
            )
        if is_local:
            blocked_key_rows = swap_pairs(to_blocks(level_keys, head_count, BLOCK))
            blocked_value_rows = swap_pairs(to_blocks(level_values, head_count, BLOCK))
        else:
            far_keys, far_values = partner((level_keys, level_values), "seq", partner_bit)
            partner_bit += 1
            blocked_key_rows = to_blocks(far_keys, head_count, BLOCK)
            blocked_value_rows = to_blocks(far_values, head_count, BLOCK)
        blocked_query_rows = to_blocks(
            level_queries, head_count, level_queries.shape[0] // blocked_key_rows.shape[0]
        )
        terms = level_terms(
            blocked_query_rows,
            blocked_key_rows,
            blocked_value_rows,
            2.0**coarse_level,
            logit_scale_factor,
        )
        running = merge_level(running, terms, 2**coarse_level)
    attended = (
        (running[2] / running[1][..., None]).reshape(row_count, col_count).astype(jnp.bfloat16)
    )
    partial_terms = jnp.dot(
        attended,
        lax.all_gather(out_weight, "seq", axis=1, tiled=True),
        preferred_element_type=jnp.float32,
    )
    rounded_terms = partial_terms.astype(jnp.bfloat16).astype(jnp.float32)
    mixed = lax.psum_scatter(
        rounded_terms.astype(jnp.bfloat16), "head", scatter_dimension=1, tiled=True
    )
    return mixed


def solution(mesh):
    in_specs = (P("seq", "head"), P("seq", "head"), P("seq", "head"), P("head", "seq"))
    out_specs = P("seq", "head")
    return jax.shard_map(body, mesh=mesh, in_specs=in_specs, out_specs=out_specs, check_vma=False)
```

profile of v0, /device:TPU:1, one launch (start us, length us, event | category | flops | bytes accessed | tf_op | source)
XLA Modules:
  0.0 223.5 jit_solution(2739491692825542733)
XLA Ops:
  7.3 1.7 reshape.785
  9.0 0.8 fusion.104
  10.7 8.7 %collective-permute-start = (bf16[128,512]{1,0:T(8,128)(2,1)S(1)}, bf16[128,512]{1,0:T(8,128)(2,1)}, u32[]{:S(2)}, u32[]{:S(2)}) collective-permute-start(bf16[128,512]{1,0:T(8,128)(2,1)S(1)} %fusion.53), channel_id=1, source_target_pairs={{0,4},{4,0},{8,12},{12,8},{16,20},{20,16},{24,28},{28,24},{32,36},... | collective-permute-start | bytes 393224 | tf_op jit(solution)/shard_map/ppermute | solution.py:16
  20.2 0.8 fusion.102
  22.6 2.2 collective-permute-start.1
  24.8 0.9 reshape.730
  25.7 0.9 reshape_reshape.9
  26.9 0.9 reshape.732
  28.5 0.8 fusion.103
  29.4 0.8 convert_element_type.244
  31.4 0.9 copy.285
  32.4 0.8 rev.13
  33.2 1.0 copy.283
  35.3 1.1 convert_reduce_fusion.1
  36.9 0.9 convert_reduce_fusion.3
  39.2 1.0 fusion.1
  43.9 1.0 copy.311
  47.0 1.0 copy.317
  48.4 1.7 broadcast_select_fusion.9
  51.0 1.9 collective-permute-start.3
  52.9 1.0 maximum_convert_fusion
  54.6 3.6 %collective-permute-start.2 = (bf16[128,512]{1,0:T(8,128)(2,1)S(1)}, bf16[128,512]{1,0:T(8,128)(2,1)}, u32[]{:S(2)}, u32[]{:S(2)}) collective-permute-start(bf16[128,512]{1,0:T(8,128)(2,1)S(1)} %fusion.54), channel_id=1, source_target_pairs={{0,8},{4,12},{8,0},{12,4},{16,24},{20,28},{24,16},{28,20},{32,40},... | collective-permute-start | bytes 393224 | tf_op jit(solution)/shard_map/ppermute | solution.py:16
  59.1 1.9 collective-permute-start.5
  61.3 1.0 copy.323
  62.3 1.1 fusion.115
  64.0 0.9 broadcast_select_fusion.7
  67.5 4.0 %collective-permute-start.4 = (bf16[128,512]{1,0:T(8,128)(2,1)S(1)}, bf16[128,512]{1,0:T(8,128)(2,1)}, u32[]{:S(2)}, u32[]{:S(2)}) collective-permute-start(bf16[128,512]{1,0:T(8,128)(2,1)S(1)} %fusion.55), channel_id=1, source_target_pairs={{0,16},{4,20},{8,24},{12,28},{16,0},{20,4},{24,8},{28,12},{32,48},... | collective-permute-start | bytes 393224 | tf_op jit(solution)/shard_map/ppermute | solution.py:16
  71.5 1.3 fusion.99
  72.8 0.9 broadcast_select_fusion.1
  75.1 5.7 %collective-permute-start.7 = (bf16[128,512]{1,0:T(8,128)(2,1)}, bf16[128,512]{1,0:T(8,128)(2,1)}, u32[]{:S(2)}, u32[]{:S(2)}) collective-permute-start(bf16[128,512]{1,0:T(8,128)(2,1)} %bitcast.335), channel_id=1, source_target_pairs={{0,32},{4,36},{8,40},{12,44},{16,48},{20,52},{24,56},{28,60},{32,0... | collective-permute-start | bytes 393224 | tf_op jit(solution)/shard_map/ppermute | solution.py:16
  80.8 1.0 copy.341
  81.8 1.0 copy.335
  82.9 1.0 fusion.114
  85.6 0.9 broadcast_select_fusion.3
  87.5 3.5 %collective-permute-start.6 = (bf16[128,512]{1,0:T(8,128)(2,1)S(1)}, bf16[128,512]{1,0:T(8,128)(2,1)S(1)}, u32[]{:S(2)}, u32[]{:S(2)}) collective-permute-start(bf16[128,512]{1,0:T(8,128)(2,1)S(1)} %fusion.56), channel_id=1, source_target_pairs={{0,32},{4,36},{8,40},{12,44},{16,48},{20,52},{24,56},{28,60},{32,0... | collective-permute-start | bytes 393224 | tf_op jit(solution)/shard_map/ppermute | solution.py:16
  91.4 3.5 %collective-permute-done.7 = bf16[128,512]{1,0:T(8,128)(2,1)} collective-permute-done((bf16[128,512]{1,0:T(8,128)(2,1)}, bf16[128,512]{1,0:T(8,128)(2,1)}, u32[]{:S(2)}, u32[]{:S(2)}) %collective-permute-start.7) | collective-permute-done | bytes 131104 | tf_op jit(solution)/shard_map/ppermute | solution.py:16
  94.9 1.0 copy.351
  95.9 11.2 %collective-permute-done.6 = bf16[128,512]{1,0:T(8,128)(2,1)S(1)} collective-permute-done((bf16[128,512]{1,0:T(8,128)(2,1)S(1)}, bf16[128,512]{1,0:T(8,128)(2,1)S(1)}, u32[]{:S(2)}, u32[]{:S(2)}) %collective-permute-start.6) | collective-permute-done | bytes 131104 | tf_op jit(solution)/shard_map/ppermute | solution.py:16
  110.3 0.8 copy.354
  111.2 1.6 copy.297
  112.8 1.6 copy.314
  114.3 1.6 copy.326
  115.9 0.9 copy.338
  116.7 0.9 copy.350
  117.6 53.3 %all-gather.2.cloned.1.call-done = bf16[512,2048]{0,1:T(8,128)(2,1)} async-done(((bf16[512,16]{0,1:T(8,128)(2,1)}), bf16[512,2048]{0,1:T(8,128)(2,1)}) %all-gather.2.cloned.1.call-update) | async-done | bytes 2097168 | tf_op jit(solution)/shard_map/all_gather | solution.py:152
  171.1 1.6 mul.426
  179.8 3.5 %convolution_convert_fusion = bf16[512,2048]{1,0:T(8,128)(2,1)} fusion(bf16[512,2048]{0,1:T(8,128)(2,1)S(1)} %copy-done.2, f32[64,8,4,128]{3,2,1,0:T(4,128)S(1)} %bitcast.346, f32[64,8,4,128]{3,2,1,0:T(4,128)S(1)} %bitcast.341, f32[64,8,4,128]{3,2,1,0:T(4,128)S(1)} %bitcast.351, f32[64,8,4,128]{3,2,1,0:T(4,128)S(1)} %bitcast.336, ...), kind=kOutput, calls=%fused_computation | convolution fusion | flops 1079246848 | bytes 21102592 | tf_op jit(solution)/shard_map/dot_general | solution.py:150
  183.4 33.3 %reduce-scatter.2.cloned.1.call-done = bf16[512,512]{1,0:T(8,128)(2,1)} async-done(((bf16[512,2048]{1,0:T(8,128)(2,1)}), bf16[512,512]{1,0:T(8,128)(2,1)}) %reduce-scatter.2.cloned.1.call-update) | async-done | bytes 524304 | tf_op jit(solution)/shard_map/reduce_scatter | solution.py:156
  (199 shorter events, 35.1 us)
Async XLA Ops:
  6.5 164.4 %all-gather.2.cloned.1.call-start = ((), (), s32[]{:S(2)}) async-start(), calls=%async_computation.1 | async-start | bytes 2113536 | tf_op jit(solution)/shard_map/all_gather | solution.py:152
  7.3 209.4 %reduce-scatter.2.cloned.1.call-start = ((), (), s32[]{:S(2)}) async-start(), calls=%async_computation.2 | async-start | bytes 2621440 | tf_op jit(solution)/shard_map/reduce_scatter | solution.py:156
  9.8 9.7 %copy-start.1 = (bf16[512,512]{1,0:T(8,128)(2,1)S(1)}, bf16[512,512]{1,0:T(8,128)(2,1)}, u32[]{:S(2)}) copy-start(bf16[512,512]{1,0:T(8,128)(2,1)} %param.6) | copy-start | bytes 1572868
  10.7 33.1 %collective-permute-start = (bf16[128,512]{1,0:T(8,128)(2,1)S(1)}, bf16[128,512]{1,0:T(8,128)(2,1)}, u32[]{:S(2)}, u32[]{:S(2)}) collective-permute-start(bf16[128,512]{1,0:T(8,128)(2,1)S(1)} %fusion.53), channel_id=1, source_target_pairs={{0,4},{4,0},{8,12},{12,8},{16,20},{20,16},{24,28},{28,24},{32,36},... | collective-permute-start | bytes 393224 | tf_op jit(solution)/shard_map/ppermute | solution.py:16
  21.0 3.8 %copy-start = (bf16[512,512]{1,0:T(8,128)(2,1)S(1)}, bf16[512,512]{1,0:T(8,128)(2,1)}, u32[]{:S(2)}) copy-start(bf16[512,512]{1,0:T(8,128)(2,1)} %param.5) | copy-start | bytes 1572868
  22.6 4.4 %copy-start.3 = (bf16[512,512]{1,0:T(8,128)(2,1)S(1)}, bf16[512,512]{1,0:T(8,128)(2,1)}, u32[]{:S(2)}) copy-start(bf16[512,512]{1,0:T(8,128)(2,1)} %param.4) | copy-start | bytes 1572868
  22.6 24.5 %collective-permute-start.1 = (bf16[128,512]{1,0:T(8,128)(2,1)}, bf16[128,512]{1,0:T(8,128)(2,1)}, u32[]{:S(2)}, u32[]{:S(2)}) collective-permute-start(bf16[128,512]{1,0:T(8,128)(2,1)} %fusion.50), channel_id=1, source_target_pairs={{0,4},{4,0},{8,12},{12,8},{16,20},{20,16},{24,28},{28,24},{32,36},... | collective-permute-start | bytes 393224 | tf_op jit(solution)/shard_map/ppermute | solution.py:16
  29.3 2.1 copy-start.5
  29.3 3.0 %copy-start.4 = (bf16[2,2,128,4,128]{4,3,2,1,0:T(4,128)(2,1)S(1)}, bf16[2,2,128,4,128]{4,3,2,1,0:T(4,128)(2,1)}, u32[]{:S(2)}) copy-start(bf16[2,2,128,4,128]{4,3,2,1,0:T(4,128)(2,1)} %reshape_reshape.9) | copy-start | bytes 1572868
  34.6 3.1 %copy-start.11 = (bf16[1,2,128,4,128]{4,3,2,1,0:T(4,128)(2,1)S(1)}, bf16[1,2,128,4,128]{4,3,2,1,0:T(4,128)(2,1)}, u32[]{:S(2)}) copy-start(bf16[1,2,128,4,128]{4,3,2,1,0:T(4,128)(2,1)} %convert_element_type.246) | copy-start | bytes 786436
  34.6 3.2 %copy-start.12 = (bf16[2,128,4,128]{3,2,1,0:T(4,128)(2,1)S(1)}, bf16[2,128,4,128]{3,2,1,0:T(4,128)(2,1)}, u32[]{:S(2)}) copy-start(bf16[2,128,4,128]{3,2,1,0:T(4,128)(2,1)} %convert_element_type.244) | copy-start | bytes 786436
  36.8 1.8 copy-start.13
  36.8 1.8 copy-start.14
  36.8 1.8 copy-start.15
  38.7 1.5 copy-start.6
  51.0 7.3 %collective-permute-start.3 = (bf16[128,512]{1,0:T(8,128)(2,1)S(1)}, bf16[128,512]{1,0:T(8,128)(2,1)S(1)}, u32[]{:S(2)}, u32[]{:S(2)}) collective-permute-start(bf16[128,512]{1,0:T(8,128)(2,1)S(1)} %fusion.51), channel_id=1, source_target_pairs={{0,8},{4,12},{8,0},{12,4},{16,24},{20,28},{24,16},{28,20},{32,40},... | collective-permute-start | bytes 393224 | tf_op jit(solution)/shard_map/ppermute | solution.py:16
  54.6 6.6 %collective-permute-start.2 = (bf16[128,512]{1,0:T(8,128)(2,1)S(1)}, bf16[128,512]{1,0:T(8,128)(2,1)}, u32[]{:S(2)}, u32[]{:S(2)}) collective-permute-start(bf16[128,512]{1,0:T(8,128)(2,1)S(1)} %fusion.54), channel_id=1, source_target_pairs={{0,8},{4,12},{8,0},{12,4},{16,24},{20,28},{24,16},{28,20},{32,40},... | collective-permute-start | bytes 393224 | tf_op jit(solution)/shard_map/ppermute | solution.py:16
  59.1 13.7 %collective-permute-start.5 = (bf16[128,512]{1,0:T(8,128)(2,1)S(1)}, bf16[128,512]{1,0:T(8,128)(2,1)}, u32[]{:S(2)}, u32[]{:S(2)}) collective-permute-start(bf16[128,512]{1,0:T(8,128)(2,1)S(1)} %fusion.52), channel_id=1, source_target_pairs={{0,16},{4,20},{8,24},{12,28},{16,0},{20,4},{24,8},{28,12},{32,48},... | collective-permute-start | bytes 393224 | tf_op jit(solution)/shard_map/ppermute | solution.py:16
  67.5 14.4 %collective-permute-start.4 = (bf16[128,512]{1,0:T(8,128)(2,1)S(1)}, bf16[128,512]{1,0:T(8,128)(2,1)}, u32[]{:S(2)}, u32[]{:S(2)}) collective-permute-start(bf16[128,512]{1,0:T(8,128)(2,1)S(1)} %fusion.55), channel_id=1, source_target_pairs={{0,16},{4,20},{8,24},{12,28},{16,0},{20,4},{24,8},{28,12},{32,48},... | collective-permute-start | bytes 393224 | tf_op jit(solution)/shard_map/ppermute | solution.py:16
  75.1 19.7 %collective-permute-start.7 = (bf16[128,512]{1,0:T(8,128)(2,1)}, bf16[128,512]{1,0:T(8,128)(2,1)}, u32[]{:S(2)}, u32[]{:S(2)}) collective-permute-start(bf16[128,512]{1,0:T(8,128)(2,1)} %bitcast.335), channel_id=1, source_target_pairs={{0,32},{4,36},{8,40},{12,44},{16,48},{20,52},{24,56},{28,60},{32,0... | collective-permute-start | bytes 393224 | tf_op jit(solution)/shard_map/ppermute | solution.py:16
  83.9 2.6 %copy-start.22 = (f32[4,32]{1,0:T(4,128)}, f32[4,32]{1,0:T(4,128)S(1)}, u32[]{:S(2)}) copy-start(f32[4,32]{1,0:T(4,128)S(1)} %get-tuple-element.60) | copy-start | bytes 1540
  86.5 20.7 %copy-start.20 = (bf16[16,512]{1,0:T(8,128)(2,1)S(1)}, bf16[16,512]{1,0:T(8,128)(2,1)}, u32[]{:S(2)}) copy-start(bf16[16,512]{1,0:T(8,128)(2,1)} %convert_reduce_fusion.4) | copy-start | bytes 49156
  86.6 4.4 %copy-start.23 = (f32[4,32]{1,0:T(4,128)S(1)}, f32[4,32]{1,0:T(4,128)}, u32[]{:S(2)}) copy-start(f32[4,32]{1,0:T(4,128)} %copy-done.22) | copy-start | bytes 1540
  86.6 22.2 %copy-start.18 = (f32[512,4]{0,1:T(4,128)S(1)}, f32[512,4]{0,1:T(4,128)}, u32[]{:S(2)}) copy-start(f32[512,4]{0,1:T(4,128)} %reshape.749) | copy-start | bytes 24580
  86.6 22.2 %copy-start.19 = (f32[512,4]{0,1:T(4,128)S(1)}, f32[512,4]{0,1:T(4,128)}, u32[]{:S(2)}) copy-start(f32[512,4]{0,1:T(4,128)} %reshape.755) | copy-start | bytes 24580
  86.6 22.2 %copy-start.21 = (f32[4,4,128]{2,1,0:T(4,128)S(1)}, f32[4,4,128]{2,1,0:T(4,128)}, u32[]{:S(2)}) copy-start(f32[4,4,128]{2,1,0:T(4,128)} %fusion.1) | copy-start | bytes 24580
  86.6 22.2 %copy-start.24 = (f32[512,4]{0,1:T(4,128)S(1)}, f32[512,4]{0,1:T(4,128)}, u32[]{:S(2)}) copy-start(f32[512,4]{0,1:T(4,128)} %copy.356) | copy-start | bytes 24580
  86.6 22.2 %copy-start.25 = (f32[512,4]{0,1:T(4,128)S(1)}, f32[512,4]{0,1:T(4,128)}, u32[]{:S(2)}) copy-start(f32[512,4]{0,1:T(4,128)} %reshape.775) | copy-start | bytes 24580
  87.0 21.9 %copy-start.26 = (f32[512,4]{0,1:T(4,128)S(1)}, f32[512,4]{0,1:T(4,128)}, u32[]{:S(2)}) copy-start(f32[512,4]{0,1:T(4,128)} %reshape.777) | copy-start | bytes 24580
  87.0 21.9 %copy-start.27 = (f32[512,4]{0,1:T(4,128)S(1)}, f32[512,4]{0,1:T(4,128)}, u32[]{:S(2)}) copy-start(f32[512,4]{0,1:T(4,128)} %reshape.761) | copy-start | bytes 24580
  87.0 21.9 %copy-start.30 = (f32[512,4]{0,1:T(4,128)S(1)}, f32[512,4]{0,1:T(4,128)}, u32[]{:S(2)}) copy-start(f32[512,4]{0,1:T(4,128)} %get-tuple-element.18) | copy-start | bytes 24580
  87.0 21.9 %copy-start.31 = (f32[512,4]{0,1:T(4,128)S(1)}, f32[512,4]{0,1:T(4,128)}, u32[]{:S(2)}) copy-start(f32[512,4]{0,1:T(4,128)} %get-tuple-element.19) | copy-start | bytes 24580
  87.5 19.6 %collective-permute-start.6 = (bf16[128,512]{1,0:T(8,128)(2,1)S(1)}, bf16[128,512]{1,0:T(8,128)(2,1)S(1)}, u32[]{:S(2)}, u32[]{:S(2)}) collective-permute-start(bf16[128,512]{1,0:T(8,128)(2,1)S(1)} %fusion.56), channel_id=1, source_target_pairs={{0,32},{4,36},{8,40},{12,44},{16,48},{20,52},{24,56},{28,60},{32,0... | collective-permute-start | bytes 393224 | tf_op jit(solution)/shard_map/ppermute | solution.py:16
  109.6 6.3 %copy-start.29 = (f32[512,4]{0,1:T(4,128)S(1)}, f32[512,4]{0,1:T(4,128)}, u32[]{:S(2)}) copy-start(f32[512,4]{0,1:T(4,128)} %get-tuple-element.14) | copy-start | bytes 24580
  109.6 7.2 %copy-start.28 = (f32[512,4]{0,1:T(4,128)S(1)}, f32[512,4]{0,1:T(4,128)}, u32[]{:S(2)}) copy-start(f32[512,4]{0,1:T(4,128)} %get-tuple-element.15) | copy-start | bytes 24580
  170.9 1.8 copy-start.10
  170.9 2.4 %copy-start.9 = (f32[512,4]{1,0:T(8,128)S(1)}, f32[512,4]{1,0:T(8,128)}, u32[]{:S(2)}) copy-start(f32[512,4]{1,0:T(8,128)} %copy.326) | copy-start | bytes 24580
  171.1 2.8 %copy-start.8 = (f32[512,4]{1,0:T(8,128)S(1)}, f32[512,4]{1,0:T(8,128)}, u32[]{:S(2)}) copy-start(f32[512,4]{1,0:T(8,128)} %copy.314) | copy-start | bytes 24580
  172.7 1.8 copy-start.7
  177.6 1.4 copy-start.16
  178.2 0.9 copy-start.17
  178.2 1.6 copy-start.2
Sparse Core Ops, SparseCore 0:
  10.5 160.4 all-gather.1
  183.5 33.1 reduce-scatter.1
where the time goes:
time: 224 us; the launch traced here: 223 us
  waiting for transfers between devices  102 us (46%)
  local copies, waits for them, and re-layouts  52.1 us (23%)
  starting transfers between devices  31.7 us (14%)
  between operations  14.6 us (7%)
  other arithmetic  14.2 us (6%)
  matrix products  8.56 us (4%)
    all_gather x1, waiting for transfers between devices, body(): lax.all_gather(out_weight, 'seq', axis=1, tiled=True)  53.3 us
    reduce_scatter x1, waiting for transfers between devices, body(): lax.psum_scatter(rounded_terms.astype(jnp.bfloat16), 'head', scatter_dime...  33.3 us
    ppermute x8, starting transfers between devices, partner(): return lax.ppermute(value, axis, pairs)  31.6 us
    ppermute x8, waiting for transfers between devices, partner(): return lax.ppermute(value, axis, pairs)  15 us
    exp x5, local copies, waits for them, and re-layouts, merge_level(): keep_old = jnp.exp(running_max - newest)  6.4 us
    ppermute x8, local copies, waits for them, and re-layouts, partner(): return lax.ppermute(value, axis, pairs)  6.36 us
  transfers between devices with their start and end apart: 10, of which 5 were waited for; matrix products, arithmetic and copies ran while one was open for 28% of the time, Pallas kernels for 0%

commit v1 on v0

v1 whole, which is shorter than its diff:
```python
import math

import jax
import jax.numpy as jnp
from jax import lax
from jax.experimental import pallas as pl
from jax.experimental.pallas import tpu as pltpu
from jax.sharding import Mesh, PartitionSpec as P


HEAD_DIM = 128
BLOCK = 128
SCORE_FACTOR = math.log2(math.e) / math.sqrt(HEAD_DIM)
SEQ = ("y", "z", "core")
VMEM_LIMIT = pltpu.CompilerParams(vmem_limit_bytes=20 * 2**20)


def swap(value, axis, mask):
    return lax.ppermute(value, axis, [(s, s ^ mask) for s in range(lax.axis_size(axis))])


def shift(value, axis, step):
    size = lax.axis_size(axis)
    return lax.ppermute(value, axis, [(s, (s + step) % size) for s in range(size)])


def pooling(rows, weight):
    out = lax.broadcasted_iota(jnp.int32, (rows // 2, rows), 0)
    source = lax.broadcasted_iota(jnp.int32, (rows // 2, rows), 1)
    return jnp.where((source >> 1) == out, weight, 0.0).astype(jnp.bfloat16)


def pool(array_in, weight):
    rows = array_in.shape[0]
    if rows > 256:
        return jnp.concatenate(
            [pool(array_in[start : start + 256], weight) for start in range(0, rows, 256)], axis=0
        )
    pooled = jnp.dot(pooling(rows, weight), array_in, preferred_element_type=jnp.float32)
    return pooled.astype(jnp.bfloat16)


def scores(query_rows, key_rows):
    products = lax.dot_general(
        query_rows, key_rows, (((1,), (1,)), ((), ())), preferred_element_type=jnp.float32
    )
    return products * SCORE_FACTOR


def weighted(prob, value_rows):
    return jnp.dot(prob.astype(jnp.bfloat16), value_rows, preferred_element_type=jnp.float32)


def pool_kernel(key_ref, value_ref, p2_ref, p3_ref, p4_ref, p5_ref):
    for side, (ref, weight) in enumerate(((key_ref, 0.5), (value_ref, 1.0))):
        level = pool(ref[...], weight)
        for out_ref in (p2_ref, p3_ref, p4_ref, p5_ref):
            level = pool(level, weight)
            out_ref[side] = level


def stat_rows(stat):
    wide = jnp.broadcast_to(stat, (stat.shape[0], HEAD_DIM))
    rows = [wide[i : i + 128].T[0:1] for i in range(0, stat.shape[0], 128)]
    return rows[0] if len(rows) == 1 else jnp.concatenate(rows, axis=0)


def three_parts(value):
    high = value.astype(jnp.bfloat16)
    rest = value - high.astype(jnp.float32)
    middle = rest.astype(jnp.bfloat16)
    low = (rest - middle.astype(jnp.float32)).astype(jnp.bfloat16)
    return high, middle, low


def stat_tile(stat):
    parts = jnp.concatenate(
        [p.astype(jnp.float32) for p in three_parts(stat_rows(stat))], axis=0
    )
    blank = jnp.zeros((16 - parts.shape[0], HEAD_DIM), jnp.float32)
    return jnp.concatenate([parts, blank], axis=0).astype(jnp.bfloat16)


def near_head(queries, keys, values):
    half = 2 * BLOCK
    q1, k1, v1 = pool(queries, 0.5), pool(keys, 0.5), pool(values, 1.0)
    coarse = []
    level = q1
    for _ in range(4):
        level = pool(level, 0.5)
        coarse.append(level)
    fine = lax.broadcasted_iota(jnp.int32, (half, BLOCK), 0)
    pooled = lax.broadcasted_iota(jnp.int32, (half, BLOCK), 1)
    spread = jnp.where((fine >> 1) == pooled, 1.0, 0.0).astype(jnp.bfloat16)
    means, stats = [], []
    for group in range(2):
        rows = slice(group * half, (group + 1) * half)
        own = slice(group * BLOCK, (group + 1) * BLOCK)
        other = slice((1 - group) * BLOCK, (2 - group) * BLOCK)
        q1_rows = jnp.dot(spread, q1[own], preferred_element_type=jnp.float32)
        near = scores(queries[rows], keys[rows])
        level1 = scores(q1_rows.astype(jnp.bfloat16), k1[other])
        peak = jnp.maximum(
            jnp.max(near, axis=1, keepdims=True), jnp.max(level1, axis=1, keepdims=True)
        )
        near, level1 = jnp.exp2(near - peak), jnp.exp2(level1 - peak)
        mass = jnp.sum(near, axis=1, keepdims=True) + 2.0 * jnp.sum(level1, axis=1, keepdims=True)
        total = weighted(near, values[rows]) + weighted(level1, v1[other])
        means.append((total / mass).astype(jnp.bfloat16))
        stats.append(peak + jnp.log2(mass))
    return (
        jnp.concatenate(means, axis=0),
        stat_tile(jnp.concatenate(stats, axis=0)),
        jnp.concatenate(coarse, axis=0),
    )


def near_kernel(query_ref, key_ref, value_ref, *refs):
    out_ref, coarse_ref = refs[-2:]
    rows = query_ref.shape[0]
    for start in range(0, query_ref.shape[1], HEAD_DIM):
        lanes = slice(start, start + HEAD_DIM)
        mean, tile, coarse = near_head(query_ref[:, lanes], key_ref[:, lanes], value_ref[:, lanes])
        coarse_ref[:, lanes] = coarse
        out_ref[:rows, lanes] = mean
        out_ref[rows:, lanes] = tile


def repeat_rows(value, factor, scratch_ref):
    rows = value.shape[0]
    for offset in range(factor):
        scratch_ref[pl.ds(offset, rows, stride=factor), :] = value
    return scratch_ref[0 : rows * factor, :]


def merge(one, two):
    top = jnp.maximum(one[0], two[0])
    keep_one, keep_two = jnp.exp2(one[0] - top), jnp.exp2(two[0] - top)
    return (top, one[1] * keep_one + two[1] * keep_two, one[2] * keep_one + two[2] * keep_two)


def far_head(coarse, keys, values, scratch):
    terms, start = [], 0
    for level in range(4):
        rows = BLOCK >> level
        logits = scores(coarse[start : start + rows], keys[level])
        start += rows
        peak = jnp.max(logits, axis=1, keepdims=True)
        prob = jnp.exp2(logits - peak)
        mass = 2.0 ** (level + 2) * jnp.sum(prob, axis=1, keepdims=True)
        terms.append(
            (
                jnp.broadcast_to(peak, (rows, HEAD_DIM)),
                jnp.broadcast_to(mass, (rows, HEAD_DIM)),
                weighted(prob, values[level]),
            )
        )
    running = terms[3]
    for level in (2, 1, 0):
        spread = tuple(repeat_rows(v, 2, ref) for v, ref in zip(running, scratch))
        running = merge(terms[level], spread)
    peak, mass, total = running
    return (total / mass).astype(jnp.bfloat16), stat_tile((peak + jnp.log2(mass))[:, 0:1])


def far_kernel(coarse_ref, a_ref, b_ref, c_ref, d_ref, out_ref, *scratch):
    for head in range(coarse_ref.shape[1] // HEAD_DIM):
        lanes = slice(head * HEAD_DIM, (head + 1) * HEAD_DIM)

        def rows_of(side):
            a, b, c, d = (ref[side, :, lanes] for ref in (a_ref, b_ref, c_ref, d_ref))
            return (
                d[192:320],
                jnp.concatenate([c[64:128], d[128:192]], axis=0),
                jnp.concatenate([b[16:48], c[32:64], d[32:64], d[96:128]], axis=0),
                jnp.concatenate([a[:16], b[:16], c[:32], d[:32], d[64:96]], axis=0),
            )

        mean, tile = far_head(
            coarse_ref[:, lanes], rows_of(0), rows_of(1), scratch[3 * head : 3 * head + 3]
        )
        for copy in range(out_ref.shape[0]):
            out_ref[copy, :BLOCK, lanes] = mean
            out_ref[copy, BLOCK:, lanes] = tile


def shape(dims, dtype=jnp.bfloat16):
    return jax.ShapeDtypeStruct(dims, dtype)


def pooled_levels(keys, values):
    width = keys.shape[1]
    return pl.pallas_call(
        pool_kernel, compiler_params=VMEM_LIMIT, out_shape=[shape((2, BLOCK >> level, width)) for level in range(4)]
    )(keys, values)


def near_part(queries, keys, values, part, parts, buffers=()):
    rows, width = queries.shape
    coarse, lanes = 240, width // parts
    columns = pl.BlockSpec((rows, lanes), lambda i: (0, part))
    return pl.pallas_call(
        near_kernel,
        grid=(1,),
        compiler_params=VMEM_LIMIT,
        in_specs=[columns] * 3 + [pl.BlockSpec(memory_space=pl.ANY)] * len(buffers),
        out_specs=[
            pl.BlockSpec((rows + 16, lanes), lambda i: (0, part)),
            pl.BlockSpec((coarse, lanes), lambda i: (0, part)),
        ],
        out_shape=[shape((rows + 16, width)), shape((coarse, width))],
        input_output_aliases={3 + i: i for i in range(len(buffers))},
    )(queries, keys, values, *buffers)


def in_vmem(value):
    return pltpu.with_memory_space_constraint(value, pltpu.VMEM)


def far_part(coarse, pieces, copies):
    width = coarse.shape[1]
    heads = width // HEAD_DIM
    return pl.pallas_call(
        far_kernel,
        compiler_params=VMEM_LIMIT,
        out_shape=shape((copies, BLOCK + 16, width)),
        scratch_shapes=[pltpu.VMEM((BLOCK, HEAD_DIM), jnp.float32)] * (3 * heads),
    )(in_vmem(coarse), *map(in_vmem, pieces))


def times(rows, weight_rows):
    return lax.dot_general(
        rows, weight_rows, (((1,), (1,)), ((), ())), preferred_element_type=jnp.float32
    )


def opposite(z):
    return (z + jnp.where((z & 4) == 4, 4, 12)) & 15


def placed(total, z, core):
    width = total.shape[1]
    source = lax.broadcasted_iota(jnp.int32, (width, 1), 0)
    slot = source >> 4
    origin = z ^ ((slot >> 3) & 1) ^ (((slot >> 2) & 1) << 1) ^ (((slot >> 1) & 1) << 2)
    origin = jnp.where((slot & 1) == 1, opposite(origin), origin)
    target = origin * 32 + core * 16 + (source & 15)
    column = lax.broadcasted_iota(jnp.int32, (width, 2 * width), 1)
    choice = jnp.where(column == target, 1.0, 0.0).astype(jnp.bfloat16)
    return jnp.dot(total.astype(jnp.bfloat16), choice, preferred_element_type=jnp.float32)


def mix_kernel(place_ref, *refs):
    groups = 4
    near_refs, own_refs = refs[:groups], refs[groups : 2 * groups]
    far_ref, other_ref, out_ref, attended_ref = refs[2 * groups :]
    z, core, x, y = (place_ref[i] for i in range(4))
    width = near_refs[0].shape[1]
    rows, coarse_rows = out_ref.shape[0], BLOCK
    tiles, ratio = rows // BLOCK, rows // coarse_rows
    heads = width // HEAD_DIM
    steps = (0, groups - 1, 1, 2)
    sources = [(x + step) & (groups - 1) for step in steps]
    near_stats = [ref[rows:].astype(jnp.float32) for ref in near_refs]
    far_stats = [far_ref[g, coarse_rows:] for g in sources]
    coarse = lax.broadcasted_iota(jnp.int32, (HEAD_DIM, BLOCK), 0)
    fine = lax.broadcasted_iota(jnp.int32, (HEAD_DIM, BLOCK), 1)
    depth = BLOCK // ratio
    out_row = lax.broadcasted_iota(jnp.int32, (BLOCK, depth), 0)
    in_row = lax.broadcasted_iota(jnp.int32, (BLOCK, depth), 1)
    spread_rows = jnp.where(out_row // ratio == in_row, 1.0, 0.0).astype(jnp.bfloat16)
    for i, g in enumerate(sources):
        shares = []
        for tile in range(tiles):
            chosen = jnp.where(fine // ratio + tile * depth == coarse, 1.0, 0.0)
            chosen = chosen.astype(jnp.bfloat16)
            for head in range(heads):
                lanes = slice(head * HEAD_DIM, (head + 1) * HEAD_DIM)
                parts = jnp.dot(far_stats[i][:, lanes], chosen, preferred_element_type=jnp.float32)
                far = parts[0:1] + (parts[1:2] + parts[2:3])
                part = [near_stats[i][p * tiles + tile : p * tiles + tile + 1, lanes] for p in range(3)]
                near = part[0] + (part[1] + part[2])
                shares.append(1.0 / (1.0 + jnp.exp2(jnp.minimum(far - near, 120.0))))
        shares = jnp.concatenate(shares, axis=0)
        blank = jnp.zeros((BLOCK - shares.shape[0], BLOCK), jnp.float32)
        shares = jnp.concatenate([shares, blank], axis=0).T
        for tile in range(tiles):
            far = jnp.dot(
                spread_rows,
                far_ref[g, tile * depth : (tile + 1) * depth],
                preferred_element_type=jnp.float32,
            )
            near = near_refs[i][tile * BLOCK : (tile + 1) * BLOCK].astype(jnp.float32)
            share = jnp.concatenate(
                [
                    jnp.broadcast_to(shares[:, k : k + 1], (BLOCK, HEAD_DIM))
                    for k in range(tile * heads, (tile + 1) * heads)
                ],
                axis=1,
            )
            attended = (far + share * (near - far)).astype(jnp.bfloat16)
            attended_ref[g, tile * BLOCK : (tile + 1) * BLOCK] = attended
    own, other = 0.0, 0.0
    for i, step in enumerate(steps):
        attended = attended_ref[(y + step) & (groups - 1)]
        own = own + times(attended, own_refs[i][...])
        other = other + times(attended, other_ref[i])
    out_ref[...] = (placed(own, z, core) + placed(other, z, 1 - core)).astype(jnp.bfloat16)


def mix_part(place, near, own, far, other):
    rows, width = near[0].shape[0] - 16, near[0].shape[1]
    vmem = pl.BlockSpec(memory_space=pltpu.VMEM)
    return pl.pallas_call(
        mix_kernel,
        compiler_params=VMEM_LIMIT,
        in_specs=[pl.BlockSpec(memory_space=pltpu.SMEM)] + [vmem] * (2 * len(near) + 2),
        out_shape=shape((rows, 2 * own[0].shape[0])),
        scratch_shapes=[pltpu.VMEM((len(near), rows, width), jnp.bfloat16)],
    )(place, *map(in_vmem, (*near, *own, far, other)))


def body(queries, key_vectors, values, out_weight):
    heads, ring = lax.axis_size("head"), lax.axis_size("z")
    width = queries.shape[1]

    turn = [(y * heads + x, x * heads + y) for y in range(heads) for x in range(heads)]

    def across(z):
        return (z + (4 if z & 4 else 12)) % 16

    def paired(weights):
        return weights.reshape(2, weights.shape[0] // 2, width)

    def joined(weights):
        return weights.reshape(-1, width)

    w_own = lax.ppermute(out_weight.T, ("y", "head"), turn)
    p2, p3, p4, p5 = pooled_levels(key_vectors, values)
    w_across = lax.ppermute(w_own, "z", [(z, across(z)) for z in range(ring)])
    weights = jnp.concatenate([w_own, w_across], axis=0)
    a = swap(jnp.concatenate([p5, paired(weights)], axis=1), "z", 4)
    weights = jnp.concatenate([weights, joined(a[:, 16:])], axis=0)
    near, coarse = near_part(queries, key_vectors, values, 0, 1)
    b = swap(jnp.concatenate([a[:, :16], p4, paired(weights)], axis=1), "z", 2)
    weights = jnp.concatenate([weights, joined(b[:, 48:])], axis=0)
    right = shift(near, "head", 1)
    left = shift(near, "head", -1)
    c = swap(jnp.concatenate([a[:, :16], b[:, :48], p3, paired(weights)], axis=1), "z", 1)
    weights = jnp.concatenate([weights, joined(c[:, 128:])], axis=0)
    over = shift(near, "head", 2)
    d = swap(jnp.concatenate([a[:, :16], b[:, :48], c[:, :128], p2], axis=1), "core", 1)
    own = [weights]
    for step in (1, -1, 2):
        own.append(shift(weights, "y", step))
    far = far_part(coarse, (a, b, c, d), heads)
    far = lax.all_to_all(far, "head", 0, 0)
    other = swap(jnp.stack(own), "core", 1)
    place = jnp.stack([lax.axis_index(name) for name in ("z", "core", "head", "y")]).astype(jnp.int32)
    return mix_part(place, (near, right, left, over), own, far, other)


def solution(mesh):
    fine = Mesh(mesh.devices.reshape(4, 16, 2, 4), SEQ + ("head",))
    rows = P(SEQ, "head")

    return jax.shard_map(
        body, mesh=fine, in_specs=(rows, rows, rows, P("head", SEQ)), out_specs=rows, check_vma=False
    )
```

time: 224 us -> 128 us (0.57)
  waiting for transfers between devices: 102 us -> 44.9 us
  local copies, waits for them, and re-layouts: 52.1 us -> 2.17 us
  starting transfers between devices: 31.7 us -> 59.2 us
  Pallas kernels: 0 us -> 17.9 us
  between operations: 14.6 us -> 0.31 us
  other arithmetic: 14.2 us -> 1.33 us
  matrix products: 8.56 us -> 0 us
    all_gather x1 -> x0, waiting for transfers between devices: 53.3 us -> none  [body(): lax.all_gather(out_weight, 'seq', axis=1, tiled=True)]
    reduce_scatter x1 -> x0, waiting for transfers between devices: 33.3 us -> none  [body(): lax.psum_scatter(rounded_terms.astype(jnp.bfloat16), 'head', scatter_dime...]
    ppermute x8 -> x13, starting transfers between devices: 31.6 us -> 55.8 us  [the longest x5 22 us: swap(): lax.ppermute(value, axis, [(s, s ^ mask) for s in range(lax.axis_size(axi...]
    ppermute x8 -> x13, waiting for transfers between devices: 15 us -> 38.7 us  [the longest x5 28.1 us: swap(): lax.ppermute(value, axis, [(s, s ^ mask) for s in range(lax.axis_size(axi...]
    pallas_call x0 -> x4, Pallas kernels: none -> 17.9 us  [the longest x1 5.83 us: mix_part(): pl.pallas_call(mix_kernel, compiler_params=VMEM_LIMIT, in_specs=[pl.Block...]
    reshape x27 -> x0, local copies, waits for them, and re-layouts: 14.1 us -> none  [the longest x5 3.91 us: to_blocks(): array_in.reshape(-1, block_rows, head_count, array_in.shape[1] // head_co...]
    dot_general x13 -> x0, matrix products: 8.56 us -> none  [the longest x1 3.52 us: body(): jnp.dot(attended, lax.all_gather(out_weight, 'seq', axis=1, tiled=True),...]
    exp x10 -> x0, local copies, waits for them, and re-layouts: 7.84 us -> none  [the longest x5 6.4 us: merge_level(): keep_old = jnp.exp(running_max - newest)]
  transfers between devices with their start and end apart: 10 -> 14, of which waited for: 5 -> 5; matrix products, arithmetic and copies ran while one was open for 28% -> 1% of each run, Pallas kernels for 0% -> 10%
where the time goes in v1:
time: 128 us; the launch traced here: 126 us
  starting transfers between devices  59.2 us (46%)
  waiting for transfers between devices  44.9 us (35%)
  Pallas kernels  17.9 us (14%)
  local copies, waits for them, and re-layouts  2.17 us (2%)
  other arithmetic  1.33 us (1%)
    ppermute x5, waiting for transfers between devices, swap(): lax.ppermute(value, axis, [(s, s ^ mask) for s in range(lax.axis_size(axi...  28.1 us
    ppermute x5, starting transfers between devices, swap(): lax.ppermute(value, axis, [(s, s ^ mask) for s in range(lax.axis_size(axi...  22 us
    ppermute x6, starting transfers between devices, shift(): lax.ppermute(value, axis, [(s, (s + step) % size) for s in range(size)])  19.2 us
    ppermute x1, starting transfers between devices, body(): w_across = lax.ppermute(w_own, 'z', [(z, across(z)) for z in range(ring)])  13.3 us
    ppermute x6, waiting for transfers between devices, shift(): lax.ppermute(value, axis, [(s, (s + step) % size) for s in range(size)])  10.6 us
    all_to_all x1, waiting for transfers between devices, body(): far = lax.all_to_all(far, 'head', 0, 0)  6.21 us
    pallas_call x1, Pallas kernels, mix_part(): pl.pallas_call(mix_kernel, compiler_params=VMEM_LIMIT, in_specs=[pl.Block...  5.83 us
    pallas_call x1, Pallas kernels, near_part(): pl.pallas_call(near_kernel, grid=(1,), compiler_params=VMEM_LIMIT, in_spe...  5.82 us
  transfers between devices with their start and end apart: 14, of which 5 were waited for; matrix products, arithmetic and copies ran while one was open for 1% of the time, Pallas kernels for 10%

profile of v1, /device:TPU:1, one launch (start us, length us, event | category | flops | bytes accessed | tf_op | source)
XLA Modules:
  0.0 126.0 jit_solution(7887866830926687814)
XLA Ops:
  0.0 1.4 %collective-permute-start.3 = (bf16[16,512]{1,0:T(8,128)(2,1)}, bf16[16,512]{1,0:T(8,128)(2,1)S(1)}, u32[]{:S(2)}, u32[]{:S(2)}) collective-permute-start(bf16[16,512]{1,0:T(8,128)(2,1)} %bitcast.28), channel_id=1, source_target_pairs={{0,0},{1,128},{2,256},{3,384},{128,1},{129,129},{130,257},{131,385... | collective-permute-start | bytes 49160 | tf_op jit(solution)/shard_map/ppermute | solution.py:338
  1.4 0.0 collective-permute-done.3
  1.4 13.3 %collective-permute-start.4 = (bf16[16,512]{1,0:T(8,128)(2,1)S(1)}, bf16[16,512]{1,0:T(8,128)(2,1)S(1)}, u32[]{:S(2)}, u32[]{:S(2)}) collective-permute-start(bf16[16,512]{1,0:T(8,128)(2,1)S(1)} %collective-permute-done.3), channel_id=1, source_target_pairs={{0,96},{8,104},{16,112},{24,120},{32,64},{40,72},{48,80},{56,88},{... | collective-permute-start | bytes 49160 | tf_op jit(solution)/shard_map/ppermute | solution.py:340
  14.6 0.0 copy-start
  14.6 1.0 copy-done
  15.7 0.0 copy-start.2
  15.7 1.0 copy-done.2
  16.7 1.4 %shard_map.47 = (bf16[2,128,512]{2,1,0:T(8,128)(2,1)S(1)}, bf16[2,64,512]{2,1,0:T(8,128)(2,1)S(1)}, bf16[2,32,512]{2,1,0:T(8,128)(2,1)S(1)}, bf16[2,16,512]{2,1,0:T(8,128)(2,1)S(1)}) custom-call(bf16[512,512]{1,0:T(8,128)(2,1)S(1)} %copy-done, bf16[512,512]{1,0:T(8,128)(2,1)S(1)} %copy-done.2), custom_call_target="tpu_custom_call" | custom-call | tf_op jit(solution)/shard_map/pallas_call | solution.py:193
  18.1 0.0 collective-permute-done.4
  18.2 5.2 %collective-permute-start.5 = (bf16[2,32,512]{2,1,0:T(8,128)(2,1)S(1)}, bf16[2,32,512]{2,1,0:T(8,128)(2,1)S(1)}, u32[]{:S(2)}, u32[]{:S(2)}) collective-permute-start(bf16[2,32,512]{2,1,0:T(8,128)(2,1)S(1)} %pad_maximum_fusion.5), channel_id=1, source_target_pairs={{0,32},{8,40},{16,48},{24,56},{32,0},{40,8},{48,16},{56,24},{64,96... | collective-permute-start | bytes 196616 | tf_op jit(solution)/shard_map/ppermute | solution.py:19
  23.3 8.4 %collective-permute-done.5.a_ref = bf16[2,32,512]{2,1,0:T(8,128)(2,1)S(1)} collective-permute-done((bf16[2,32,512]{2,1,0:T(8,128)(2,1)S(1)}, bf16[2,32,512]{2,1,0:T(8,128)(2,1)S(1)}, u32[]{:S(2)}, u32[]{:S(2)}) %collective-permute-start.5) | collective-permute-done | bytes 65568 | tf_op jit(solution)/shard_map/ppermute | solution.py:19
  31.8 1.9 %collective-permute-start.6 = (bf16[2,80,512]{2,1,0:T(8,128)(2,1)S(1)}, bf16[2,80,512]{2,1,0:T(8,128)(2,1)S(1)}, u32[]{:S(2)}, u32[]{:S(2)}) collective-permute-start(bf16[2,80,512]{2,1,0:T(8,128)(2,1)S(1)} %pad_maximum_fusion.3), channel_id=1, source_target_pairs={{0,16},{8,24},{16,0},{24,8},{32,48},{40,56},{48,32},{56,40},{64,80... | collective-permute-start | bytes 491528 | tf_op jit(solution)/shard_map/ppermute | solution.py:19
  33.7 9.6 %collective-permute-done.6.b_ref = bf16[2,80,512]{2,1,0:T(8,128)(2,1)S(1)} collective-permute-done((bf16[2,80,512]{2,1,0:T(8,128)(2,1)S(1)}, bf16[2,80,512]{2,1,0:T(8,128)(2,1)S(1)}, u32[]{:S(2)}, u32[]{:S(2)}) %collective-permute-start.6) | collective-permute-done | bytes 163872 | tf_op jit(solution)/shard_map/ppermute | solution.py:19
  43.4 1.9 %collective-permute-start.7 = (bf16[2,192,512]{2,1,0:T(8,128)(2,1)S(1)}, bf16[2,192,512]{2,1,0:T(8,128)(2,1)S(1)}, u32[]{:S(2)}, u32[]{:S(2)}) collective-permute-start(bf16[2,192,512]{2,1,0:T(8,128)(2,1)S(1)} %pad_maximum_fusion.2), channel_id=1, source_target_pairs={{0,8},{8,0},{16,24},{24,16},{32,40},{40,32},{48,56},{56,48},{64,72... | collective-permute-start | bytes 1179656 | tf_op jit(solution)/shard_map/ppermute | solution.py:19
  45.4 10.1 %collective-permute-done.7.c_ref = bf16[2,192,512]{2,1,0:T(8,128)(2,1)S(1)} collective-permute-done((bf16[2,192,512]{2,1,0:T(8,128)(2,1)S(1)}, bf16[2,192,512]{2,1,0:T(8,128)(2,1)S(1)}, u32[]{:S(2)}, u32[]{:S(2)}) %collective-permute-start.7) | collective-permute-done | bytes 393248 | tf_op jit(solution)/shard_map/ppermute | solution.py:19
  55.5 1.9 %collective-permute-start.8 = (bf16[256,512]{1,0:T(8,128)(2,1)S(1)}, bf16[256,512]{1,0:T(8,128)(2,1)S(1)}, u32[]{:S(2)}, u32[]{:S(2)}) collective-permute-start(bf16[256,512]{1,0:T(8,128)(2,1)S(1)} %constant_dynamic-update-slice_fusion.refs_4_), channel_id=1, source_target_pairs={{0,128},{128,256},{256,384},{384,0},{1,129},{129,257},{257,385},{3... | collective-permute-start | bytes 786440 | tf_op jit(solution)/shard_map/ppermute | solution.py:24
  57.4 4.6 %collective-permute-start.9 = (bf16[256,512]{1,0:T(8,128)(2,1)S(1)}, bf16[256,512]{1,0:T(8,128)(2,1)S(1)}, u32[]{:S(2)}, u32[]{:S(2)}) collective-permute-start(bf16[256,512]{1,0:T(8,128)(2,1)S(1)} %constant_dynamic-update-slice_fusion.refs_4_), channel_id=1, source_target_pairs={{0,384},{128,0},{256,128},{384,256},{1,385},{129,1},{257,129},{385... | collective-permute-start | bytes 786440 | tf_op jit(solution)/shard_map/ppermute | solution.py:24
  62.0 1.9 %collective-permute-start.10 = (bf16[256,512]{1,0:T(8,128)(2,1)S(1)}, bf16[256,512]{1,0:T(8,128)(2,1)S(1)}, u32[]{:S(2)}, u32[]{:S(2)}) collective-permute-start(bf16[256,512]{1,0:T(8,128)(2,1)S(1)} %constant_dynamic-update-slice_fusion.refs_4_), channel_id=1, source_target_pairs={{0,256},{128,384},{256,0},{384,128},{1,257},{129,385},{257,1},{385... | collective-permute-start | bytes 786440 | tf_op jit(solution)/shard_map/ppermute | solution.py:24
  64.0 8.1 %collective-permute-start.11 = (bf16[2,320,512]{2,1,0:T(8,128)(2,1)S(1)}, bf16[2,320,512]{2,1,0:T(8,128)(2,1)S(1)}, u32[]{:S(2)}, u32[]{:S(2)}) collective-permute-start(bf16[2,320,512]{2,1,0:T(8,128)(2,1)S(1)} %pad_maximum_fusion.1), channel_id=1, source_target_pairs={{0,4},{4,0},{1,5},{5,1},{2,6},{6,2},{3,7},{7,3},{8,12},{12,8},{9,1... | collective-permute-start | bytes 1966088 | tf_op jit(solution)/shard_map/ppermute | solution.py:19
  72.1 0.0 collective-permute-done.8.refs_5_
  72.1 0.0 collective-permute-done.9.refs_6_
  72.1 0.0 collective-permute-done.10.refs_7_
  72.1 0.0 copy-start.1
  72.1 0.0 copy-start.3
  72.1 0.0 copy-start.4
  72.1 1.1 pad_maximum_fusion
  73.3 4.9 %collective-permute-start.12 = (bf16[4,256,512]{2,1,0:T(8,128)(2,1)}, bf16[4,256,512]{2,1,0:T(8,128)(2,1)S(1)}, u32[]{:S(2)}, u32[]{:S(2)}) collective-permute-start(bf16[4,256,512]{2,1,0:T(8,128)(2,1)} %pad_maximum_fusion), channel_id=1, source_target_pairs={{0,4},{4,0},{1,5},{5,1},{2,6},{6,2},{3,7},{7,3},{8,12},{12,8},{9,1... | collective-permute-start | bytes 3145736 | tf_op jit(solution)/shard_map/ppermute | solution.py:19
  78.2 0.0 copy-done.1
  78.2 0.0 copy-done.3
  78.2 0.0 copy-done.4
  78.2 5.8 %shard_map.46 = (bf16[528,512]{1,0:T(8,128)(2,1)S(1)}, bf16[240,512]{1,0:T(8,128)(2,1)S(1)}) custom-call(bf16[512,512]{1,0:T(8,128)(2,1)S(1)} %copy-done.4, bf16[512,512]{1,0:T(8,128)(2,1)S(1)} %copy-done.1, bf16[512,512]{1,0:T(8,128)(2,1)S(1)} %copy-done.3), custom_call_target="tpu_custom_call" | custom-call | tf_op jit(solution)/shard_map/pallas_call | solution.py:202
  84.0 3.7 %collective-permute-start = (bf16[528,512]{1,0:T(8,128)(2,1)S(1)}, bf16[528,512]{1,0:T(8,128)(2,1)}, u32[]{:S(2)}, u32[]{:S(2)}) collective-permute-start(bf16[528,512]{1,0:T(8,128)(2,1)S(1)} %get-tuple-element.11.refs_0_), channel_id=1, source_target_pairs={{0,1},{1,2},{2,3},{3,0},{4,5},{5,6},{6,7},{7,4},{8,9},{9,10},{10,1... | collective-permute-start | bytes 1622024 | tf_op jit(solution)/shard_map/ppermute | solution.py:24
  87.8 2.8 %collective-permute-start.1 = (bf16[528,512]{1,0:T(8,128)(2,1)S(1)}, bf16[528,512]{1,0:T(8,128)(2,1)}, u32[]{:S(2)}, u32[]{:S(2)}) collective-permute-start(bf16[528,512]{1,0:T(8,128)(2,1)S(1)} %get-tuple-element.11.refs_0_), channel_id=1, source_target_pairs={{0,3},{1,0},{2,1},{3,2},{4,7},{5,4},{6,5},{7,6},{8,11},{9,8},{10,9... | collective-permute-start | bytes 1622024 | tf_op jit(solution)/shard_map/ppermute | solution.py:24
  90.6 4.2 %collective-permute-start.2 = (bf16[528,512]{1,0:T(8,128)(2,1)S(1)}, bf16[528,512]{1,0:T(8,128)(2,1)}, u32[]{:S(2)}, u32[]{:S(2)}) collective-permute-start(bf16[528,512]{1,0:T(8,128)(2,1)S(1)} %get-tuple-element.11.refs_0_), channel_id=1, source_target_pairs={{0,2},{1,3},{2,0},{3,1},{4,6},{5,7},{6,4},{7,5},{8,10},{9,11},{10,... | collective-permute-start | bytes 1622024 | tf_op jit(solution)/shard_map/ppermute | solution.py:24
  94.8 0.0 collective-permute-done.11.d_ref
  94.8 4.9 %shard_map.48 = bf16[4,144,512]{2,1,0:T(8,128)(2,1)} custom-call(bf16[240,512]{1,0:T(8,128)(2,1)S(1)} %get-tuple-element.15.coarse_ref, bf16[2,32,512]{2,1,0:T(8,128)(2,1)S(1)} %collective-permute-done.5.a_ref, bf16[2,80,512]{2,1,0:T(8,128)(2,1)S(1)} %collective-permute-done.6.b_ref, bf16[2,192,512]{2,1,0:T(8,128)(2,1)S(1)} %collective-permute-done.7.c_ref, ...), custom_call_target="tpu_custom_call" | custom-call | tf_op jit(solution)/shard_map/pallas_call | solution.py:223
  99.7 3.5 %all-to-all-start = ((bf16[4,144,512]{2,1,0:T(8,128)(2,1)}), bf16[4,144,512]{2,1,0:T(8,128)(2,1)S(1)}, u32[]{:S(2)}, u32[]{:S(2)}) async-start(bf16[4,144,512]{2,1,0:T(8,128)(2,1)} %shard_map.48), calls=%async_computation | async-start | bytes 1179648 | tf_op jit(solution)/shard_map/all_to_all | solution.py:357
  103.2 0.1 pad_add_fusion.place_ref
  103.3 0.0 collective-permute-done.refs_1_
  103.3 0.0 collective-permute-done.1.refs_2_
  103.3 10.6 %collective-permute-done.2.refs_3_ = bf16[528,512]{1,0:T(8,128)(2,1)} collective-permute-done((bf16[528,512]{1,0:T(8,128)(2,1)S(1)}, bf16[528,512]{1,0:T(8,128)(2,1)}, u32[]{:S(2)}, u32[]{:S(2)}) %collective-permute-start.2) | collective-permute-done | bytes 540704 | tf_op jit(solution)/shard_map/ppermute | solution.py:24
  113.9 6.2 %all-to-all-done.refs_8_ = bf16[4,144,512]{2,1,0:T(8,128)(2,1)S(1)} async-done(((bf16[4,144,512]{2,1,0:T(8,128)(2,1)}), bf16[4,144,512]{2,1,0:T(8,128)(2,1)S(1)}, u32[]{:S(2)}, u32[]{:S(2)}) %all-to-all-start) | async-done | bytes 589856 | tf_op jit(solution)/shard_map/all_to_all | solution.py:357
  120.1 0.0 collective-permute-done.12.refs_9_
  120.1 5.8 %shard_map.49 = bf16[512,512]{1,0:T(8,128)(2,1)} custom-call(s32[4]{0:T(128)S(1)} %pad_add_fusion.place_ref, bf16[528,512]{1,0:T(8,128)(2,1)S(1)} %get-tuple-element.11.refs_0_, bf16[528,512]{1,0:T(8,128)(2,1)} %collective-permute-done.refs_1_, bf16[528,512]{1,0:T(8,128)(2,1)} %collective-permute-done.1.refs_2_, ...), custom_call_target="tpu_custom_call" | custom-call | tf_op jit(solution)/shard_map/pallas_call | solution.py:314
  (17 shorter events, 0.2 us)
Async XLA Ops:
  0.0 1.4 %collective-permute-start.3 = (bf16[16,512]{1,0:T(8,128)(2,1)}, bf16[16,512]{1,0:T(8,128)(2,1)S(1)}, u32[]{:S(2)}, u32[]{:S(2)}) collective-permute-start(bf16[16,512]{1,0:T(8,128)(2,1)} %bitcast.28), channel_id=1, source_target_pairs={{0,0},{1,128},{2,256},{3,384},{128,1},{129,129},{130,257},{131,385... | collective-permute-start | bytes 49160 | tf_op jit(solution)/shard_map/ppermute | solution.py:338
  1.4 16.8 %collective-permute-start.4 = (bf16[16,512]{1,0:T(8,128)(2,1)S(1)}, bf16[16,512]{1,0:T(8,128)(2,1)S(1)}, u32[]{:S(2)}, u32[]{:S(2)}) collective-permute-start(bf16[16,512]{1,0:T(8,128)(2,1)S(1)} %collective-permute-done.3), channel_id=1, source_target_pairs={{0,96},{8,104},{16,112},{24,120},{32,64},{40,72},{48,80},{56,88},{... | collective-permute-start | bytes 49160 | tf_op jit(solution)/shard_map/ppermute | solution.py:340
  14.6 1.0 copy-start
  15.7 1.0 copy-start.2
  18.2 13.6 %collective-permute-start.5 = (bf16[2,32,512]{2,1,0:T(8,128)(2,1)S(1)}, bf16[2,32,512]{2,1,0:T(8,128)(2,1)S(1)}, u32[]{:S(2)}, u32[]{:S(2)}) collective-permute-start(bf16[2,32,512]{2,1,0:T(8,128)(2,1)S(1)} %pad_maximum_fusion.5), channel_id=1, source_target_pairs={{0,32},{8,40},{16,48},{24,56},{32,0},{40,8},{48,16},{56,24},{64,96... | collective-permute-start | bytes 196616 | tf_op jit(solution)/shard_map/ppermute | solution.py:19
  31.8 11.5 %collective-permute-start.6 = (bf16[2,80,512]{2,1,0:T(8,128)(2,1)S(1)}, bf16[2,80,512]{2,1,0:T(8,128)(2,1)S(1)}, u32[]{:S(2)}, u32[]{:S(2)}) collective-permute-start(bf16[2,80,512]{2,1,0:T(8,128)(2,1)S(1)} %pad_maximum_fusion.3), channel_id=1, source_target_pairs={{0,16},{8,24},{16,0},{24,8},{32,48},{40,56},{48,32},{56,40},{64,80... | collective-permute-start | bytes 491528 | tf_op jit(solution)/shard_map/ppermute | solution.py:19
  43.4 12.1 %collective-permute-start.7 = (bf16[2,192,512]{2,1,0:T(8,128)(2,1)S(1)}, bf16[2,192,512]{2,1,0:T(8,128)(2,1)S(1)}, u32[]{:S(2)}, u32[]{:S(2)}) collective-permute-start(bf16[2,192,512]{2,1,0:T(8,128)(2,1)S(1)} %pad_maximum_fusion.2), channel_id=1, source_target_pairs={{0,8},{8,0},{16,24},{24,16},{32,40},{40,32},{48,56},{56,48},{64,72... | collective-permute-start | bytes 1179656 | tf_op jit(solution)/shard_map/ppermute | solution.py:19
  55.5 16.6 %collective-permute-start.8 = (bf16[256,512]{1,0:T(8,128)(2,1)S(1)}, bf16[256,512]{1,0:T(8,128)(2,1)S(1)}, u32[]{:S(2)}, u32[]{:S(2)}) collective-permute-start(bf16[256,512]{1,0:T(8,128)(2,1)S(1)} %constant_dynamic-update-slice_fusion.refs_4_), channel_id=1, source_target_pairs={{0,128},{128,256},{256,384},{384,0},{1,129},{129,257},{257,385},{3... | collective-permute-start | bytes 786440 | tf_op jit(solution)/shard_map/ppermute | solution.py:24
  57.4 14.7 %collective-permute-start.9 = (bf16[256,512]{1,0:T(8,128)(2,1)S(1)}, bf16[256,512]{1,0:T(8,128)(2,1)S(1)}, u32[]{:S(2)}, u32[]{:S(2)}) collective-permute-start(bf16[256,512]{1,0:T(8,128)(2,1)S(1)} %constant_dynamic-update-slice_fusion.refs_4_), channel_id=1, source_target_pairs={{0,384},{128,0},{256,128},{384,256},{1,385},{129,1},{257,129},{385... | collective-permute-start | bytes 786440 | tf_op jit(solution)/shard_map/ppermute | solution.py:24
  62.0 10.1 %collective-permute-start.10 = (bf16[256,512]{1,0:T(8,128)(2,1)S(1)}, bf16[256,512]{1,0:T(8,128)(2,1)S(1)}, u32[]{:S(2)}, u32[]{:S(2)}) collective-permute-start(bf16[256,512]{1,0:T(8,128)(2,1)S(1)} %constant_dynamic-update-slice_fusion.refs_4_), channel_id=1, source_target_pairs={{0,256},{128,384},{256,0},{384,128},{1,257},{129,385},{257,1},{385... | collective-permute-start | bytes 786440 | tf_op jit(solution)/shard_map/ppermute | solution.py:24
  64.0 30.8 %collective-permute-start.11 = (bf16[2,320,512]{2,1,0:T(8,128)(2,1)S(1)}, bf16[2,320,512]{2,1,0:T(8,128)(2,1)S(1)}, u32[]{:S(2)}, u32[]{:S(2)}) collective-permute-start(bf16[2,320,512]{2,1,0:T(8,128)(2,1)S(1)} %pad_maximum_fusion.1), channel_id=1, source_target_pairs={{0,4},{4,0},{1,5},{5,1},{2,6},{6,2},{3,7},{7,3},{8,12},{12,8},{9,1... | collective-permute-start | bytes 1966088 | tf_op jit(solution)/shard_map/ppermute | solution.py:19
  72.1 6.1 %copy-start.1 = (bf16[512,512]{1,0:T(8,128)(2,1)S(1)}, bf16[512,512]{1,0:T(8,128)(2,1)}, u32[]{:S(2)}) copy-start(bf16[512,512]{1,0:T(8,128)(2,1)} %key_ref.3) | copy-start | bytes 1572868
  72.1 6.1 %copy-start.3 = (bf16[512,512]{1,0:T(8,128)(2,1)S(1)}, bf16[512,512]{1,0:T(8,128)(2,1)}, u32[]{:S(2)}) copy-start(bf16[512,512]{1,0:T(8,128)(2,1)} %value_ref.3) | copy-start | bytes 1572868
  72.1 6.1 %copy-start.4 = (bf16[512,512]{1,0:T(8,128)(2,1)S(1)}, bf16[512,512]{1,0:T(8,128)(2,1)}, u32[]{:S(2)}) copy-start(bf16[512,512]{1,0:T(8,128)(2,1)} %query_ref.1) | copy-start | bytes 1572868
  73.3 46.8 %collective-permute-start.12 = (bf16[4,256,512]{2,1,0:T(8,128)(2,1)}, bf16[4,256,512]{2,1,0:T(8,128)(2,1)S(1)}, u32[]{:S(2)}, u32[]{:S(2)}) collective-permute-start(bf16[4,256,512]{2,1,0:T(8,128)(2,1)} %pad_maximum_fusion), channel_id=1, source_target_pairs={{0,4},{4,0},{1,5},{5,1},{2,6},{6,2},{3,7},{7,3},{8,12},{12,8},{9,1... | collective-permute-start | bytes 3145736 | tf_op jit(solution)/shard_map/ppermute | solution.py:19
  84.0 19.2 %collective-permute-start = (bf16[528,512]{1,0:T(8,128)(2,1)S(1)}, bf16[528,512]{1,0:T(8,128)(2,1)}, u32[]{:S(2)}, u32[]{:S(2)}) collective-permute-start(bf16[528,512]{1,0:T(8,128)(2,1)S(1)} %get-tuple-element.11.refs_0_), channel_id=1, source_target_pairs={{0,1},{1,2},{2,3},{3,0},{4,5},{5,6},{6,7},{7,4},{8,9},{9,10},{10,1... | collective-permute-start | bytes 1622024 | tf_op jit(solution)/shard_map/ppermute | solution.py:24
  87.8 15.5 %collective-permute-start.1 = (bf16[528,512]{1,0:T(8,128)(2,1)S(1)}, bf16[528,512]{1,0:T(8,128)(2,1)}, u32[]{:S(2)}, u32[]{:S(2)}) collective-permute-start(bf16[528,512]{1,0:T(8,128)(2,1)S(1)} %get-tuple-element.11.refs_0_), channel_id=1, source_target_pairs={{0,3},{1,0},{2,1},{3,2},{4,7},{5,4},{6,5},{7,6},{8,11},{9,8},{10,9... | collective-permute-start | bytes 1622024 | tf_op jit(solution)/shard_map/ppermute | solution.py:24
  90.6 23.3 %collective-permute-start.2 = (bf16[528,512]{1,0:T(8,128)(2,1)S(1)}, bf16[528,512]{1,0:T(8,128)(2,1)}, u32[]{:S(2)}, u32[]{:S(2)}) collective-permute-start(bf16[528,512]{1,0:T(8,128)(2,1)S(1)} %get-tuple-element.11.refs_0_), channel_id=1, source_target_pairs={{0,2},{1,3},{2,0},{3,1},{4,6},{5,7},{6,4},{7,5},{8,10},{9,11},{10,... | collective-permute-start | bytes 1622024 | tf_op jit(solution)/shard_map/ppermute | solution.py:24
  99.7 20.4 %all-to-all-start = ((bf16[4,144,512]{2,1,0:T(8,128)(2,1)}), bf16[4,144,512]{2,1,0:T(8,128)(2,1)S(1)}, u32[]{:S(2)}, u32[]{:S(2)}) async-start(bf16[4,144,512]{2,1,0:T(8,128)(2,1)} %shard_map.48), calls=%async_computation | async-start | bytes 1179648 | tf_op jit(solution)/shard_map/all_to_all | solution.py:357

commit v2 on v1

--- a/solution.py
+++ b/solution.py
@@ -73,33 +73,43 @@
     return high, middle, low
 
 
-def stat_tile(stat):
-    parts = jnp.concatenate(
-        [p.astype(jnp.float32) for p in three_parts(stat_rows(stat))], axis=0
-    )
+def stat_tile(rows):
+    parts = jnp.concatenate([p.astype(jnp.float32) for p in three_parts(rows)], axis=0)
     blank = jnp.zeros((16 - parts.shape[0], HEAD_DIM), jnp.float32)
     return jnp.concatenate([parts, blank], axis=0).astype(jnp.bfloat16)
+
+
+def read_stats(tile):
+    parts = tile.astype(jnp.float32)
+    return parts[0:4] + (parts[4:8] + parts[8:12])
+
+
+def repeated(rows, factor):
+    out = lax.broadcasted_iota(jnp.int32, (rows * factor, rows), 0)
+    source = lax.broadcasted_iota(jnp.int32, (rows * factor, rows), 1)
+    return jnp.where(out // factor == source, 1.0, 0.0).astype(jnp.bfloat16)
+
+
+def repeat_exactly(value, factor):
+    choice = repeated(value.shape[0], factor)
+    return jnp.dot(choice, value, preferred_element_type=jnp.float32).astype(jnp.bfloat16)
 
 
 def near_head(queries, keys, values):
     half = 2 * BLOCK
     q1, k1, v1 = pool(queries, 0.5), pool(keys, 0.5), pool(values, 1.0)
-    coarse = []
-    level = q1
-    for _ in range(4):
+    level = pool(q1, 0.5)
+    coarse = [level]
+    for factor in (2, 4, 8):
         level = pool(level, 0.5)
-        coarse.append(level)
-    fine = lax.broadcasted_iota(jnp.int32, (half, BLOCK), 0)
-    pooled = lax.broadcasted_iota(jnp.int32, (half, BLOCK), 1)
-    spread = jnp.where((fine >> 1) == pooled, 1.0, 0.0).astype(jnp.bfloat16)
+        coarse.append(repeat_exactly(level, factor))
     means, stats = [], []
     for group in range(2):
         rows = slice(group * half, (group + 1) * half)
         own = slice(group * BLOCK, (group + 1) * BLOCK)
         other = slice((1 - group) * BLOCK, (2 - group) * BLOCK)
-        q1_rows = jnp.dot(spread, q1[own], preferred_element_type=jnp.float32)
         near = scores(queries[rows], keys[rows])
-        level1 = scores(q1_rows.astype(jnp.bfloat16), k1[other])
+        level1 = scores(repeat_exactly(q1[own], 2), k1[other])
         peak = jnp.maximum(
             jnp.max(near, axis=1, keepdims=True), jnp.max(level1, axis=1, keepdims=True)
         )
@@ -110,7 +120,7 @@
         stats.append(peak + jnp.log2(mass))
     return (
         jnp.concatenate(means, axis=0),
-        stat_tile(jnp.concatenate(stats, axis=0)),
+        stat_tile(stat_rows(jnp.concatenate(stats, axis=0))),
         jnp.concatenate(coarse, axis=0),
     )
 
@@ -126,45 +136,24 @@
         out_ref[rows:, lanes] = tile
 
 
-def repeat_rows(value, factor, scratch_ref):
-    rows = value.shape[0]
-    for offset in range(factor):
-        scratch_ref[pl.ds(offset, rows, stride=factor), :] = value
-    return scratch_ref[0 : rows * factor, :]
-
-
-def merge(one, two):
-    top = jnp.maximum(one[0], two[0])
-    keep_one, keep_two = jnp.exp2(one[0] - top), jnp.exp2(two[0] - top)
-    return (top, one[1] * keep_one + two[1] * keep_two, one[2] * keep_one + two[2] * keep_two)
-
-
-def far_head(coarse, keys, values, scratch):
-    terms, start = [], 0
-    for level in range(4):
-        rows = BLOCK >> level
-        logits = scores(coarse[start : start + rows], keys[level])
-        start += rows
-        peak = jnp.max(logits, axis=1, keepdims=True)
-        prob = jnp.exp2(logits - peak)
-        mass = 2.0 ** (level + 2) * jnp.sum(prob, axis=1, keepdims=True)
-        terms.append(
-            (
-                jnp.broadcast_to(peak, (rows, HEAD_DIM)),
-                jnp.broadcast_to(mass, (rows, HEAD_DIM)),
-                weighted(prob, values[level]),
-            )
-        )
-    running = terms[3]
-    for level in (2, 1, 0):
-        spread = tuple(repeat_rows(v, 2, ref) for v, ref in zip(running, scratch))
-        running = merge(terms[level], spread)
-    peak, mass, total = running
-    return (total / mass).astype(jnp.bfloat16), stat_tile((peak + jnp.log2(mass))[:, 0:1])
-
-
-def far_kernel(coarse_ref, a_ref, b_ref, c_ref, d_ref, out_ref, *scratch):
-    for head in range(coarse_ref.shape[1] // HEAD_DIM):
+def far_head(coarse, keys, values):
+    logits = [scores(coarse[BLOCK * i : BLOCK * (i + 1)], keys[i]) for i in range(4)]
+    top = jnp.maximum(jnp.maximum(logits[0], logits[1]), jnp.maximum(logits[2], logits[3]))
+    peak = jnp.max(top, axis=1, keepdims=True)
+    prob = [jnp.exp2(x - peak) for x in logits]
+    mass = 4.0 * jnp.sum(
+        prob[0] + 2.0 * (prob[1] + 2.0 * (prob[2] + 2.0 * prob[3])), axis=1, keepdims=True
+    )
+    total = weighted(prob[0], values[0])
+    for i in range(1, 4):
+        total = total + weighted(prob[i], values[i])
+    return (total / mass).astype(jnp.bfloat16), peak + jnp.log2(mass)
+
+
+def far_kernel(coarse_ref, a_ref, b_ref, c_ref, d_ref, out_ref):
+    copies, heads = out_ref.shape[0], out_ref.shape[2] // HEAD_DIM
+    stats = []
+    for head in range(heads):
         lanes = slice(head * HEAD_DIM, (head + 1) * HEAD_DIM)
 
         def rows_of(side):
@@ -176,12 +165,29 @@
                 jnp.concatenate([a[:16], b[:16], c[:32], d[:32], d[64:96]], axis=0),
             )
 
-        mean, tile = far_head(
-            coarse_ref[:, lanes], rows_of(0), rows_of(1), scratch[3 * head : 3 * head + 3]
+        mean, stat = far_head(coarse_ref[:, lanes], rows_of(0), rows_of(1))
+        for copy in range(copies):
+            out_ref[copy, :BLOCK, lanes] = mean
+        stats.extend(p.astype(jnp.float32) for p in three_parts(stat_rows(stat)))
+    blank = jnp.zeros((16 - len(stats), BLOCK), jnp.float32)
+    stats = jnp.concatenate(stats + [blank], axis=0).astype(jnp.bfloat16)
+    source = lax.broadcasted_iota(jnp.int32, (BLOCK, BLOCK), 0)
+    fine = lax.broadcasted_iota(jnp.int32, (BLOCK, BLOCK), 1)
+    tiles = []
+    for tile in range(4):
+        choice = jnp.where(fine // 4 + tile * (BLOCK // 4) == source, 1.0, 0.0)
+        tiles.append(
+            jnp.dot(stats, choice.astype(jnp.bfloat16), preferred_element_type=jnp.float32)
         )
-        for copy in range(out_ref.shape[0]):
-            out_ref[copy, :BLOCK, lanes] = mean
-            out_ref[copy, BLOCK:, lanes] = tile
+    for head in range(heads):
+        lanes = slice(head * HEAD_DIM, (head + 1) * HEAD_DIM)
+        rows = [
+            jnp.concatenate([t[3 * head + p : 3 * head + p + 1] for t in tiles], axis=0)
+            for p in range(3)
+        ]
+        spread = stat_tile(rows[0] + (rows[1] + rows[2]))
+        for copy in range(copies):
+            out_ref[copy, BLOCK:, lanes] = spread
 
 
 def shape(dims, dtype=jnp.bfloat16):
@@ -189,15 +195,22 @@
 
 
 def pooled_levels(keys, values):
-    width = keys.shape[1]
+    rows, width = keys.shape
+    column = pl.BlockSpec((rows, HEAD_DIM), lambda h: (0, h))
+    sizes = [BLOCK >> level for level in range(4)]
     return pl.pallas_call(
-        pool_kernel, compiler_params=VMEM_LIMIT, out_shape=[shape((2, BLOCK >> level, width)) for level in range(4)]
-    )(keys, values)
+        pool_kernel,
+        grid=(width // HEAD_DIM,),
+        compiler_params=VMEM_LIMIT,
+        in_specs=[column] * 2,
+        out_specs=[pl.BlockSpec((2, n, HEAD_DIM), lambda h: (0, 0, h)) for n in sizes],
+        out_shape=[shape((2, n, width)) for n in sizes],
+    )(*(pltpu.with_memory_space_constraint(x, pltpu.HBM) for x in (keys, values)))
 
 
 def near_part(queries, keys, values, part, parts, buffers=()):
     rows, width = queries.shape
-    coarse, lanes = 240, width // parts
+    coarse, lanes = 4 * BLOCK, width // parts
     columns = pl.BlockSpec((rows, lanes), lambda i: (0, part))
     return pl.pallas_call(
         near_kernel,
@@ -219,12 +232,10 @@
 
 def far_part(coarse, pieces, copies):
     width = coarse.shape[1]
-    heads = width // HEAD_DIM
     return pl.pallas_call(
         far_kernel,
         compiler_params=VMEM_LIMIT,
         out_shape=shape((copies, BLOCK + 16, width)),
-        scratch_shapes=[pltpu.VMEM((BLOCK, HEAD_DIM), jnp.float32)] * (3 * heads),
     )(in_vmem(coarse), *map(in_vmem, pieces))
 
 
@@ -261,29 +272,16 @@
     heads = width // HEAD_DIM
     steps = (0, groups - 1, 1, 2)
     sources = [(x + step) & (groups - 1) for step in steps]
-    near_stats = [ref[rows:].astype(jnp.float32) for ref in near_refs]
-    far_stats = [far_ref[g, coarse_rows:] for g in sources]
-    coarse = lax.broadcasted_iota(jnp.int32, (HEAD_DIM, BLOCK), 0)
-    fine = lax.broadcasted_iota(jnp.int32, (HEAD_DIM, BLOCK), 1)
     depth = BLOCK // ratio
-    out_row = lax.broadcasted_iota(jnp.int32, (BLOCK, depth), 0)
-    in_row = lax.broadcasted_iota(jnp.int32, (BLOCK, depth), 1)
-    spread_rows = jnp.where(out_row // ratio == in_row, 1.0, 0.0).astype(jnp.bfloat16)
+    spread_rows = repeated(depth, ratio)
+    shares = []
     for i, g in enumerate(sources):
-        shares = []
-        for tile in range(tiles):
-            chosen = jnp.where(fine // ratio + tile * depth == coarse, 1.0, 0.0)
-            chosen = chosen.astype(jnp.bfloat16)
-            for head in range(heads):
-                lanes = slice(head * HEAD_DIM, (head + 1) * HEAD_DIM)
-                parts = jnp.dot(far_stats[i][:, lanes], chosen, preferred_element_type=jnp.float32)
-                far = parts[0:1] + (parts[1:2] + parts[2:3])
-                part = [near_stats[i][p * tiles + tile : p * tiles + tile + 1, lanes] for p in range(3)]
-                near = part[0] + (part[1] + part[2])
-                shares.append(1.0 / (1.0 + jnp.exp2(jnp.minimum(far - near, 120.0))))
-        shares = jnp.concatenate(shares, axis=0)
-        blank = jnp.zeros((BLOCK - shares.shape[0], BLOCK), jnp.float32)
-        shares = jnp.concatenate([shares, blank], axis=0).T
+        excess = read_stats(far_ref[g, coarse_rows:]) - read_stats(near_refs[i][rows:])
+        share = 1.0 / (1.0 + jnp.exp2(jnp.minimum(excess, 120.0)))
+        shares.extend(share[:, h * HEAD_DIM : (h + 1) * HEAD_DIM] for h in range(heads))
+    blank = jnp.zeros((BLOCK - groups * heads * tiles, BLOCK), jnp.float32)
+    shares = jnp.concatenate(shares + [blank], axis=0).T
+    for i, g in enumerate(sources):
         for tile in range(tiles):
             far = jnp.dot(
                 spread_rows,
@@ -291,12 +289,9 @@
                 preferred_element_type=jnp.float32,
             )
             near = near_refs[i][tile * BLOCK : (tile + 1) * BLOCK].astype(jnp.float32)
+            columns = [(i * heads + h) * tiles + tile for h in range(heads)]
             share = jnp.concatenate(
-                [
-                    jnp.broadcast_to(shares[:, k : k + 1], (BLOCK, HEAD_DIM))
-                    for k in range(tile * heads, (tile + 1) * heads)
-                ],
-                axis=1,
+                [jnp.broadcast_to(shares[:, k : k + 1], (BLOCK, HEAD_DIM)) for k in columns], axis=1
             )
             attended = (far + share * (near - far)).astype(jnp.bfloat16)
             attended_ref[g, tile * BLOCK : (tile + 1) * BLOCK] = attended
@@ -324,7 +319,11 @@
     heads, ring = lax.axis_size("head"), lax.axis_size("z")
     width = queries.shape[1]
 
-    turn = [(y * heads + x, x * heads + y) for y in range(heads) for x in range(heads)]
+    def turned(value, step):
+        pairs = [
+            (y * heads + x, (x + step) % heads * heads + y) for y in range(heads) for x in range(heads)
+        ]
+        return lax.ppermute(value, ("y", "head"), pairs)
 
     def across(z):
         return (z + (4 if z & 4 else 12)) % 16
@@ -335,7 +334,7 @@
     def joined(weights):
         return weights.reshape(-1, width)
 
-    w_own = lax.ppermute(out_weight.T, ("y", "head"), turn)
+    w_own = out_weight.T
     p2, p3, p4, p5 = pooled_levels(key_vectors, values)
     w_across = lax.ppermute(w_own, "z", [(z, across(z)) for z in range(ring)])
     weights = jnp.concatenate([w_own, w_across], axis=0)
@@ -350,9 +349,9 @@
     weights = jnp.concatenate([weights, joined(c[:, 128:])], axis=0)
     over = shift(near, "head", 2)
     d = swap(jnp.concatenate([a[:, :16], b[:, :48], c[:, :128], p2], axis=1), "core", 1)
-    own = [weights]
-    for step in (1, -1, 2):
-        own.append(shift(weights, "y", step))
+    own = []
+    for step in (0, 1, -1, 2):
+        own.append(turned(weights, step))
     far = far_part(coarse, (a, b, c, d), heads)
     far = lax.all_to_all(far, "head", 0, 0)
     other = swap(jnp.stack(own), "core", 1)

time: 128 us -> 166 us (1.30)
  waiting for transfers between devices: 44.9 us -> 80.3 us
  Pallas kernels: 17.9 us -> 20.2 us
  local copies, waits for them, and re-layouts: 2.17 us -> 0.09 us
    ppermute x1 -> x4, waiting for transfers between devices: 0.01 us -> 35 us  [turned(): return lax.ppermute(value, ('y', 'head'), pairs)]
    ppermute x1 -> x4, starting transfers between devices: 1.36 us -> 12.5 us  [turned(): return lax.ppermute(value, ('y', 'head'), pairs)]
    ppermute x5, starting transfers between devices: 22 us -> 15.6 us  [swap(): lax.ppermute(value, axis, [(s, s ^ mask) for s in range(lax.axis_size(axi...]
    pallas_call x1, Pallas kernels: 1.4 us -> 6.1 us  [pooled_levels(): pl.pallas_call(pool_kernel, grid=(width // HEAD_DIM,), compiler_params=VM...]
    ppermute x6 -> x3, waiting for transfers between devices: 10.6 us -> 14.2 us  [shift(): lax.ppermute(value, axis, [(s, (s + step) % size) for s in range(size)])]
    ppermute x6 -> x3, starting transfers between devices: 19.2 us -> 15.8 us  [shift(): lax.ppermute(value, axis, [(s, (s + step) % size) for s in range(size)])]
    all_to_all x1, waiting for transfers between devices: 6.21 us -> 3.05 us  [body(): far = lax.all_to_all(far, 'head', 0, 0)]
    pallas_call x1, Pallas kernels: 4.89 us -> 2.46 us  [far_part(): pl.pallas_call(far_kernel, compiler_params=VMEM_LIMIT, out_shape=shape((c...]
  transfers between devices with their start and end apart: 14 -> 14, of which waited for: 5 -> 7; matrix products, arithmetic and copies ran while one was open for 1% -> 1% of each run, Pallas kernels for 10% -> 9%
where the time goes in v2:
time: 166 us; the launch traced here: 163 us
  waiting for transfers between devices  80.3 us (48%)
  starting transfers between devices  60.8 us (37%)
  Pallas kernels  20.2 us (12%)
    ppermute x4, waiting for transfers between devices, turned(): return lax.ppermute(value, ('y', 'head'), pairs)  35 us
    ppermute x5, waiting for transfers between devices, swap(): lax.ppermute(value, axis, [(s, s ^ mask) for s in range(lax.axis_size(axi...  28.1 us
    ppermute x3, starting transfers between devices, shift(): lax.ppermute(value, axis, [(s, (s + step) % size) for s in range(size)])  15.8 us
    ppermute x5, starting transfers between devices, swap(): lax.ppermute(value, axis, [(s, s ^ mask) for s in range(lax.axis_size(axi...  15.6 us
    ppermute x3, waiting for transfers between devices, shift(): lax.ppermute(value, axis, [(s, (s + step) % size) for s in range(size)])  14.2 us
    ppermute x1, starting transfers between devices, body(): w_across = lax.ppermute(w_own, 'z', [(z, across(z)) for z in range(ring)])  13.4 us
    ppermute x4, starting transfers between devices, turned(): return lax.ppermute(value, ('y', 'head'), pairs)  12.5 us
    pallas_call x1, Pallas kernels, near_part(): pl.pallas_call(near_kernel, grid=(1,), compiler_params=VMEM_LIMIT, in_spe...  6.36 us
  transfers between devices with their start and end apart: 14, of which 7 were waited for; matrix products, arithmetic and copies ran while one was open for 1% of the time, Pallas kernels for 9%

profile of v2, /device:TPU:1, one launch (start us, length us, event | category | flops | bytes accessed | tf_op | source)
XLA Modules:
  0.0 163.0 jit_solution(1975526632298724488)
XLA Ops:
  0.0 0.0 copy-start.3
  0.0 13.4 %collective-permute-start.3 = (bf16[16,512]{1,0:T(8,128)(2,1)}, bf16[16,512]{1,0:T(8,128)(2,1)S(1)}, u32[]{:S(2)}, u32[]{:S(2)}) collective-permute-start(bf16[16,512]{1,0:T(8,128)(2,1)} %bitcast.28), channel_id=1, source_target_pairs={{0,96},{8,104},{16,112},{24,120},{32,64},{40,72},{48,80},{56,88},{... | collective-permute-start | bytes 49160 | tf_op jit(solution)/shard_map/ppermute | solution.py:339
  13.4 6.1 %shard_map.47 = (bf16[2,128,512]{2,1,0:T(8,128)(2,1)S(1)}, bf16[2,64,512]{2,1,0:T(8,128)(2,1)S(1)}, bf16[2,32,512]{2,1,0:T(8,128)(2,1)S(1)}, bf16[2,16,512]{2,1,0:T(8,128)(2,1)S(1)}) custom-call(bf16[512,512]{1,0:T(8,128)(2,1)} %key_ref.3, bf16[512,512]{1,0:T(8,128)(2,1)} %value_ref.3), custom_call_target="tpu_custom_call" | custom-call | tf_op jit(solution)/shard_map/pallas_call | solution.py:201
  19.5 0.0 collective-permute-done.3
  19.5 0.0 copy-done.3
  19.6 5.2 %collective-permute-start.4 = (bf16[2,32,512]{2,1,0:T(8,128)(2,1)S(1)}, bf16[2,32,512]{2,1,0:T(8,128)(2,1)S(1)}, u32[]{:S(2)}, u32[]{:S(2)}) collective-permute-start(bf16[2,32,512]{2,1,0:T(8,128)(2,1)S(1)} %pad_maximum_fusion.5), channel_id=1, source_target_pairs={{0,32},{8,40},{16,48},{24,56},{32,0},{40,8},{48,16},{56,24},{64,96... | collective-permute-start | bytes 196616 | tf_op jit(solution)/shard_map/ppermute | solution.py:19
  24.7 8.4 %collective-permute-done.4.a_ref = bf16[2,32,512]{2,1,0:T(8,128)(2,1)S(1)} collective-permute-done((bf16[2,32,512]{2,1,0:T(8,128)(2,1)S(1)}, bf16[2,32,512]{2,1,0:T(8,128)(2,1)S(1)}, u32[]{:S(2)}, u32[]{:S(2)}) %collective-permute-start.4) | collective-permute-done | bytes 65568 | tf_op jit(solution)/shard_map/ppermute | solution.py:19
  33.2 1.9 %collective-permute-start.5 = (bf16[2,80,512]{2,1,0:T(8,128)(2,1)S(1)}, bf16[2,80,512]{2,1,0:T(8,128)(2,1)S(1)}, u32[]{:S(2)}, u32[]{:S(2)}) collective-permute-start(bf16[2,80,512]{2,1,0:T(8,128)(2,1)S(1)} %pad_maximum_fusion.3), channel_id=1, source_target_pairs={{0,16},{8,24},{16,0},{24,8},{32,48},{40,56},{48,32},{56,40},{64,80... | collective-permute-start | bytes 491528 | tf_op jit(solution)/shard_map/ppermute | solution.py:19
  35.1 9.6 %collective-permute-done.5.b_ref = bf16[2,80,512]{2,1,0:T(8,128)(2,1)S(1)} collective-permute-done((bf16[2,80,512]{2,1,0:T(8,128)(2,1)S(1)}, bf16[2,80,512]{2,1,0:T(8,128)(2,1)S(1)}, u32[]{:S(2)}, u32[]{:S(2)}) %collective-permute-start.5) | collective-permute-done | bytes 163872 | tf_op jit(solution)/shard_map/ppermute | solution.py:19
  44.8 1.9 %collective-permute-start.6 = (bf16[2,192,512]{2,1,0:T(8,128)(2,1)S(1)}, bf16[2,192,512]{2,1,0:T(8,128)(2,1)S(1)}, u32[]{:S(2)}, u32[]{:S(2)}) collective-permute-start(bf16[2,192,512]{2,1,0:T(8,128)(2,1)S(1)} %pad_maximum_fusion.2), channel_id=1, source_target_pairs={{0,8},{8,0},{16,24},{24,16},{32,40},{40,32},{48,56},{56,48},{64,72... | collective-permute-start | bytes 1179656 | tf_op jit(solution)/shard_map/ppermute | solution.py:19
  46.7 10.1 %collective-permute-done.6.c_ref = bf16[2,192,512]{2,1,0:T(8,128)(2,1)S(1)} collective-permute-done((bf16[2,192,512]{2,1,0:T(8,128)(2,1)S(1)}, bf16[2,192,512]{2,1,0:T(8,128)(2,1)S(1)}, u32[]{:S(2)}, u32[]{:S(2)}) %collective-permute-start.6) | collective-permute-done | bytes 393248 | tf_op jit(solution)/shard_map/ppermute | solution.py:19
  56.9 4.8 %collective-permute-start.10 = (bf16[256,512]{1,0:T(8,128)(2,1)S(1)}, bf16[256,512]{1,0:T(8,128)(2,1)S(1)}, u32[]{:S(2)}, u32[]{:S(2)}) collective-permute-start(bf16[256,512]{1,0:T(8,128)(2,1)S(1)} %constant_dynamic-update-slice_fusion), channel_id=1, source_target_pairs={{0,256},{1,384},{2,0},{3,128},{128,257},{129,385},{130,1},{131,129... | collective-permute-start | bytes 786440 | tf_op jit(solution)/shard_map/ppermute | solution.py:326
  61.7 4.4 %collective-permute-start.9 = (bf16[256,512]{1,0:T(8,128)(2,1)S(1)}, bf16[256,512]{1,0:T(8,128)(2,1)S(1)}, u32[]{:S(2)}, u32[]{:S(2)}) collective-permute-start(bf16[256,512]{1,0:T(8,128)(2,1)S(1)} %constant_dynamic-update-slice_fusion), channel_id=1, source_target_pairs={{0,384},{1,0},{2,128},{3,256},{128,385},{129,1},{130,129},{131,257... | collective-permute-start | bytes 786440 | tf_op jit(solution)/shard_map/ppermute | solution.py:326
  66.1 2.6 %collective-permute-start.8 = (bf16[256,512]{1,0:T(8,128)(2,1)S(1)}, bf16[256,512]{1,0:T(8,128)(2,1)S(1)}, u32[]{:S(2)}, u32[]{:S(2)}) collective-permute-start(bf16[256,512]{1,0:T(8,128)(2,1)S(1)} %constant_dynamic-update-slice_fusion), channel_id=1, source_target_pairs={{0,128},{1,256},{2,384},{3,0},{128,129},{129,257},{130,385},{131,1... | collective-permute-start | bytes 786440 | tf_op jit(solution)/shard_map/ppermute | solution.py:326
  68.7 0.7 collective-permute-start.7
  69.5 4.1 %collective-permute-start.11 = (bf16[2,320,512]{2,1,0:T(8,128)(2,1)S(1)}, bf16[2,320,512]{2,1,0:T(8,128)(2,1)S(1)}, u32[]{:S(2)}, u32[]{:S(2)}) collective-permute-start(bf16[2,320,512]{2,1,0:T(8,128)(2,1)S(1)} %pad_maximum_fusion.1), channel_id=1, source_target_pairs={{0,4},{4,0},{1,5},{5,1},{2,6},{6,2},{3,7},{7,3},{8,12},{12,8},{9,1... | collective-permute-start | bytes 1966088 | tf_op jit(solution)/shard_map/ppermute | solution.py:19
  73.6 0.0 collective-permute-done.10.refs_7_
  73.6 0.5 collective-permute-done.9.refs_6_
  74.1 34.5 %collective-permute-done.8.refs_5_ = bf16[256,512]{1,0:T(8,128)(2,1)S(1)} collective-permute-done((bf16[256,512]{1,0:T(8,128)(2,1)S(1)}, bf16[256,512]{1,0:T(8,128)(2,1)S(1)}, u32[]{:S(2)}, u32[]{:S(2)}) %collective-permute-start.8) | collective-permute-done | bytes 262176 | tf_op jit(solution)/shard_map/ppermute | solution.py:326
  108.6 0.0 collective-permute-done.7.refs_4_
  108.6 0.0 copy-start
  108.6 0.0 copy-start.1
  108.6 0.0 copy-start.2
  108.6 1.1 pad_maximum_fusion
  109.7 2.5 %collective-permute-start.12 = (bf16[4,256,512]{2,1,0:T(8,128)(2,1)}, bf16[4,256,512]{2,1,0:T(8,128)(2,1)S(1)}, u32[]{:S(2)}, u32[]{:S(2)}) collective-permute-start(bf16[4,256,512]{2,1,0:T(8,128)(2,1)} %pad_maximum_fusion), channel_id=1, source_target_pairs={{0,4},{4,0},{1,5},{5,1},{2,6},{6,2},{3,7},{7,3},{8,12},{12,8},{9,1... | collective-permute-start | bytes 3145736 | tf_op jit(solution)/shard_map/ppermute | solution.py:19
  112.2 0.0 copy-done
  112.2 0.0 copy-done.1
  112.3 0.0 copy-done.2
  112.3 6.4 %shard_map.46 = (bf16[528,512]{1,0:T(8,128)(2,1)S(1)}, bf16[512,512]{1,0:T(8,128)(2,1)S(1)}) custom-call(bf16[512,512]{1,0:T(8,128)(2,1)S(1)} %copy-done.2, bf16[512,512]{1,0:T(8,128)(2,1)S(1)} %copy-done, bf16[512,512]{1,0:T(8,128)(2,1)S(1)} %copy-done.1), custom_call_target="tpu_custom_call" | custom-call | tf_op jit(solution)/shard_map/pallas_call | solution.py:215
  118.6 1.9 %collective-permute-start.2 = (bf16[528,512]{1,0:T(8,128)(2,1)S(1)}, bf16[528,512]{1,0:T(8,128)(2,1)}, u32[]{:S(2)}, u32[]{:S(2)}) collective-permute-start(bf16[528,512]{1,0:T(8,128)(2,1)S(1)} %get-tuple-element.11.refs_0_), channel_id=1, source_target_pairs={{0,2},{1,3},{2,0},{3,1},{4,6},{5,7},{6,4},{7,5},{8,10},{9,11},{10,... | collective-permute-start | bytes 1622024 | tf_op jit(solution)/shard_map/ppermute | solution.py:24
  120.6 11.4 %collective-permute-start.1 = (bf16[528,512]{1,0:T(8,128)(2,1)S(1)}, bf16[528,512]{1,0:T(8,128)(2,1)}, u32[]{:S(2)}, u32[]{:S(2)}) collective-permute-start(bf16[528,512]{1,0:T(8,128)(2,1)S(1)} %get-tuple-element.11.refs_0_), channel_id=1, source_target_pairs={{0,3},{1,0},{2,1},{3,2},{4,7},{5,4},{6,5},{7,6},{8,11},{9,8},{10,9... | collective-permute-start | bytes 1622024 | tf_op jit(solution)/shard_map/ppermute | solution.py:24
  132.0 2.5 %collective-permute-start = (bf16[528,512]{1,0:T(8,128)(2,1)S(1)}, bf16[528,512]{1,0:T(8,128)(2,1)}, u32[]{:S(2)}, u32[]{:S(2)}) collective-permute-start(bf16[528,512]{1,0:T(8,128)(2,1)S(1)} %get-tuple-element.11.refs_0_), channel_id=1, source_target_pairs={{0,1},{1,2},{2,3},{3,0},{4,5},{5,6},{6,7},{7,4},{8,9},{9,10},{10,1... | collective-permute-start | bytes 1622024 | tf_op jit(solution)/shard_map/ppermute | solution.py:24
  134.5 0.0 collective-permute-done.11.d_ref
  134.5 2.5 %shard_map.48 = bf16[4,144,512]{2,1,0:T(8,128)(2,1)} custom-call(bf16[512,512]{1,0:T(8,128)(2,1)S(1)} %get-tuple-element.15.coarse_ref, bf16[2,32,512]{2,1,0:T(8,128)(2,1)S(1)} %collective-permute-done.4.a_ref, bf16[2,80,512]{2,1,0:T(8,128)(2,1)S(1)} %collective-permute-done.5.b_ref, bf16[2,192,512]{2,1,0:T(8,128)(2,1)S(1)} %collective-permute-done.6.c_ref, ...), custom_call_target="tpu_custom_call" | custom-call | tf_op jit(solution)/shard_map/pallas_call | solution.py:235
  136.9 3.5 %all-to-all-start = ((bf16[4,144,512]{2,1,0:T(8,128)(2,1)}), bf16[4,144,512]{2,1,0:T(8,128)(2,1)S(1)}, u32[]{:S(2)}, u32[]{:S(2)}) async-start(bf16[4,144,512]{2,1,0:T(8,128)(2,1)} %shard_map.48), calls=%async_computation | async-start | bytes 1179648 | tf_op jit(solution)/shard_map/all_to_all | solution.py:356
  140.4 0.1 pad_add_fusion.place_ref
  140.5 0.0 collective-permute-done.2.refs_3_
  140.5 14.2 %collective-permute-done.1.refs_2_ = bf16[528,512]{1,0:T(8,128)(2,1)} collective-permute-done((bf16[528,512]{1,0:T(8,128)(2,1)S(1)}, bf16[528,512]{1,0:T(8,128)(2,1)}, u32[]{:S(2)}, u32[]{:S(2)}) %collective-permute-start.1) | collective-permute-done | bytes 540704 | tf_op jit(solution)/shard_map/ppermute | solution.py:24
  154.7 0.0 collective-permute-done.refs_1_
  154.7 3.1 %all-to-all-done.refs_8_ = bf16[4,144,512]{2,1,0:T(8,128)(2,1)S(1)} async-done(((bf16[4,144,512]{2,1,0:T(8,128)(2,1)}), bf16[4,144,512]{2,1,0:T(8,128)(2,1)S(1)}, u32[]{:S(2)}, u32[]{:S(2)}) %all-to-all-start) | async-done | bytes 589856 | tf_op jit(solution)/shard_map/all_to_all | solution.py:356
  157.7 0.0 collective-permute-done.12.refs_9_
  157.7 5.3 %shard_map.49 = bf16[512,512]{1,0:T(8,128)(2,1)} custom-call(s32[4]{0:T(128)S(1)} %pad_add_fusion.place_ref, bf16[528,512]{1,0:T(8,128)(2,1)S(1)} %get-tuple-element.11.refs_0_, bf16[528,512]{1,0:T(8,128)(2,1)} %collective-permute-done.refs_1_, bf16[528,512]{1,0:T(8,128)(2,1)} %collective-permute-done.1.refs_2_, ...), custom_call_target="tpu_custom_call" | custom-call | tf_op jit(solution)/shard_map/pallas_call | solution.py:309
  (17 shorter events, 0.2 us)
Async XLA Ops:
  0.0 19.5 %copy-start.3 = (bf16[512,16]{0,1:T(8,128)(2,1)S(1)}, bf16[512,16]{0,1:T(8,128)(2,1)}, u32[]{:S(2)}) copy-start(bf16[512,16]{0,1:T(8,128)(2,1)} %param.7) | copy-start | bytes 49156
  0.0 19.5 %collective-permute-start.3 = (bf16[16,512]{1,0:T(8,128)(2,1)}, bf16[16,512]{1,0:T(8,128)(2,1)S(1)}, u32[]{:S(2)}, u32[]{:S(2)}) collective-permute-start(bf16[16,512]{1,0:T(8,128)(2,1)} %bitcast.28), channel_id=1, source_target_pairs={{0,96},{8,104},{16,112},{24,120},{32,64},{40,72},{48,80},{56,88},{... | collective-permute-start | bytes 49160 | tf_op jit(solution)/shard_map/ppermute | solution.py:339
  19.6 13.6 %collective-permute-start.4 = (bf16[2,32,512]{2,1,0:T(8,128)(2,1)S(1)}, bf16[2,32,512]{2,1,0:T(8,128)(2,1)S(1)}, u32[]{:S(2)}, u32[]{:S(2)}) collective-permute-start(bf16[2,32,512]{2,1,0:T(8,128)(2,1)S(1)} %pad_maximum_fusion.5), channel_id=1, source_target_pairs={{0,32},{8,40},{16,48},{24,56},{32,0},{40,8},{48,16},{56,24},{64,96... | collective-permute-start | bytes 196616 | tf_op jit(solution)/shard_map/ppermute | solution.py:19
  33.2 11.5 %collective-permute-start.5 = (bf16[2,80,512]{2,1,0:T(8,128)(2,1)S(1)}, bf16[2,80,512]{2,1,0:T(8,128)(2,1)S(1)}, u32[]{:S(2)}, u32[]{:S(2)}) collective-permute-start(bf16[2,80,512]{2,1,0:T(8,128)(2,1)S(1)} %pad_maximum_fusion.3), channel_id=1, source_target_pairs={{0,16},{8,24},{16,0},{24,8},{32,48},{40,56},{48,32},{56,40},{64,80... | collective-permute-start | bytes 491528 | tf_op jit(solution)/shard_map/ppermute | solution.py:19
  44.8 12.1 %collective-permute-start.6 = (bf16[2,192,512]{2,1,0:T(8,128)(2,1)S(1)}, bf16[2,192,512]{2,1,0:T(8,128)(2,1)S(1)}, u32[]{:S(2)}, u32[]{:S(2)}) collective-permute-start(bf16[2,192,512]{2,1,0:T(8,128)(2,1)S(1)} %pad_maximum_fusion.2), channel_id=1, source_target_pairs={{0,8},{8,0},{16,24},{24,16},{32,40},{40,32},{48,56},{56,48},{64,72... | collective-permute-start | bytes 1179656 | tf_op jit(solution)/shard_map/ppermute | solution.py:19
  56.9 16.7 %collective-permute-start.10 = (bf16[256,512]{1,0:T(8,128)(2,1)S(1)}, bf16[256,512]{1,0:T(8,128)(2,1)S(1)}, u32[]{:S(2)}, u32[]{:S(2)}) collective-permute-start(bf16[256,512]{1,0:T(8,128)(2,1)S(1)} %constant_dynamic-update-slice_fusion), channel_id=1, source_target_pairs={{0,256},{1,384},{2,0},{3,128},{128,257},{129,385},{130,1},{131,129... | collective-permute-start | bytes 786440 | tf_op jit(solution)/shard_map/ppermute | solution.py:326
  61.7 12.4 %collective-permute-start.9 = (bf16[256,512]{1,0:T(8,128)(2,1)S(1)}, bf16[256,512]{1,0:T(8,128)(2,1)S(1)}, u32[]{:S(2)}, u32[]{:S(2)}) collective-permute-start(bf16[256,512]{1,0:T(8,128)(2,1)S(1)} %constant_dynamic-update-slice_fusion), channel_id=1, source_target_pairs={{0,384},{1,0},{2,128},{3,256},{128,385},{129,1},{130,129},{131,257... | collective-permute-start | bytes 786440 | tf_op jit(solution)/shard_map/ppermute | solution.py:326
  66.1 42.5 %collective-permute-start.8 = (bf16[256,512]{1,0:T(8,128)(2,1)S(1)}, bf16[256,512]{1,0:T(8,128)(2,1)S(1)}, u32[]{:S(2)}, u32[]{:S(2)}) collective-permute-start(bf16[256,512]{1,0:T(8,128)(2,1)S(1)} %constant_dynamic-update-slice_fusion), channel_id=1, source_target_pairs={{0,128},{1,256},{2,384},{3,0},{128,129},{129,257},{130,385},{131,1... | collective-permute-start | bytes 786440 | tf_op jit(solution)/shard_map/ppermute | solution.py:326
  68.7 39.9 %collective-permute-start.7 = (bf16[256,512]{1,0:T(8,128)(2,1)S(1)}, bf16[256,512]{1,0:T(8,128)(2,1)S(1)}, u32[]{:S(2)}, u32[]{:S(2)}) collective-permute-start(bf16[256,512]{1,0:T(8,128)(2,1)S(1)} %constant_dynamic-update-slice_fusion), channel_id=1, source_target_pairs={{0,0},{1,128},{2,256},{3,384},{128,1},{129,129},{130,257},{131,385... | collective-permute-start | bytes 786440 | tf_op jit(solution)/shard_map/ppermute | solution.py:326
  69.5 65.0 %collective-permute-start.11 = (bf16[2,320,512]{2,1,0:T(8,128)(2,1)S(1)}, bf16[2,320,512]{2,1,0:T(8,128)(2,1)S(1)}, u32[]{:S(2)}, u32[]{:S(2)}) collective-permute-start(bf16[2,320,512]{2,1,0:T(8,128)(2,1)S(1)} %pad_maximum_fusion.1), channel_id=1, source_target_pairs={{0,4},{4,0},{1,5},{5,1},{2,6},{6,2},{3,7},{7,3},{8,12},{12,8},{9,1... | collective-permute-start | bytes 1966088 | tf_op jit(solution)/shard_map/ppermute | solution.py:19
  108.6 3.6 %copy-start = (bf16[512,512]{1,0:T(8,128)(2,1)S(1)}, bf16[512,512]{1,0:T(8,128)(2,1)}, u32[]{:S(2)}) copy-start(bf16[512,512]{1,0:T(8,128)(2,1)} %key_ref.3) | copy-start | bytes 1572868
  108.6 3.6 %copy-start.1 = (bf16[512,512]{1,0:T(8,128)(2,1)S(1)}, bf16[512,512]{1,0:T(8,128)(2,1)}, u32[]{:S(2)}) copy-start(bf16[512,512]{1,0:T(8,128)(2,1)} %value_ref.3) | copy-start | bytes 1572868
  108.6 3.6 %copy-start.2 = (bf16[512,512]{1,0:T(8,128)(2,1)S(1)}, bf16[512,512]{1,0:T(8,128)(2,1)}, u32[]{:S(2)}) copy-start(bf16[512,512]{1,0:T(8,128)(2,1)} %query_ref.1) | copy-start | bytes 1572868
  109.7 48.0 %collective-permute-start.12 = (bf16[4,256,512]{2,1,0:T(8,128)(2,1)}, bf16[4,256,512]{2,1,0:T(8,128)(2,1)S(1)}, u32[]{:S(2)}, u32[]{:S(2)}) collective-permute-start(bf16[4,256,512]{2,1,0:T(8,128)(2,1)} %pad_maximum_fusion), channel_id=1, source_target_pairs={{0,4},{4,0},{1,5},{5,1},{2,6},{6,2},{3,7},{7,3},{8,12},{12,8},{9,1... | collective-permute-start | bytes 3145736 | tf_op jit(solution)/shard_map/ppermute | solution.py:19
  118.6 21.9 %collective-permute-start.2 = (bf16[528,512]{1,0:T(8,128)(2,1)S(1)}, bf16[528,512]{1,0:T(8,128)(2,1)}, u32[]{:S(2)}, u32[]{:S(2)}) collective-permute-start(bf16[528,512]{1,0:T(8,128)(2,1)S(1)} %get-tuple-element.11.refs_0_), channel_id=1, source_target_pairs={{0,2},{1,3},{2,0},{3,1},{4,6},{5,7},{6,4},{7,5},{8,10},{9,11},{10,... | collective-permute-start | bytes 1622024 | tf_op jit(solution)/shard_map/ppermute | solution.py:24
  120.6 34.1 %collective-permute-start.1 = (bf16[528,512]{1,0:T(8,128)(2,1)S(1)}, bf16[528,512]{1,0:T(8,128)(2,1)}, u32[]{:S(2)}, u32[]{:S(2)}) collective-permute-start(bf16[528,512]{1,0:T(8,128)(2,1)S(1)} %get-tuple-element.11.refs_0_), channel_id=1, source_target_pairs={{0,3},{1,0},{2,1},{3,2},{4,7},{5,4},{6,5},{7,6},{8,11},{9,8},{10,9... | collective-permute-start | bytes 1622024 | tf_op jit(solution)/shard_map/ppermute | solution.py:24
  132.0 22.7 %collective-permute-start = (bf16[528,512]{1,0:T(8,128)(2,1)S(1)}, bf16[528,512]{1,0:T(8,128)(2,1)}, u32[]{:S(2)}, u32[]{:S(2)}) collective-permute-start(bf16[528,512]{1,0:T(8,128)(2,1)S(1)} %get-tuple-element.11.refs_0_), channel_id=1, source_target_pairs={{0,1},{1,2},{2,3},{3,0},{4,5},{5,6},{6,7},{7,4},{8,9},{9,10},{10,1... | collective-permute-start | bytes 1622024 | tf_op jit(solution)/shard_map/ppermute | solution.py:24
  136.9 20.8 %all-to-all-start = ((bf16[4,144,512]{2,1,0:T(8,128)(2,1)}), bf16[4,144,512]{2,1,0:T(8,128)(2,1)S(1)}, u32[]{:S(2)}, u32[]{:S(2)}) async-start(bf16[4,144,512]{2,1,0:T(8,128)(2,1)} %shard_map.48), calls=%async_computation | async-start | bytes 1179648 | tf_op jit(solution)/shard_map/all_to_all | solution.py:356

commit v3 on v2

--- a/solution.py
+++ b/solution.py
@@ -51,9 +51,19 @@
     return jnp.dot(prob.astype(jnp.bfloat16), value_rows, preferred_element_type=jnp.float32)
 
 
-def pool_kernel(key_ref, value_ref, p2_ref, p3_ref, p4_ref, p5_ref):
-    for side, (ref, weight) in enumerate(((key_ref, 0.5), (value_ref, 1.0))):
-        level = pool(ref[...], weight)
+def pool_kernel(key_ref, value_ref, p2_ref, p3_ref, p4_ref, p5_ref, held_ref, sems):
+    rows = key_ref.shape[0] // 4
+    copies = []
+    for side, ref in enumerate((key_ref, value_ref)):
+        for part in range(4):
+            at = pl.ds(part * rows, rows)
+            copy = pltpu.make_async_copy(ref.at[at], held_ref.at[side, at], sems.at[side, part])
+            copy.start()
+            copies.append(copy)
+    for copy in copies:
+        copy.wait()
+    for side, weight in enumerate((0.5, 1.0)):
+        level = pool(held_ref[side], weight)
         for out_ref in (p2_ref, p3_ref, p4_ref, p5_ref):
             level = pool(level, weight)
             out_ref[side] = level
@@ -196,15 +206,16 @@
 
 def pooled_levels(keys, values):
     rows, width = keys.shape
-    column = pl.BlockSpec((rows, HEAD_DIM), lambda h: (0, h))
-    sizes = [BLOCK >> level for level in range(4)]
+    hbm = pl.BlockSpec(memory_space=pl.ANY)
     return pl.pallas_call(
         pool_kernel,
-        grid=(width // HEAD_DIM,),
         compiler_params=VMEM_LIMIT,
-        in_specs=[column] * 2,
-        out_specs=[pl.BlockSpec((2, n, HEAD_DIM), lambda h: (0, 0, h)) for n in sizes],
-        out_shape=[shape((2, n, width)) for n in sizes],
+        in_specs=[hbm] * 2,
+        out_shape=[shape((2, BLOCK >> level, width)) for level in range(4)],
+        scratch_shapes=[
+            pltpu.VMEM((2, rows, width), jnp.bfloat16),
+            pltpu.SemaphoreType.DMA((2, 4)),
+        ],
     )(*(pltpu.with_memory_space_constraint(x, pltpu.HBM) for x in (keys, values)))
 
 
@@ -319,11 +330,7 @@
     heads, ring = lax.axis_size("head"), lax.axis_size("z")
     width = queries.shape[1]
 
-    def turned(value, step):
-        pairs = [
-            (y * heads + x, (x + step) % heads * heads + y) for y in range(heads) for x in range(heads)
-        ]
-        return lax.ppermute(value, ("y", "head"), pairs)
+    turn = [(y * heads + x, x * heads + y) for y in range(heads) for x in range(heads)]
 
     def across(z):
         return (z + (4 if z & 4 else 12)) % 16
@@ -334,13 +341,14 @@
     def joined(weights):
         return weights.reshape(-1, width)
 
-    w_own = out_weight.T
+    w_own = lax.ppermute(out_weight.T, ("y", "head"), turn)
     p2, p3, p4, p5 = pooled_levels(key_vectors, values)
     w_across = lax.ppermute(w_own, "z", [(z, across(z)) for z in range(ring)])
+    buffers = near_part(queries, key_vectors, values, 0, 2)
     weights = jnp.concatenate([w_own, w_across], axis=0)
     a = swap(jnp.concatenate([p5, paired(weights)], axis=1), "z", 4)
     weights = jnp.concatenate([weights, joined(a[:, 16:])], axis=0)
-    near, coarse = near_part(queries, key_vectors, values, 0, 1)
+    near, coarse = near_part(queries, key_vectors, values, 1, 2, buffers)
     b = swap(jnp.concatenate([a[:, :16], p4, paired(weights)], axis=1), "z", 2)
     weights = jnp.concatenate([weights, joined(b[:, 48:])], axis=0)
     right = shift(near, "head", 1)
@@ -349,9 +357,9 @@
     weights = jnp.concatenate([weights, joined(c[:, 128:])], axis=0)
     over = shift(near, "head", 2)
     d = swap(jnp.concatenate([a[:, :16], b[:, :48], c[:, :128], p2], axis=1), "core", 1)
-    own = []
-    for step in (0, 1, -1, 2):
-        own.append(turned(weights, step))
+    own = [weights]
+    for step in (1, -1, 2):
+        own.append(shift(weights, "y", step))
     far = far_part(coarse, (a, b, c, d), heads)
     far = lax.all_to_all(far, "head", 0, 0)
     other = swap(jnp.stack(own), "core", 1)

time: 166 us -> 128 us (0.77)
  waiting for transfers between devices: 80.3 us -> 47.4 us
  Pallas kernels: 20.2 us -> 17.4 us
    ppermute x4 -> x1, waiting for transfers between devices: 35 us -> 0.01 us  [body(): w_own = lax.ppermute(out_weight.T, ('y', 'head'), turn)]
    ppermute x4 -> x1, starting transfers between devices: 12.5 us -> 1.36 us  [body(): w_own = lax.ppermute(out_weight.T, ('y', 'head'), turn)]
    ppermute x5, starting transfers between devices: 15.6 us -> 22 us  [swap(): lax.ppermute(value, axis, [(s, s ^ mask) for s in range(lax.axis_size(axi...]
    ppermute x3 -> x6, starting transfers between devices: 15.8 us -> 19.2 us  [shift(): lax.ppermute(value, axis, [(s, (s + step) % size) for s in range(size)])]
    pallas_call x1, Pallas kernels: 6.1 us -> 2.77 us  [pooled_levels(): pl.pallas_call(pool_kernel, compiler_params=VMEM_LIMIT, in_specs=[hbm] *...]
    all_to_all x1, waiting for transfers between devices: 3.05 us -> 6.21 us  [body(): far = lax.all_to_all(far, 'head', 0, 0)]
    ppermute x3 -> x6, waiting for transfers between devices: 14.2 us -> 13.1 us  [shift(): lax.ppermute(value, axis, [(s, (s + step) % size) for s in range(size)])]
    pallas_call x1 -> x2, Pallas kernels: 6.36 us -> 6.86 us  [near_part(): pl.pallas_call(near_kernel, grid=(1,), compiler_params=VMEM_LIMIT, in_spe...]
  transfers between devices with their start and end apart: 14 -> 14, of which waited for: 7 -> 7; matrix products, arithmetic and copies ran while one was open for 1% -> 1% of each run, Pallas kernels for 9% -> 10%
where the time goes in v3:
time: 128 us; the launch traced here: 126 us
  starting transfers between devices  59.3 us (46%)
  waiting for transfers between devices  47.4 us (37%)
  Pallas kernels  17.4 us (14%)
  other arithmetic  1.31 us (1%)
    ppermute x5, waiting for transfers between devices, swap(): lax.ppermute(value, axis, [(s, s ^ mask) for s in range(lax.axis_size(axi...  28.1 us
    ppermute x5, starting transfers between devices, swap(): lax.ppermute(value, axis, [(s, s ^ mask) for s in range(lax.axis_size(axi...  22 us
    ppermute x6, starting transfers between devices, shift(): lax.ppermute(value, axis, [(s, (s + step) % size) for s in range(size)])  19.2 us
    ppermute x1, starting transfers between devices, body(): w_across = lax.ppermute(w_own, 'z', [(z, across(z)) for z in range(ring)])  13.3 us
    ppermute x6, waiting for transfers between devices, shift(): lax.ppermute(value, axis, [(s, (s + step) % size) for s in range(size)])  13.1 us
    pallas_call x2, Pallas kernels, near_part(): pl.pallas_call(near_kernel, grid=(1,), compiler_params=VMEM_LIMIT, in_spe...  6.86 us
    all_to_all x1, waiting for transfers between devices, body(): far = lax.all_to_all(far, 'head', 0, 0)  6.21 us
    pallas_call x1, Pallas kernels, mix_part(): pl.pallas_call(mix_kernel, compiler_params=VMEM_LIMIT, in_specs=[pl.Block...  5.28 us
  transfers between devices with their start and end apart: 14, of which 7 were waited for; matrix products, arithmetic and copies ran while one was open for 1% of the time, Pallas kernels for 10%

profile of v3, /device:TPU:1, one launch (start us, length us, event | category | flops | bytes accessed | tf_op | source)
XLA Modules:
  0.0 125.7 jit_solution(11218408883409780882)
XLA Ops:
  0.0 1.4 %collective-permute-start.3 = (bf16[16,512]{1,0:T(8,128)(2,1)}, bf16[16,512]{1,0:T(8,128)(2,1)S(1)}, u32[]{:S(2)}, u32[]{:S(2)}) collective-permute-start(bf16[16,512]{1,0:T(8,128)(2,1)} %bitcast.28), channel_id=1, source_target_pairs={{0,0},{1,128},{2,256},{3,384},{128,1},{129,129},{130,257},{131,385... | collective-permute-start | bytes 49160 | tf_op jit(solution)/shard_map/ppermute | solution.py:344
  1.4 0.0 collective-permute-done.3
  1.4 13.3 %collective-permute-start.4 = (bf16[16,512]{1,0:T(8,128)(2,1)S(1)}, bf16[16,512]{1,0:T(8,128)(2,1)S(1)}, u32[]{:S(2)}, u32[]{:S(2)}) collective-permute-start(bf16[16,512]{1,0:T(8,128)(2,1)S(1)} %collective-permute-done.3), channel_id=1, source_target_pairs={{0,96},{8,104},{16,112},{24,120},{32,64},{40,72},{48,80},{56,88},{... | collective-permute-start | bytes 49160 | tf_op jit(solution)/shard_map/ppermute | solution.py:346
  14.6 2.8 %shard_map.48 = (bf16[2,128,512]{2,1,0:T(8,128)(2,1)S(1)}, bf16[2,64,512]{2,1,0:T(8,128)(2,1)S(1)}, bf16[2,32,512]{2,1,0:T(8,128)(2,1)S(1)}, bf16[2,16,512]{2,1,0:T(8,128)(2,1)S(1)}) custom-call(bf16[512,512]{1,0:T(8,128)(2,1)} %key_ref.5, bf16[512,512]{1,0:T(8,128)(2,1)} %value_ref.5), custom_call_target="tpu_custom_call" | custom-call | tf_op jit(solution)/shard_map/pallas_call | solution.py:210
  17.4 0.0 collective-permute-done.4
  17.4 5.2 %collective-permute-start.5 = (bf16[2,32,512]{2,1,0:T(8,128)(2,1)S(1)}, bf16[2,32,512]{2,1,0:T(8,128)(2,1)S(1)}, u32[]{:S(2)}, u32[]{:S(2)}) collective-permute-start(bf16[2,32,512]{2,1,0:T(8,128)(2,1)S(1)} %pad_maximum_fusion.5), channel_id=1, source_target_pairs={{0,32},{8,40},{16,48},{24,56},{32,0},{40,8},{48,16},{56,24},{64,96... | collective-permute-start | bytes 196616 | tf_op jit(solution)/shard_map/ppermute | solution.py:19
  22.6 8.4 %collective-permute-done.5.a_ref = bf16[2,32,512]{2,1,0:T(8,128)(2,1)S(1)} collective-permute-done((bf16[2,32,512]{2,1,0:T(8,128)(2,1)S(1)}, bf16[2,32,512]{2,1,0:T(8,128)(2,1)S(1)}, u32[]{:S(2)}, u32[]{:S(2)}) %collective-permute-start.5) | collective-permute-done | bytes 65568 | tf_op jit(solution)/shard_map/ppermute | solution.py:19
  31.1 1.9 %collective-permute-start.6 = (bf16[2,80,512]{2,1,0:T(8,128)(2,1)S(1)}, bf16[2,80,512]{2,1,0:T(8,128)(2,1)S(1)}, u32[]{:S(2)}, u32[]{:S(2)}) collective-permute-start(bf16[2,80,512]{2,1,0:T(8,128)(2,1)S(1)} %pad_maximum_fusion.3), channel_id=1, source_target_pairs={{0,16},{8,24},{16,0},{24,8},{32,48},{40,56},{48,32},{56,40},{64,80... | collective-permute-start | bytes 491528 | tf_op jit(solution)/shard_map/ppermute | solution.py:19
  33.0 9.6 %collective-permute-done.6.b_ref = bf16[2,80,512]{2,1,0:T(8,128)(2,1)S(1)} collective-permute-done((bf16[2,80,512]{2,1,0:T(8,128)(2,1)S(1)}, bf16[2,80,512]{2,1,0:T(8,128)(2,1)S(1)}, u32[]{:S(2)}, u32[]{:S(2)}) %collective-permute-start.6) | collective-permute-done | bytes 163872 | tf_op jit(solution)/shard_map/ppermute | solution.py:19
  42.7 1.9 %collective-permute-start.7 = (bf16[2,192,512]{2,1,0:T(8,128)(2,1)S(1)}, bf16[2,192,512]{2,1,0:T(8,128)(2,1)S(1)}, u32[]{:S(2)}, u32[]{:S(2)}) collective-permute-start(bf16[2,192,512]{2,1,0:T(8,128)(2,1)S(1)} %pad_maximum_fusion.2), channel_id=1, source_target_pairs={{0,8},{8,0},{16,24},{24,16},{32,40},{40,32},{48,56},{56,48},{64,72... | collective-permute-start | bytes 1179656 | tf_op jit(solution)/shard_map/ppermute | solution.py:19
  44.6 10.1 %collective-permute-done.7.c_ref = bf16[2,192,512]{2,1,0:T(8,128)(2,1)S(1)} collective-permute-done((bf16[2,192,512]{2,1,0:T(8,128)(2,1)S(1)}, bf16[2,192,512]{2,1,0:T(8,128)(2,1)S(1)}, u32[]{:S(2)}, u32[]{:S(2)}) %collective-permute-start.7) | collective-permute-done | bytes 393248 | tf_op jit(solution)/shard_map/ppermute | solution.py:19
  54.8 1.9 %collective-permute-start.8 = (bf16[256,512]{1,0:T(8,128)(2,1)S(1)}, bf16[256,512]{1,0:T(8,128)(2,1)S(1)}, u32[]{:S(2)}, u32[]{:S(2)}) collective-permute-start(bf16[256,512]{1,0:T(8,128)(2,1)S(1)} %constant_dynamic-update-slice_fusion.refs_4_), channel_id=1, source_target_pairs={{0,128},{128,256},{256,384},{384,0},{1,129},{129,257},{257,385},{3... | collective-permute-start | bytes 786440 | tf_op jit(solution)/shard_map/ppermute | solution.py:24
  56.7 4.6 %collective-permute-start.9 = (bf16[256,512]{1,0:T(8,128)(2,1)S(1)}, bf16[256,512]{1,0:T(8,128)(2,1)S(1)}, u32[]{:S(2)}, u32[]{:S(2)}) collective-permute-start(bf16[256,512]{1,0:T(8,128)(2,1)S(1)} %constant_dynamic-update-slice_fusion.refs_4_), channel_id=1, source_target_pairs={{0,384},{128,0},{256,128},{384,256},{1,385},{129,1},{257,129},{385... | collective-permute-start | bytes 786440 | tf_op jit(solution)/shard_map/ppermute | solution.py:24
  61.3 1.9 %collective-permute-start.10 = (bf16[256,512]{1,0:T(8,128)(2,1)S(1)}, bf16[256,512]{1,0:T(8,128)(2,1)S(1)}, u32[]{:S(2)}, u32[]{:S(2)}) collective-permute-start(bf16[256,512]{1,0:T(8,128)(2,1)S(1)} %constant_dynamic-update-slice_fusion.refs_4_), channel_id=1, source_target_pairs={{0,256},{128,384},{256,0},{384,128},{1,257},{129,385},{257,1},{385... | collective-permute-start | bytes 786440 | tf_op jit(solution)/shard_map/ppermute | solution.py:24
  63.3 8.1 %collective-permute-start.11 = (bf16[2,320,512]{2,1,0:T(8,128)(2,1)S(1)}, bf16[2,320,512]{2,1,0:T(8,128)(2,1)S(1)}, u32[]{:S(2)}, u32[]{:S(2)}) collective-permute-start(bf16[2,320,512]{2,1,0:T(8,128)(2,1)S(1)} %pad_maximum_fusion.1), channel_id=1, source_target_pairs={{0,4},{4,0},{1,5},{5,1},{2,6},{6,2},{3,7},{7,3},{8,12},{12,8},{9,1... | collective-permute-start | bytes 1966088 | tf_op jit(solution)/shard_map/ppermute | solution.py:19
  71.4 0.0 collective-permute-done.8.refs_5_
  71.4 0.0 collective-permute-done.9.refs_6_
  71.4 0.0 collective-permute-done.10.refs_7_
  71.4 0.0 copy-start
  71.4 0.0 copy-start.1
  71.4 0.0 copy-start.2
  71.4 1.1 pad_maximum_fusion
  72.5 4.9 %collective-permute-start.12 = (bf16[4,256,512]{2,1,0:T(8,128)(2,1)}, bf16[4,256,512]{2,1,0:T(8,128)(2,1)S(1)}, u32[]{:S(2)}, u32[]{:S(2)}) collective-permute-start(bf16[4,256,512]{2,1,0:T(8,128)(2,1)} %pad_maximum_fusion), channel_id=1, source_target_pairs={{0,4},{4,0},{1,5},{5,1},{2,6},{6,2},{3,7},{7,3},{8,12},{12,8},{9,1... | collective-permute-start | bytes 3145736 | tf_op jit(solution)/shard_map/ppermute | solution.py:19
  77.5 0.0 copy-done
  77.5 0.0 copy-done.1
  77.5 0.0 copy-done.2
  77.5 3.4 %shard_map.46 = (bf16[528,512]{1,0:T(8,128)(2,1)S(1)}, bf16[512,512]{1,0:T(8,128)(2,1)S(1)}) custom-call(bf16[512,512]{1,0:T(8,128)(2,1)S(1)} %copy-done.2, bf16[512,512]{1,0:T(8,128)(2,1)S(1)} %copy-done, bf16[512,512]{1,0:T(8,128)(2,1)S(1)} %copy-done.1), custom_call_target="tpu_custom_call" | custom-call | tf_op jit(solution)/shard_map/pallas_call | solution.py:226
  80.9 3.4 %shard_map.47 = (bf16[528,512]{1,0:T(8,128)(2,1)S(1)}, bf16[512,512]{1,0:T(8,128)(2,1)S(1)}) custom-call(bf16[512,512]{1,0:T(8,128)(2,1)S(1)} %copy-done.2, bf16[512,512]{1,0:T(8,128)(2,1)S(1)} %copy-done, bf16[512,512]{1,0:T(8,128)(2,1)S(1)} %copy-done.1, ...), custom_call_target="tpu_custom_call", output_to_operand_aliasing={{0}: (3, {}), {1}: (4, {})} | custom-call | tf_op jit(solution)/shard_map/pallas_call | solution.py:226
  84.4 3.7 %collective-permute-start = (bf16[528,512]{1,0:T(8,128)(2,1)S(1)}, bf16[528,512]{1,0:T(8,128)(2,1)}, u32[]{:S(2)}, u32[]{:S(2)}) collective-permute-start(bf16[528,512]{1,0:T(8,128)(2,1)S(1)} %get-tuple-element.15.refs_0_), channel_id=1, source_target_pairs={{0,1},{1,2},{2,3},{3,0},{4,5},{5,6},{6,7},{7,4},{8,9},{9,10},{10,1... | collective-permute-start | bytes 1622024 | tf_op jit(solution)/shard_map/ppermute | solution.py:24
  88.1 2.8 %collective-permute-start.1 = (bf16[528,512]{1,0:T(8,128)(2,1)S(1)}, bf16[528,512]{1,0:T(8,128)(2,1)}, u32[]{:S(2)}, u32[]{:S(2)}) collective-permute-start(bf16[528,512]{1,0:T(8,128)(2,1)S(1)} %get-tuple-element.15.refs_0_), channel_id=1, source_target_pairs={{0,3},{1,0},{2,1},{3,2},{4,7},{5,4},{6,5},{7,6},{8,11},{9,8},{10,9... | collective-permute-start | bytes 1622024 | tf_op jit(solution)/shard_map/ppermute | solution.py:24
  90.9 4.2 %collective-permute-start.2 = (bf16[528,512]{1,0:T(8,128)(2,1)S(1)}, bf16[528,512]{1,0:T(8,128)(2,1)}, u32[]{:S(2)}, u32[]{:S(2)}) collective-permute-start(bf16[528,512]{1,0:T(8,128)(2,1)S(1)} %get-tuple-element.15.refs_0_), channel_id=1, source_target_pairs={{0,2},{1,3},{2,0},{3,1},{4,6},{5,7},{6,4},{7,5},{8,10},{9,11},{10,... | collective-permute-start | bytes 1622024 | tf_op jit(solution)/shard_map/ppermute | solution.py:24
  95.1 0.0 collective-permute-done.11.d_ref
  95.1 2.5 %shard_map.49 = bf16[4,144,512]{2,1,0:T(8,128)(2,1)} custom-call(bf16[512,512]{1,0:T(8,128)(2,1)S(1)} %get-tuple-element.19.coarse_ref, bf16[2,32,512]{2,1,0:T(8,128)(2,1)S(1)} %collective-permute-done.5.a_ref, bf16[2,80,512]{2,1,0:T(8,128)(2,1)S(1)} %collective-permute-done.6.b_ref, bf16[2,192,512]{2,1,0:T(8,128)(2,1)S(1)} %collective-permute-done.7.c_ref, ...), custom_call_target="tpu_custom_call" | custom-call | tf_op jit(solution)/shard_map/pallas_call | solution.py:246
  97.6 3.5 %all-to-all-start = ((bf16[4,144,512]{2,1,0:T(8,128)(2,1)}), bf16[4,144,512]{2,1,0:T(8,128)(2,1)S(1)}, u32[]{:S(2)}, u32[]{:S(2)}) async-start(bf16[4,144,512]{2,1,0:T(8,128)(2,1)} %shard_map.49), calls=%async_computation | async-start | bytes 1179648 | tf_op jit(solution)/shard_map/all_to_all | solution.py:364
  101.1 0.1 pad_add_fusion.place_ref
  101.2 0.3 collective-permute-done.refs_1_
  101.4 2.2 %collective-permute-done.1.refs_2_ = bf16[528,512]{1,0:T(8,128)(2,1)} collective-permute-done((bf16[528,512]{1,0:T(8,128)(2,1)S(1)}, bf16[528,512]{1,0:T(8,128)(2,1)}, u32[]{:S(2)}, u32[]{:S(2)}) %collective-permute-start.1) | collective-permute-done | bytes 540704 | tf_op jit(solution)/shard_map/ppermute | solution.py:24
  103.6 10.6 %collective-permute-done.2.refs_3_ = bf16[528,512]{1,0:T(8,128)(2,1)} collective-permute-done((bf16[528,512]{1,0:T(8,128)(2,1)S(1)}, bf16[528,512]{1,0:T(8,128)(2,1)}, u32[]{:S(2)}, u32[]{:S(2)}) %collective-permute-start.2) | collective-permute-done | bytes 540704 | tf_op jit(solution)/shard_map/ppermute | solution.py:24
  114.2 6.2 %all-to-all-done.refs_8_ = bf16[4,144,512]{2,1,0:T(8,128)(2,1)S(1)} async-done(((bf16[4,144,512]{2,1,0:T(8,128)(2,1)}), bf16[4,144,512]{2,1,0:T(8,128)(2,1)S(1)}, u32[]{:S(2)}, u32[]{:S(2)}) %all-to-all-start) | async-done | bytes 589856 | tf_op jit(solution)/shard_map/all_to_all | solution.py:364
  120.4 0.0 collective-permute-done.12.refs_9_
  120.4 5.3 %shard_map.50 = bf16[512,512]{1,0:T(8,128)(2,1)} custom-call(s32[4]{0:T(128)S(1)} %pad_add_fusion.place_ref, bf16[528,512]{1,0:T(8,128)(2,1)S(1)} %get-tuple-element.15.refs_0_, bf16[528,512]{1,0:T(8,128)(2,1)} %collective-permute-done.refs_1_, bf16[528,512]{1,0:T(8,128)(2,1)} %collective-permute-done.1.refs_2_, ...), custom_call_target="tpu_custom_call" | custom-call | tf_op jit(solution)/shard_map/pallas_call | solution.py:320
  (17 shorter events, 0.2 us)
Async XLA Ops:
  0.0 1.4 %collective-permute-start.3 = (bf16[16,512]{1,0:T(8,128)(2,1)}, bf16[16,512]{1,0:T(8,128)(2,1)S(1)}, u32[]{:S(2)}, u32[]{:S(2)}) collective-permute-start(bf16[16,512]{1,0:T(8,128)(2,1)} %bitcast.28), channel_id=1, source_target_pairs={{0,0},{1,128},{2,256},{3,384},{128,1},{129,129},{130,257},{131,385... | collective-permute-start | bytes 49160 | tf_op jit(solution)/shard_map/ppermute | solution.py:344
  1.4 16.0 %collective-permute-start.4 = (bf16[16,512]{1,0:T(8,128)(2,1)S(1)}, bf16[16,512]{1,0:T(8,128)(2,1)S(1)}, u32[]{:S(2)}, u32[]{:S(2)}) collective-permute-start(bf16[16,512]{1,0:T(8,128)(2,1)S(1)} %collective-permute-done.3), channel_id=1, source_target_pairs={{0,96},{8,104},{16,112},{24,120},{32,64},{40,72},{48,80},{56,88},{... | collective-permute-start | bytes 49160 | tf_op jit(solution)/shard_map/ppermute | solution.py:346
  17.4 13.6 %collective-permute-start.5 = (bf16[2,32,512]{2,1,0:T(8,128)(2,1)S(1)}, bf16[2,32,512]{2,1,0:T(8,128)(2,1)S(1)}, u32[]{:S(2)}, u32[]{:S(2)}) collective-permute-start(bf16[2,32,512]{2,1,0:T(8,128)(2,1)S(1)} %pad_maximum_fusion.5), channel_id=1, source_target_pairs={{0,32},{8,40},{16,48},{24,56},{32,0},{40,8},{48,16},{56,24},{64,96... | collective-permute-start | bytes 196616 | tf_op jit(solution)/shard_map/ppermute | solution.py:19
  31.1 11.5 %collective-permute-start.6 = (bf16[2,80,512]{2,1,0:T(8,128)(2,1)S(1)}, bf16[2,80,512]{2,1,0:T(8,128)(2,1)S(1)}, u32[]{:S(2)}, u32[]{:S(2)}) collective-permute-start(bf16[2,80,512]{2,1,0:T(8,128)(2,1)S(1)} %pad_maximum_fusion.3), channel_id=1, source_target_pairs={{0,16},{8,24},{16,0},{24,8},{32,48},{40,56},{48,32},{56,40},{64,80... | collective-permute-start | bytes 491528 | tf_op jit(solution)/shard_map/ppermute | solution.py:19
  42.7 12.1 %collective-permute-start.7 = (bf16[2,192,512]{2,1,0:T(8,128)(2,1)S(1)}, bf16[2,192,512]{2,1,0:T(8,128)(2,1)S(1)}, u32[]{:S(2)}, u32[]{:S(2)}) collective-permute-start(bf16[2,192,512]{2,1,0:T(8,128)(2,1)S(1)} %pad_maximum_fusion.2), channel_id=1, source_target_pairs={{0,8},{8,0},{16,24},{24,16},{32,40},{40,32},{48,56},{56,48},{64,72... | collective-permute-start | bytes 1179656 | tf_op jit(solution)/shard_map/ppermute | solution.py:19
  54.8 16.6 %collective-permute-start.8 = (bf16[256,512]{1,0:T(8,128)(2,1)S(1)}, bf16[256,512]{1,0:T(8,128)(2,1)S(1)}, u32[]{:S(2)}, u32[]{:S(2)}) collective-permute-start(bf16[256,512]{1,0:T(8,128)(2,1)S(1)} %constant_dynamic-update-slice_fusion.refs_4_), channel_id=1, source_target_pairs={{0,128},{128,256},{256,384},{384,0},{1,129},{129,257},{257,385},{3... | collective-permute-start | bytes 786440 | tf_op jit(solution)/shard_map/ppermute | solution.py:24
  56.7 14.7 %collective-permute-start.9 = (bf16[256,512]{1,0:T(8,128)(2,1)S(1)}, bf16[256,512]{1,0:T(8,128)(2,1)S(1)}, u32[]{:S(2)}, u32[]{:S(2)}) collective-permute-start(bf16[256,512]{1,0:T(8,128)(2,1)S(1)} %constant_dynamic-update-slice_fusion.refs_4_), channel_id=1, source_target_pairs={{0,384},{128,0},{256,128},{384,256},{1,385},{129,1},{257,129},{385... | collective-permute-start | bytes 786440 | tf_op jit(solution)/shard_map/ppermute | solution.py:24
  61.3 10.1 %collective-permute-start.10 = (bf16[256,512]{1,0:T(8,128)(2,1)S(1)}, bf16[256,512]{1,0:T(8,128)(2,1)S(1)}, u32[]{:S(2)}, u32[]{:S(2)}) collective-permute-start(bf16[256,512]{1,0:T(8,128)(2,1)S(1)} %constant_dynamic-update-slice_fusion.refs_4_), channel_id=1, source_target_pairs={{0,256},{128,384},{256,0},{384,128},{1,257},{129,385},{257,1},{385... | collective-permute-start | bytes 786440 | tf_op jit(solution)/shard_map/ppermute | solution.py:24
  63.3 31.8 %collective-permute-start.11 = (bf16[2,320,512]{2,1,0:T(8,128)(2,1)S(1)}, bf16[2,320,512]{2,1,0:T(8,128)(2,1)S(1)}, u32[]{:S(2)}, u32[]{:S(2)}) collective-permute-start(bf16[2,320,512]{2,1,0:T(8,128)(2,1)S(1)} %pad_maximum_fusion.1), channel_id=1, source_target_pairs={{0,4},{4,0},{1,5},{5,1},{2,6},{6,2},{3,7},{7,3},{8,12},{12,8},{9,1... | collective-permute-start | bytes 1966088 | tf_op jit(solution)/shard_map/ppermute | solution.py:19
  71.4 6.1 %copy-start = (bf16[512,512]{1,0:T(8,128)(2,1)S(1)}, bf16[512,512]{1,0:T(8,128)(2,1)}, u32[]{:S(2)}) copy-start(bf16[512,512]{1,0:T(8,128)(2,1)} %key_ref.5) | copy-start | bytes 1572868
  71.4 6.1 %copy-start.1 = (bf16[512,512]{1,0:T(8,128)(2,1)S(1)}, bf16[512,512]{1,0:T(8,128)(2,1)}, u32[]{:S(2)}) copy-start(bf16[512,512]{1,0:T(8,128)(2,1)} %value_ref.5) | copy-start | bytes 1572868
  71.4 6.1 %copy-start.2 = (bf16[512,512]{1,0:T(8,128)(2,1)S(1)}, bf16[512,512]{1,0:T(8,128)(2,1)}, u32[]{:S(2)}) copy-start(bf16[512,512]{1,0:T(8,128)(2,1)} %query_ref.3) | copy-start | bytes 1572868
  72.5 47.9 %collective-permute-start.12 = (bf16[4,256,512]{2,1,0:T(8,128)(2,1)}, bf16[4,256,512]{2,1,0:T(8,128)(2,1)S(1)}, u32[]{:S(2)}, u32[]{:S(2)}) collective-permute-start(bf16[4,256,512]{2,1,0:T(8,128)(2,1)} %pad_maximum_fusion), channel_id=1, source_target_pairs={{0,4},{4,0},{1,5},{5,1},{2,6},{6,2},{3,7},{7,3},{8,12},{12,8},{9,1... | collective-permute-start | bytes 3145736 | tf_op jit(solution)/shard_map/ppermute | solution.py:19
  84.4 17.1 %collective-permute-start = (bf16[528,512]{1,0:T(8,128)(2,1)S(1)}, bf16[528,512]{1,0:T(8,128)(2,1)}, u32[]{:S(2)}, u32[]{:S(2)}) collective-permute-start(bf16[528,512]{1,0:T(8,128)(2,1)S(1)} %get-tuple-element.15.refs_0_), channel_id=1, source_target_pairs={{0,1},{1,2},{2,3},{3,0},{4,5},{5,6},{6,7},{7,4},{8,9},{9,10},{10,1... | collective-permute-start | bytes 1622024 | tf_op jit(solution)/shard_map/ppermute | solution.py:24
  88.1 15.5 %collective-permute-start.1 = (bf16[528,512]{1,0:T(8,128)(2,1)S(1)}, bf16[528,512]{1,0:T(8,128)(2,1)}, u32[]{:S(2)}, u32[]{:S(2)}) collective-permute-start(bf16[528,512]{1,0:T(8,128)(2,1)S(1)} %get-tuple-element.15.refs_0_), channel_id=1, source_target_pairs={{0,3},{1,0},{2,1},{3,2},{4,7},{5,4},{6,5},{7,6},{8,11},{9,8},{10,9... | collective-permute-start | bytes 1622024 | tf_op jit(solution)/shard_map/ppermute | solution.py:24
  90.9 23.3 %collective-permute-start.2 = (bf16[528,512]{1,0:T(8,128)(2,1)S(1)}, bf16[528,512]{1,0:T(8,128)(2,1)}, u32[]{:S(2)}, u32[]{:S(2)}) collective-permute-start(bf16[528,512]{1,0:T(8,128)(2,1)S(1)} %get-tuple-element.15.refs_0_), channel_id=1, source_target_pairs={{0,2},{1,3},{2,0},{3,1},{4,6},{5,7},{6,4},{7,5},{8,10},{9,11},{10,... | collective-permute-start | bytes 1622024 | tf_op jit(solution)/shard_map/ppermute | solution.py:24
  97.6 22.8 %all-to-all-start = ((bf16[4,144,512]{2,1,0:T(8,128)(2,1)}), bf16[4,144,512]{2,1,0:T(8,128)(2,1)S(1)}, u32[]{:S(2)}, u32[]{:S(2)}) async-start(bf16[4,144,512]{2,1,0:T(8,128)(2,1)} %shard_map.49), calls=%async_computation | async-start | bytes 1179648 | tf_op jit(solution)/shard_map/all_to_all | solution.py:364

commit v4 on v3

--- a/solution.py
+++ b/solution.py
@@ -135,8 +135,7 @@
     )
 
 
-def near_kernel(query_ref, key_ref, value_ref, *refs):
-    out_ref, coarse_ref = refs[-2:]
+def near_kernel(query_ref, key_ref, value_ref, out_ref, coarse_ref):
     rows = query_ref.shape[0]
     for start in range(0, query_ref.shape[1], HEAD_DIM):
         lanes = slice(start, start + HEAD_DIM)
@@ -219,22 +218,13 @@
     )(*(pltpu.with_memory_space_constraint(x, pltpu.HBM) for x in (keys, values)))
 
 
-def near_part(queries, keys, values, part, parts, buffers=()):
+def near_part(queries, keys, values):
     rows, width = queries.shape
-    coarse, lanes = 4 * BLOCK, width // parts
-    columns = pl.BlockSpec((rows, lanes), lambda i: (0, part))
     return pl.pallas_call(
         near_kernel,
-        grid=(1,),
         compiler_params=VMEM_LIMIT,
-        in_specs=[columns] * 3 + [pl.BlockSpec(memory_space=pl.ANY)] * len(buffers),
-        out_specs=[
-            pl.BlockSpec((rows + 16, lanes), lambda i: (0, part)),
-            pl.BlockSpec((coarse, lanes), lambda i: (0, part)),
-        ],
-        out_shape=[shape((rows + 16, width)), shape((coarse, width))],
-        input_output_aliases={3 + i: i for i in range(len(buffers))},
-    )(queries, keys, values, *buffers)
+        out_shape=[shape((rows + 16, width)), shape((4 * BLOCK, width))],
+    )(queries, keys, values)
 
 
 def in_vmem(value):
@@ -263,11 +253,14 @@
 def placed(total, z, core):
     width = total.shape[1]
     source = lax.broadcasted_iota(jnp.int32, (width, 1), 0)
+    core = jnp.where(source < width // 2, core, 1 - core)
+    source = source & (width // 2 - 1)
     slot = source >> 4
-    origin = z ^ ((slot >> 3) & 1) ^ (((slot >> 2) & 1) << 1) ^ (((slot >> 1) & 1) << 2)
-    origin = jnp.where((slot & 1) == 1, opposite(origin), origin)
+    origin = z ^ ((slot >> 2) & 1)
+    origin = jnp.where((slot & 8) == 8, opposite(origin), origin)
+    origin = origin ^ ((slot & 1) << 2) ^ (slot & 2)
     target = origin * 32 + core * 16 + (source & 15)
-    column = lax.broadcasted_iota(jnp.int32, (width, 2 * width), 1)
+    column = lax.broadcasted_iota(jnp.int32, (width, width), 1)
     choice = jnp.where(column == target, 1.0, 0.0).astype(jnp.bfloat16)
     return jnp.dot(total.astype(jnp.bfloat16), choice, preferred_element_type=jnp.float32)
 
@@ -293,6 +286,9 @@
     blank = jnp.zeros((BLOCK - groups * heads * tiles, BLOCK), jnp.float32)
     shares = jnp.concatenate(shares + [blank], axis=0).T
     for i, g in enumerate(sources):
+        ahead = (g - y) & (groups - 1)
+        index = jnp.where(ahead == 0, 0, jnp.where(ahead == 3, 1, ahead + 1))
+        at = pl.multiple_of(index * width, width)
         for tile in range(tiles):
             far = jnp.dot(
                 spread_rows,
@@ -305,13 +301,12 @@
                 [jnp.broadcast_to(shares[:, k : k + 1], (BLOCK, HEAD_DIM)) for k in columns], axis=1
             )
             attended = (far + share * (near - far)).astype(jnp.bfloat16)
-            attended_ref[g, tile * BLOCK : (tile + 1) * BLOCK] = attended
-    own, other = 0.0, 0.0
-    for i, step in enumerate(steps):
-        attended = attended_ref[(y + step) & (groups - 1)]
-        own = own + times(attended, own_refs[i][...])
-        other = other + times(attended, other_ref[i])
-    out_ref[...] = (placed(own, z, core) + placed(other, z, 1 - core)).astype(jnp.bfloat16)
+            attended_ref[tile * BLOCK : (tile + 1) * BLOCK, pl.ds(at, width)] = attended
+    weights = [
+        jnp.concatenate([own_refs[i][...], other_ref[i]], axis=0) for i in range(groups)
+    ]
+    total = times(attended_ref[...], jnp.concatenate(weights, axis=1))
+    out_ref[...] = placed(total, z, core).astype(jnp.bfloat16)
 
 
 def mix_part(place, near, own, far, other):
@@ -322,7 +317,7 @@
         compiler_params=VMEM_LIMIT,
         in_specs=[pl.BlockSpec(memory_space=pltpu.SMEM)] + [vmem] * (2 * len(near) + 2),
         out_shape=shape((rows, 2 * own[0].shape[0])),
-        scratch_shapes=[pltpu.VMEM((len(near), rows, width), jnp.bfloat16)],
+        scratch_shapes=[pltpu.VMEM((rows, len(near) * width), jnp.bfloat16)],
     )(place, *map(in_vmem, (*near, *own, far, other)))
 
 
@@ -341,22 +336,21 @@
     def joined(weights):
         return weights.reshape(-1, width)
 
-    w_own = lax.ppermute(out_weight.T, ("y", "head"), turn)
+    weights = lax.ppermute(out_weight.T, ("y", "head"), turn)
     p2, p3, p4, p5 = pooled_levels(key_vectors, values)
-    w_across = lax.ppermute(w_own, "z", [(z, across(z)) for z in range(ring)])
-    buffers = near_part(queries, key_vectors, values, 0, 2)
-    weights = jnp.concatenate([w_own, w_across], axis=0)
     a = swap(jnp.concatenate([p5, paired(weights)], axis=1), "z", 4)
     weights = jnp.concatenate([weights, joined(a[:, 16:])], axis=0)
-    near, coarse = near_part(queries, key_vectors, values, 1, 2, buffers)
+    near, coarse = near_part(queries, key_vectors, values)
     b = swap(jnp.concatenate([a[:, :16], p4, paired(weights)], axis=1), "z", 2)
     weights = jnp.concatenate([weights, joined(b[:, 48:])], axis=0)
     right = shift(near, "head", 1)
     left = shift(near, "head", -1)
     c = swap(jnp.concatenate([a[:, :16], b[:, :48], p3, paired(weights)], axis=1), "z", 1)
-    weights = jnp.concatenate([weights, joined(c[:, 128:])], axis=0)
+    w_across = lax.ppermute(weights, "z", [(z, across(z)) for z in range(ring)])
     over = shift(near, "head", 2)
+    w_beside = swap(w_across, "z", 1)
     d = swap(jnp.concatenate([a[:, :16], b[:, :48], c[:, :128], p2], axis=1), "core", 1)
+    weights = jnp.concatenate([weights, joined(c[:, 128:]), w_across, w_beside], axis=0)
     own = [weights]
     for step in (1, -1, 2):
         own.append(shift(weights, "y", step))

time: 128 us -> 124 us (0.969)
  the two profiles are of different devices: /device:TPU:1 before, /device:TPU:70 now
where the time goes in v4:
time: 124 us
  starting transfers between devices  60.1 us (48%)
  waiting for transfers between devices  44.8 us (36%)
  Pallas kernels  16.9 us (14%)
  other arithmetic  1.3 us (1%)
    ppermute x6, starting transfers between devices, swap(): lax.ppermute(value, axis, [(s, s ^ mask) for s in range(lax.axis_size(axi...  21.4 us
    ppermute x6, starting transfers between devices, shift(): lax.ppermute(value, axis, [(s, (s + step) % size) for s in range(size)])  19.7 us
    ppermute x6, waiting for transfers between devices, shift(): lax.ppermute(value, axis, [(s, (s + step) % size) for s in range(size)])  19.1 us
    ppermute x6, waiting for transfers between devices, swap(): lax.ppermute(value, axis, [(s, s ^ mask) for s in range(lax.axis_size(axi...  12.2 us
    ppermute x1, starting transfers between devices, body(): w_across = lax.ppermute(weights, 'z', [(z, across(z)) for z in range(ring)])  9.68 us
    pallas_call x1, Pallas kernels, near_part(): pl.pallas_call(near_kernel, compiler_params=VMEM_LIMIT, out_shape=[shape(...  6.36 us
    all_to_all x1, waiting for transfers between devices, body(): far = lax.all_to_all(far, 'head', 0, 0)  6.2 us
    ppermute x1, waiting for transfers between devices, body(): w_across = lax.ppermute(weights, 'z', [(z, across(z)) for z in range(ring)])  5.78 us
  transfers between devices with their start and end apart: 15, of which 9 were waited for; matrix products, arithmetic and copies ran while one was open for 1% of the time, Pallas kernels for 9%

profile of v4, /device:TPU:70, one launch (start us, length us, event | category | flops | bytes accessed | tf_op | source)
XLA Modules:
  0.0 123.5 jit_solution(18124822283563099854)
XLA Ops:
  0.0 4.8 %collective-permute-start.3 = (bf16[16,512]{1,0:T(8,128)(2,1)}, bf16[16,512]{1,0:T(8,128)(2,1)S(1)}, u32[]{:S(2)}, u32[]{:S(2)}) collective-permute-start(bf16[16,512]{1,0:T(8,128)(2,1)} %bitcast.28), channel_id=1, source_target_pairs={{0,0},{1,128},{2,256},{3,384},{128,1},{129,129},{130,257},{131,385... | collective-permute-start | bytes 49160 | tf_op jit(solution)/shard_map/ppermute | solution.py:339
  4.8 2.8 %shard_map.47 = (bf16[2,128,512]{2,1,0:T(8,128)(2,1)S(1)}, bf16[2,64,512]{2,1,0:T(8,128)(2,1)S(1)}, bf16[2,32,512]{2,1,0:T(8,128)(2,1)S(1)}, bf16[2,16,512]{2,1,0:T(8,128)(2,1)S(1)}) custom-call(bf16[512,512]{1,0:T(8,128)(2,1)} %key_ref.3, bf16[512,512]{1,0:T(8,128)(2,1)} %value_ref.3), custom_call_target="tpu_custom_call" | custom-call | tf_op jit(solution)/shard_map/pallas_call | solution.py:209
  7.6 1.5 %collective-permute-done.3 = bf16[16,512]{1,0:T(8,128)(2,1)S(1)} collective-permute-done((bf16[16,512]{1,0:T(8,128)(2,1)}, bf16[16,512]{1,0:T(8,128)(2,1)S(1)}, u32[]{:S(2)}, u32[]{:S(2)}) %collective-permute-start.3) | collective-permute-done | bytes 16416 | tf_op jit(solution)/shard_map/ppermute | solution.py:339
  9.2 9.1 %collective-permute-start.4 = (bf16[2,24,512]{2,1,0:T(8,128)(2,1)S(1)}, bf16[2,24,512]{2,1,0:T(8,128)(2,1)S(1)}, u32[]{:S(2)}, u32[]{:S(2)}) collective-permute-start(bf16[2,24,512]{2,1,0:T(8,128)(2,1)S(1)} %pad_maximum_fusion.5), channel_id=1, source_target_pairs={{0,32},{8,40},{16,48},{24,56},{32,0},{40,8},{48,16},{56,24},{64,96... | collective-permute-start | bytes 147464 | tf_op jit(solution)/shard_map/ppermute | solution.py:19
  18.2 2.1 %collective-permute-done.4.a_ref = bf16[2,24,512]{2,1,0:T(8,128)(2,1)S(1)} collective-permute-done((bf16[2,24,512]{2,1,0:T(8,128)(2,1)S(1)}, bf16[2,24,512]{2,1,0:T(8,128)(2,1)S(1)}, u32[]{:S(2)}, u32[]{:S(2)}) %collective-permute-start.4) | collective-permute-done | bytes 49184 | tf_op jit(solution)/shard_map/ppermute | solution.py:19
  20.3 1.9 %collective-permute-start.5 = (bf16[2,64,512]{2,1,0:T(8,128)(2,1)S(1)}, bf16[2,64,512]{2,1,0:T(8,128)(2,1)S(1)}, u32[]{:S(2)}, u32[]{:S(2)}) collective-permute-start(bf16[2,64,512]{2,1,0:T(8,128)(2,1)S(1)} %pad_maximum_fusion.3), channel_id=1, source_target_pairs={{0,16},{8,24},{16,0},{24,8},{32,48},{40,56},{48,32},{56,40},{64,80... | collective-permute-start | bytes 393224 | tf_op jit(solution)/shard_map/ppermute | solution.py:19
  22.3 5.9 %collective-permute-done.5.b_ref = bf16[2,64,512]{2,1,0:T(8,128)(2,1)S(1)} collective-permute-done((bf16[2,64,512]{2,1,0:T(8,128)(2,1)S(1)}, bf16[2,64,512]{2,1,0:T(8,128)(2,1)S(1)}, u32[]{:S(2)}, u32[]{:S(2)}) %collective-permute-start.5) | collective-permute-done | bytes 131104 | tf_op jit(solution)/shard_map/ppermute | solution.py:19
  28.3 4.7 %collective-permute-start.6 = (bf16[2,160,512]{2,1,0:T(8,128)(2,1)S(1)}, bf16[2,160,512]{2,1,0:T(8,128)(2,1)S(1)}, u32[]{:S(2)}, u32[]{:S(2)}) collective-permute-start(bf16[2,160,512]{2,1,0:T(8,128)(2,1)S(1)} %pad_maximum_fusion.2), channel_id=1, source_target_pairs={{0,8},{8,0},{16,24},{24,16},{32,40},{40,32},{48,56},{56,48},{64,72... | collective-permute-start | bytes 983048 | tf_op jit(solution)/shard_map/ppermute | solution.py:19
  33.0 9.7 %collective-permute-start.7 = (bf16[64,512]{1,0:T(8,128)(2,1)S(1)}, bf16[64,512]{1,0:T(8,128)(2,1)S(1)}, u32[]{:S(2)}, u32[]{:S(2)}) collective-permute-start(bf16[64,512]{1,0:T(8,128)(2,1)S(1)} %pad_maximum_fusion.4), channel_id=1, source_target_pairs={{0,96},{8,104},{16,112},{24,120},{32,64},{40,72},{48,80},{56,88},{... | collective-permute-start | bytes 196616 | tf_op jit(solution)/shard_map/ppermute | solution.py:349
  42.7 5.8 %collective-permute-done.7 = bf16[64,512]{1,0:T(8,128)(2,1)S(1)} collective-permute-done((bf16[64,512]{1,0:T(8,128)(2,1)S(1)}, bf16[64,512]{1,0:T(8,128)(2,1)S(1)}, u32[]{:S(2)}, u32[]{:S(2)}) %collective-permute-start.7) | collective-permute-done | bytes 65568 | tf_op jit(solution)/shard_map/ppermute | solution.py:349
  48.4 1.9 %collective-permute-start.8 = (bf16[64,512]{1,0:T(8,128)(2,1)S(1)}, bf16[64,512]{1,0:T(8,128)(2,1)S(1)}, u32[]{:S(2)}, u32[]{:S(2)}) collective-permute-start(bf16[64,512]{1,0:T(8,128)(2,1)S(1)} %collective-permute-done.7), channel_id=1, source_target_pairs={{0,8},{8,0},{16,24},{24,16},{32,40},{40,32},{48,56},{56,48},{64,72... | collective-permute-start | bytes 196616 | tf_op jit(solution)/shard_map/ppermute | solution.py:19
  50.4 0.0 collective-permute-done.6.c_ref
  50.4 4.2 %collective-permute-done.8 = bf16[64,512]{1,0:T(8,128)(2,1)S(1)} collective-permute-done((bf16[64,512]{1,0:T(8,128)(2,1)S(1)}, bf16[64,512]{1,0:T(8,128)(2,1)S(1)}, u32[]{:S(2)}, u32[]{:S(2)}) %collective-permute-start.8) | collective-permute-done | bytes 65568 | tf_op jit(solution)/shard_map/ppermute | solution.py:19
  54.6 3.1 %collective-permute-start.11 = (bf16[256,512]{1,0:T(8,128)(2,1)S(1)}, bf16[256,512]{1,0:T(8,128)(2,1)S(1)}, u32[]{:S(2)}, u32[]{:S(2)}) collective-permute-start(bf16[256,512]{1,0:T(8,128)(2,1)S(1)} %constant_dynamic-update-slice_fusion.refs_4_), channel_id=1, source_target_pairs={{0,256},{128,384},{256,0},{384,128},{1,257},{129,385},{257,1},{385... | collective-permute-start | bytes 786440 | tf_op jit(solution)/shard_map/ppermute | solution.py:24
  57.7 5.6 %collective-permute-start.10 = (bf16[256,512]{1,0:T(8,128)(2,1)S(1)}, bf16[256,512]{1,0:T(8,128)(2,1)S(1)}, u32[]{:S(2)}, u32[]{:S(2)}) collective-permute-start(bf16[256,512]{1,0:T(8,128)(2,1)S(1)} %constant_dynamic-update-slice_fusion.refs_4_), channel_id=1, source_target_pairs={{0,384},{128,0},{256,128},{384,256},{1,385},{129,1},{257,129},{385... | collective-permute-start | bytes 786440 | tf_op jit(solution)/shard_map/ppermute | solution.py:24
  63.3 1.9 %collective-permute-start.9 = (bf16[256,512]{1,0:T(8,128)(2,1)S(1)}, bf16[256,512]{1,0:T(8,128)(2,1)S(1)}, u32[]{:S(2)}, u32[]{:S(2)}) collective-permute-start(bf16[256,512]{1,0:T(8,128)(2,1)S(1)} %constant_dynamic-update-slice_fusion.refs_4_), channel_id=1, source_target_pairs={{0,128},{128,256},{256,384},{384,0},{1,129},{129,257},{257,385},{3... | collective-permute-start | bytes 786440 | tf_op jit(solution)/shard_map/ppermute | solution.py:24
  65.3 1.9 %collective-permute-start.12 = (bf16[2,320,512]{2,1,0:T(8,128)(2,1)S(1)}, bf16[2,320,512]{2,1,0:T(8,128)(2,1)S(1)}, u32[]{:S(2)}, u32[]{:S(2)}) collective-permute-start(bf16[2,320,512]{2,1,0:T(8,128)(2,1)S(1)} %pad_maximum_fusion.1), channel_id=1, source_target_pairs={{0,4},{4,0},{1,5},{5,1},{2,6},{6,2},{3,7},{7,3},{8,12},{12,8},{9,1... | collective-permute-start | bytes 1966088 | tf_op jit(solution)/shard_map/ppermute | solution.py:19
  67.2 0.0 collective-permute-done.11.refs_7_
  67.2 0.0 collective-permute-done.10.refs_6_
  67.2 5.5 %collective-permute-done.9.refs_5_ = bf16[256,512]{1,0:T(8,128)(2,1)S(1)} collective-permute-done((bf16[256,512]{1,0:T(8,128)(2,1)S(1)}, bf16[256,512]{1,0:T(8,128)(2,1)S(1)}, u32[]{:S(2)}, u32[]{:S(2)}) %collective-permute-start.9) | collective-permute-done | bytes 262176 | tf_op jit(solution)/shard_map/ppermute | solution.py:24
  72.7 0.0 copy-start
  72.7 0.0 copy-start.1
  72.7 0.0 copy-start.2
  72.7 1.1 pad_maximum_fusion
  73.9 1.9 %collective-permute-start.13 = (bf16[4,256,512]{2,1,0:T(8,128)(2,1)}, bf16[4,256,512]{2,1,0:T(8,128)(2,1)S(1)}, u32[]{:S(2)}, u32[]{:S(2)}) collective-permute-start(bf16[4,256,512]{2,1,0:T(8,128)(2,1)} %pad_maximum_fusion), channel_id=1, source_target_pairs={{0,4},{4,0},{1,5},{5,1},{2,6},{6,2},{3,7},{7,3},{8,12},{12,8},{9,1... | collective-permute-start | bytes 3145736 | tf_op jit(solution)/shard_map/ppermute | solution.py:19
  75.8 0.0 copy-done
  75.8 0.0 copy-done.1
  75.8 0.0 copy-done.2
  75.8 6.4 %shard_map.46 = (bf16[528,512]{1,0:T(8,128)(2,1)S(1)}, bf16[512,512]{1,0:T(8,128)(2,1)S(1)}) custom-call(bf16[512,512]{1,0:T(8,128)(2,1)S(1)} %copy-done.2, bf16[512,512]{1,0:T(8,128)(2,1)S(1)} %copy-done, bf16[512,512]{1,0:T(8,128)(2,1)S(1)} %copy-done.1), custom_call_target="tpu_custom_call" | custom-call | tf_op jit(solution)/shard_map/pallas_call | solution.py:223
  82.2 2.1 %collective-permute-start.2 = (bf16[528,512]{1,0:T(8,128)(2,1)S(1)}, bf16[528,512]{1,0:T(8,128)(2,1)}, u32[]{:S(2)}, u32[]{:S(2)}) collective-permute-start(bf16[528,512]{1,0:T(8,128)(2,1)S(1)} %get-tuple-element.11.refs_0_), channel_id=1, source_target_pairs={{0,2},{1,3},{2,0},{3,1},{4,6},{5,7},{6,4},{7,5},{8,10},{9,11},{10,... | collective-permute-start | bytes 1622024 | tf_op jit(solution)/shard_map/ppermute | solution.py:24
  84.3 2.0 %collective-permute-start.1 = (bf16[528,512]{1,0:T(8,128)(2,1)S(1)}, bf16[528,512]{1,0:T(8,128)(2,1)}, u32[]{:S(2)}, u32[]{:S(2)}) collective-permute-start(bf16[528,512]{1,0:T(8,128)(2,1)S(1)} %get-tuple-element.11.refs_0_), channel_id=1, source_target_pairs={{0,3},{1,0},{2,1},{3,2},{4,7},{5,4},{6,5},{7,6},{8,11},{9,8},{10,9... | collective-permute-start | bytes 1622024 | tf_op jit(solution)/shard_map/ppermute | solution.py:24
  86.3 5.0 %collective-permute-start = (bf16[528,512]{1,0:T(8,128)(2,1)S(1)}, bf16[528,512]{1,0:T(8,128)(2,1)}, u32[]{:S(2)}, u32[]{:S(2)}) collective-permute-start(bf16[528,512]{1,0:T(8,128)(2,1)S(1)} %get-tuple-element.11.refs_0_), channel_id=1, source_target_pairs={{0,1},{1,2},{2,3},{3,0},{4,5},{5,6},{6,7},{7,4},{8,9},{9,10},{10,1... | collective-permute-start | bytes 1622024 | tf_op jit(solution)/shard_map/ppermute | solution.py:24
  91.3 0.0 collective-permute-done.12.d_ref
  91.3 2.4 %shard_map.48 = bf16[4,144,512]{2,1,0:T(8,128)(2,1)} custom-call(bf16[512,512]{1,0:T(8,128)(2,1)S(1)} %get-tuple-element.15.coarse_ref, bf16[2,24,512]{2,1,0:T(8,128)(2,1)S(1)} %collective-permute-done.4.a_ref, bf16[2,64,512]{2,1,0:T(8,128)(2,1)S(1)} %collective-permute-done.5.b_ref, bf16[2,160,512]{2,1,0:T(8,128)(2,1)S(1)} %collective-permute-done.6.c_ref, ...), custom_call_target="tpu_custom_call" | custom-call | tf_op jit(solution)/shard_map/pallas_call | solution.py:236
  93.8 4.5 %all-to-all-start = ((bf16[4,144,512]{2,1,0:T(8,128)(2,1)}), bf16[4,144,512]{2,1,0:T(8,128)(2,1)S(1)}, u32[]{:S(2)}, u32[]{:S(2)}) async-start(bf16[4,144,512]{2,1,0:T(8,128)(2,1)} %shard_map.48), calls=%async_computation | async-start | bytes 1179648 | tf_op jit(solution)/shard_map/all_to_all | solution.py:358
  98.3 0.1 pad_add_fusion.place_ref
  98.4 2.5 %collective-permute-done.2.refs_3_ = bf16[528,512]{1,0:T(8,128)(2,1)} collective-permute-done((bf16[528,512]{1,0:T(8,128)(2,1)S(1)}, bf16[528,512]{1,0:T(8,128)(2,1)}, u32[]{:S(2)}, u32[]{:S(2)}) %collective-permute-start.2) | collective-permute-done | bytes 540704 | tf_op jit(solution)/shard_map/ppermute | solution.py:24
  100.9 11.1 %collective-permute-done.1.refs_2_ = bf16[528,512]{1,0:T(8,128)(2,1)} collective-permute-done((bf16[528,512]{1,0:T(8,128)(2,1)S(1)}, bf16[528,512]{1,0:T(8,128)(2,1)}, u32[]{:S(2)}, u32[]{:S(2)}) %collective-permute-start.1) | collective-permute-done | bytes 540704 | tf_op jit(solution)/shard_map/ppermute | solution.py:24
  112.0 0.0 collective-permute-done.refs_1_
  112.0 6.2 %all-to-all-done.refs_8_ = bf16[4,144,512]{2,1,0:T(8,128)(2,1)S(1)} async-done(((bf16[4,144,512]{2,1,0:T(8,128)(2,1)}), bf16[4,144,512]{2,1,0:T(8,128)(2,1)S(1)}, u32[]{:S(2)}, u32[]{:S(2)}) %all-to-all-start) | async-done | bytes 589856 | tf_op jit(solution)/shard_map/all_to_all | solution.py:358
  118.2 0.0 collective-permute-done.13.refs_9_
  118.2 5.3 %shard_map.49 = bf16[512,512]{1,0:T(8,128)(2,1)} custom-call(s32[4]{0:T(128)S(1)} %pad_add_fusion.place_ref, bf16[528,512]{1,0:T(8,128)(2,1)S(1)} %get-tuple-element.11.refs_0_, bf16[528,512]{1,0:T(8,128)(2,1)} %collective-permute-done.refs_1_, bf16[528,512]{1,0:T(8,128)(2,1)} %collective-permute-done.1.refs_2_, ...), custom_call_target="tpu_custom_call" | custom-call | tf_op jit(solution)/shard_map/pallas_call | solution.py:315
  (18 shorter events, 0.2 us)
Async XLA Ops:
  0.0 9.2 %collective-permute-start.3 = (bf16[16,512]{1,0:T(8,128)(2,1)}, bf16[16,512]{1,0:T(8,128)(2,1)S(1)}, u32[]{:S(2)}, u32[]{:S(2)}) collective-permute-start(bf16[16,512]{1,0:T(8,128)(2,1)} %bitcast.28), channel_id=1, source_target_pairs={{0,0},{1,128},{2,256},{3,384},{128,1},{129,129},{130,257},{131,385... | collective-permute-start | bytes 49160 | tf_op jit(solution)/shard_map/ppermute | solution.py:339
  9.2 11.1 %collective-permute-start.4 = (bf16[2,24,512]{2,1,0:T(8,128)(2,1)S(1)}, bf16[2,24,512]{2,1,0:T(8,128)(2,1)S(1)}, u32[]{:S(2)}, u32[]{:S(2)}) collective-permute-start(bf16[2,24,512]{2,1,0:T(8,128)(2,1)S(1)} %pad_maximum_fusion.5), channel_id=1, source_target_pairs={{0,32},{8,40},{16,48},{24,56},{32,0},{40,8},{48,16},{56,24},{64,96... | collective-permute-start | bytes 147464 | tf_op jit(solution)/shard_map/ppermute | solution.py:19
  20.3 7.9 %collective-permute-start.5 = (bf16[2,64,512]{2,1,0:T(8,128)(2,1)S(1)}, bf16[2,64,512]{2,1,0:T(8,128)(2,1)S(1)}, u32[]{:S(2)}, u32[]{:S(2)}) collective-permute-start(bf16[2,64,512]{2,1,0:T(8,128)(2,1)S(1)} %pad_maximum_fusion.3), channel_id=1, source_target_pairs={{0,16},{8,24},{16,0},{24,8},{32,48},{40,56},{48,32},{56,40},{64,80... | collective-permute-start | bytes 393224 | tf_op jit(solution)/shard_map/ppermute | solution.py:19
  28.3 22.1 %collective-permute-start.6 = (bf16[2,160,512]{2,1,0:T(8,128)(2,1)S(1)}, bf16[2,160,512]{2,1,0:T(8,128)(2,1)S(1)}, u32[]{:S(2)}, u32[]{:S(2)}) collective-permute-start(bf16[2,160,512]{2,1,0:T(8,128)(2,1)S(1)} %pad_maximum_fusion.2), channel_id=1, source_target_pairs={{0,8},{8,0},{16,24},{24,16},{32,40},{40,32},{48,56},{56,48},{64,72... | collective-permute-start | bytes 983048 | tf_op jit(solution)/shard_map/ppermute | solution.py:19
  33.0 15.5 %collective-permute-start.7 = (bf16[64,512]{1,0:T(8,128)(2,1)S(1)}, bf16[64,512]{1,0:T(8,128)(2,1)S(1)}, u32[]{:S(2)}, u32[]{:S(2)}) collective-permute-start(bf16[64,512]{1,0:T(8,128)(2,1)S(1)} %pad_maximum_fusion.4), channel_id=1, source_target_pairs={{0,96},{8,104},{16,112},{24,120},{32,64},{40,72},{48,80},{56,88},{... | collective-permute-start | bytes 196616 | tf_op jit(solution)/shard_map/ppermute | solution.py:349
  48.4 6.1 %collective-permute-start.8 = (bf16[64,512]{1,0:T(8,128)(2,1)S(1)}, bf16[64,512]{1,0:T(8,128)(2,1)S(1)}, u32[]{:S(2)}, u32[]{:S(2)}) collective-permute-start(bf16[64,512]{1,0:T(8,128)(2,1)S(1)} %collective-permute-done.7), channel_id=1, source_target_pairs={{0,8},{8,0},{16,24},{24,16},{32,40},{40,32},{48,56},{56,48},{64,72... | collective-permute-start | bytes 196616 | tf_op jit(solution)/shard_map/ppermute | solution.py:19
  54.6 12.6 %collective-permute-start.11 = (bf16[256,512]{1,0:T(8,128)(2,1)S(1)}, bf16[256,512]{1,0:T(8,128)(2,1)S(1)}, u32[]{:S(2)}, u32[]{:S(2)}) collective-permute-start(bf16[256,512]{1,0:T(8,128)(2,1)S(1)} %constant_dynamic-update-slice_fusion.refs_4_), channel_id=1, source_target_pairs={{0,256},{128,384},{256,0},{384,128},{1,257},{129,385},{257,1},{385... | collective-permute-start | bytes 786440 | tf_op jit(solution)/shard_map/ppermute | solution.py:24
  57.7 9.5 %collective-permute-start.10 = (bf16[256,512]{1,0:T(8,128)(2,1)S(1)}, bf16[256,512]{1,0:T(8,128)(2,1)S(1)}, u32[]{:S(2)}, u32[]{:S(2)}) collective-permute-start(bf16[256,512]{1,0:T(8,128)(2,1)S(1)} %constant_dynamic-update-slice_fusion.refs_4_), channel_id=1, source_target_pairs={{0,384},{128,0},{256,128},{384,256},{1,385},{129,1},{257,129},{385... | collective-permute-start | bytes 786440 | tf_op jit(solution)/shard_map/ppermute | solution.py:24
  63.3 9.5 %collective-permute-start.9 = (bf16[256,512]{1,0:T(8,128)(2,1)S(1)}, bf16[256,512]{1,0:T(8,128)(2,1)S(1)}, u32[]{:S(2)}, u32[]{:S(2)}) collective-permute-start(bf16[256,512]{1,0:T(8,128)(2,1)S(1)} %constant_dynamic-update-slice_fusion.refs_4_), channel_id=1, source_target_pairs={{0,128},{128,256},{256,384},{384,0},{1,129},{129,257},{257,385},{3... | collective-permute-start | bytes 786440 | tf_op jit(solution)/shard_map/ppermute | solution.py:24
  65.3 26.1 %collective-permute-start.12 = (bf16[2,320,512]{2,1,0:T(8,128)(2,1)S(1)}, bf16[2,320,512]{2,1,0:T(8,128)(2,1)S(1)}, u32[]{:S(2)}, u32[]{:S(2)}) collective-permute-start(bf16[2,320,512]{2,1,0:T(8,128)(2,1)S(1)} %pad_maximum_fusion.1), channel_id=1, source_target_pairs={{0,4},{4,0},{1,5},{5,1},{2,6},{6,2},{3,7},{7,3},{8,12},{12,8},{9,1... | collective-permute-start | bytes 1966088 | tf_op jit(solution)/shard_map/ppermute | solution.py:19
  72.7 3.0 %copy-start = (bf16[512,512]{1,0:T(8,128)(2,1)S(1)}, bf16[512,512]{1,0:T(8,128)(2,1)}, u32[]{:S(2)}) copy-start(bf16[512,512]{1,0:T(8,128)(2,1)} %key_ref.3) | copy-start | bytes 1572868
  72.7 3.1 %copy-start.1 = (bf16[512,512]{1,0:T(8,128)(2,1)S(1)}, bf16[512,512]{1,0:T(8,128)(2,1)}, u32[]{:S(2)}) copy-start(bf16[512,512]{1,0:T(8,128)(2,1)} %value_ref.3) | copy-start | bytes 1572868
  72.7 3.1 %copy-start.2 = (bf16[512,512]{1,0:T(8,128)(2,1)S(1)}, bf16[512,512]{1,0:T(8,128)(2,1)}, u32[]{:S(2)}) copy-start(bf16[512,512]{1,0:T(8,128)(2,1)} %query_ref.1) | copy-start | bytes 1572868
  73.9 44.3 %collective-permute-start.13 = (bf16[4,256,512]{2,1,0:T(8,128)(2,1)}, bf16[4,256,512]{2,1,0:T(8,128)(2,1)S(1)}, u32[]{:S(2)}, u32[]{:S(2)}) collective-permute-start(bf16[4,256,512]{2,1,0:T(8,128)(2,1)} %pad_maximum_fusion), channel_id=1, source_target_pairs={{0,4},{4,0},{1,5},{5,1},{2,6},{6,2},{3,7},{7,3},{8,12},{12,8},{9,1... | collective-permute-start | bytes 3145736 | tf_op jit(solution)/shard_map/ppermute | solution.py:19
  82.2 18.7 %collective-permute-start.2 = (bf16[528,512]{1,0:T(8,128)(2,1)S(1)}, bf16[528,512]{1,0:T(8,128)(2,1)}, u32[]{:S(2)}, u32[]{:S(2)}) collective-permute-start(bf16[528,512]{1,0:T(8,128)(2,1)S(1)} %get-tuple-element.11.refs_0_), channel_id=1, source_target_pairs={{0,2},{1,3},{2,0},{3,1},{4,6},{5,7},{6,4},{7,5},{8,10},{9,11},{10,... | collective-permute-start | bytes 1622024 | tf_op jit(solution)/shard_map/ppermute | solution.py:24
  84.3 27.7 %collective-permute-start.1 = (bf16[528,512]{1,0:T(8,128)(2,1)S(1)}, bf16[528,512]{1,0:T(8,128)(2,1)}, u32[]{:S(2)}, u32[]{:S(2)}) collective-permute-start(bf16[528,512]{1,0:T(8,128)(2,1)S(1)} %get-tuple-element.11.refs_0_), channel_id=1, source_target_pairs={{0,3},{1,0},{2,1},{3,2},{4,7},{5,4},{6,5},{7,6},{8,11},{9,8},{10,9... | collective-permute-start | bytes 1622024 | tf_op jit(solution)/shard_map/ppermute | solution.py:24
  86.3 25.7 %collective-permute-start = (bf16[528,512]{1,0:T(8,128)(2,1)S(1)}, bf16[528,512]{1,0:T(8,128)(2,1)}, u32[]{:S(2)}, u32[]{:S(2)}) collective-permute-start(bf16[528,512]{1,0:T(8,128)(2,1)S(1)} %get-tuple-element.11.refs_0_), channel_id=1, source_target_pairs={{0,1},{1,2},{2,3},{3,0},{4,5},{5,6},{6,7},{7,4},{8,9},{9,10},{10,1... | collective-permute-start | bytes 1622024 | tf_op jit(solution)/shard_map/ppermute | solution.py:24
  93.8 24.4 %all-to-all-start = ((bf16[4,144,512]{2,1,0:T(8,128)(2,1)}), bf16[4,144,512]{2,1,0:T(8,128)(2,1)S(1)}, u32[]{:S(2)}, u32[]{:S(2)}) async-start(bf16[4,144,512]{2,1,0:T(8,128)(2,1)} %shard_map.48), calls=%async_computation | async-start | bytes 1179648 | tf_op jit(solution)/shard_map/all_to_all | solution.py:358

commit v5 on v4

--- a/solution.py
+++ b/solution.py
@@ -12,6 +12,7 @@
 BLOCK = 128
 SCORE_FACTOR = math.log2(math.e) / math.sqrt(HEAD_DIM)
 SEQ = ("y", "z", "core")
+PIECE = 2
 VMEM_LIMIT = pltpu.CompilerParams(vmem_limit_bytes=20 * 2**20)
 
 
@@ -141,8 +142,9 @@
         lanes = slice(start, start + HEAD_DIM)
         mean, tile, coarse = near_head(query_ref[:, lanes], key_ref[:, lanes], value_ref[:, lanes])
         coarse_ref[:, lanes] = coarse
-        out_ref[:rows, lanes] = mean
-        out_ref[rows:, lanes] = tile
+        for copy in range(out_ref.shape[0]):
+            out_ref[copy, :rows, lanes] = mean
+            out_ref[copy, rows:, lanes] = tile
 
 
 def far_head(coarse, keys, values):
@@ -218,12 +220,22 @@
     )(*(pltpu.with_memory_space_constraint(x, pltpu.HBM) for x in (keys, values)))
 
 
-def near_part(queries, keys, values):
+def near_part(queries, keys, values, copies):
     rows, width = queries.shape
+    column = pl.BlockSpec((rows, HEAD_DIM), lambda h: (0, h))
     return pl.pallas_call(
         near_kernel,
+        grid=(width // HEAD_DIM,),
         compiler_params=VMEM_LIMIT,
-        out_shape=[shape((rows + 16, width)), shape((4 * BLOCK, width))],
+        in_specs=[column] * 3,
+        out_specs=[
+            pl.BlockSpec((copies, rows + 16, HEAD_DIM), lambda h: (0, 0, h)),
+            pl.BlockSpec((4 * BLOCK, HEAD_DIM), lambda h: (0, h)),
+        ],
+        out_shape=[
+            pltpu.HBM((copies, rows + 16, width), jnp.bfloat16),
+            shape((4 * BLOCK, width)),
+        ],
     )(queries, keys, values)
 
 
@@ -266,59 +278,62 @@
 
 
 def mix_kernel(place_ref, *refs):
-    groups = 4
-    near_refs, own_refs = refs[:groups], refs[groups : 2 * groups]
-    far_ref, other_ref, out_ref, attended_ref = refs[2 * groups :]
-    z, core, x, y = (place_ref[i] for i in range(4))
-    width = near_refs[0].shape[1]
+    own_ref, near_ref, far_ref, other_ref, out_ref, attended_ref = refs
+    groups = own_ref.shape[0]
+    z, core, y = (place_ref[i] for i in range(3))
+    width = near_ref.shape[2]
     rows, coarse_rows = out_ref.shape[0], BLOCK
     tiles, ratio = rows // BLOCK, rows // coarse_rows
     heads = width // HEAD_DIM
-    steps = (0, groups - 1, 1, 2)
-    sources = [(x + step) & (groups - 1) for step in steps]
     depth = BLOCK // ratio
     spread_rows = repeated(depth, ratio)
+    sources = [(y + step) & (groups - 1) for step in (0, groups - 1, 1, 2)]
     shares = []
-    for i, g in enumerate(sources):
-        excess = read_stats(far_ref[g, coarse_rows:]) - read_stats(near_refs[i][rows:])
+    for g in sources:
+        excess = read_stats(far_ref[g, coarse_rows:]) - read_stats(near_ref[g, rows:])
         share = 1.0 / (1.0 + jnp.exp2(jnp.minimum(excess, 120.0)))
         shares.extend(share[:, h * HEAD_DIM : (h + 1) * HEAD_DIM] for h in range(heads))
     blank = jnp.zeros((BLOCK - groups * heads * tiles, BLOCK), jnp.float32)
     shares = jnp.concatenate(shares + [blank], axis=0).T
+    piece = PIECE * HEAD_DIM
     for i, g in enumerate(sources):
-        ahead = (g - y) & (groups - 1)
-        index = jnp.where(ahead == 0, 0, jnp.where(ahead == 3, 1, ahead + 1))
-        at = pl.multiple_of(index * width, width)
         for tile in range(tiles):
-            far = jnp.dot(
-                spread_rows,
-                far_ref[g, tile * depth : (tile + 1) * depth],
-                preferred_element_type=jnp.float32,
-            )
-            near = near_refs[i][tile * BLOCK : (tile + 1) * BLOCK].astype(jnp.float32)
-            columns = [(i * heads + h) * tiles + tile for h in range(heads)]
-            share = jnp.concatenate(
-                [jnp.broadcast_to(shares[:, k : k + 1], (BLOCK, HEAD_DIM)) for k in columns], axis=1
-            )
-            attended = (far + share * (near - far)).astype(jnp.bfloat16)
-            attended_ref[tile * BLOCK : (tile + 1) * BLOCK, pl.ds(at, width)] = attended
+            at = slice(tile * BLOCK, (tile + 1) * BLOCK)
+            for first in range(0, heads, PIECE):
+                lanes = slice(first * HEAD_DIM, first * HEAD_DIM + piece)
+                far = jnp.dot(
+                    spread_rows,
+                    far_ref[g, tile * depth : (tile + 1) * depth, lanes],
+                    preferred_element_type=jnp.float32,
+                )
+                near = near_ref[g, at, lanes].astype(jnp.float32)
+                columns = [(i * heads + first + h) * tiles + tile for h in range(PIECE)]
+                share = jnp.concatenate(
+                    [jnp.broadcast_to(shares[:, k : k + 1], (BLOCK, HEAD_DIM)) for k in columns],
+                    axis=1,
+                )
+                start = i * width + first * HEAD_DIM
+                attended_ref[at, start : start + piece] = (far + share * (near - far)).astype(
+                    jnp.bfloat16
+                )
     weights = [
-        jnp.concatenate([own_refs[i][...], other_ref[i]], axis=0) for i in range(groups)
+        jnp.concatenate([own_ref[i], other_ref[i]], axis=0) for i in range(groups)
     ]
     total = times(attended_ref[...], jnp.concatenate(weights, axis=1))
     out_ref[...] = placed(total, z, core).astype(jnp.bfloat16)
 
 
-def mix_part(place, near, own, far, other):
-    rows, width = near[0].shape[0] - 16, near[0].shape[1]
+def mix_part(place, own, near, far, other):
+    groups, rows, width = near.shape
+    rows = rows - 16
     vmem = pl.BlockSpec(memory_space=pltpu.VMEM)
     return pl.pallas_call(
         mix_kernel,
         compiler_params=VMEM_LIMIT,
-        in_specs=[pl.BlockSpec(memory_space=pltpu.SMEM)] + [vmem] * (2 * len(near) + 2),
-        out_shape=shape((rows, 2 * own[0].shape[0])),
-        scratch_shapes=[pltpu.VMEM((rows, len(near) * width), jnp.bfloat16)],
-    )(place, *map(in_vmem, (*near, *own, far, other)))
+        in_specs=[pl.BlockSpec(memory_space=pltpu.SMEM)] + [vmem] * 4,
+        out_shape=shape((rows, 2 * own.shape[1])),
+        scratch_shapes=[pltpu.VMEM((rows, groups * width), jnp.bfloat16)],
+    )(place, *map(in_vmem, (own, near, far, other)))
 
 
 def body(queries, key_vectors, values, out_weight):
@@ -340,14 +355,12 @@
     p2, p3, p4, p5 = pooled_levels(key_vectors, values)
     a = swap(jnp.concatenate([p5, paired(weights)], axis=1), "z", 4)
     weights = jnp.concatenate([weights, joined(a[:, 16:])], axis=0)
-    near, coarse = near_part(queries, key_vectors, values)
+    near, coarse = near_part(queries, key_vectors, values, heads)
     b = swap(jnp.concatenate([a[:, :16], p4, paired(weights)], axis=1), "z", 2)
     weights = jnp.concatenate([weights, joined(b[:, 48:])], axis=0)
-    right = shift(near, "head", 1)
-    left = shift(near, "head", -1)
+    near = lax.all_to_all(near, "head", 0, 0)
     c = swap(jnp.concatenate([a[:, :16], b[:, :48], p3, paired(weights)], axis=1), "z", 1)
     w_across = lax.ppermute(weights, "z", [(z, across(z)) for z in range(ring)])
-    over = shift(near, "head", 2)
     w_beside = swap(w_across, "z", 1)
     d = swap(jnp.concatenate([a[:, :16], b[:, :48], c[:, :128], p2], axis=1), "core", 1)
     weights = jnp.concatenate([weights, joined(c[:, 128:]), w_across, w_beside], axis=0)
@@ -355,10 +368,12 @@
     for step in (1, -1, 2):
         own.append(shift(weights, "y", step))
     far = far_part(coarse, (a, b, c, d), heads)
+    far, near = lax.optimization_barrier((far, near))
     far = lax.all_to_all(far, "head", 0, 0)
-    other = swap(jnp.stack(own), "core", 1)
-    place = jnp.stack([lax.axis_index(name) for name in ("z", "core", "head", "y")]).astype(jnp.int32)
-    return mix_part(place, (near, right, left, over), own, far, other)
+    own = jnp.stack(own)
+    other = swap(own, "core", 1)
+    place = jnp.stack([lax.axis_index(name) for name in ("z", "core", "y")]).astype(jnp.int32)
+    return mix_part(place, own, near, far, other)
 
 
 def solution(mesh):

time: 124 us -> 107 us (0.86)
  the two profiles are of different devices: /device:TPU:70 before, /device:TPU:1 now
where the time goes in v5:
time: 107 us; the launch traced here: 106 us
  starting transfers between devices  67.4 us (63%)
  waiting for transfers between devices  19.1 us (18%)
  Pallas kernels  17.5 us (16%)
  local copies, waits for them, and re-layouts  1.71 us (2%)
    ppermute x6, starting transfers between devices, swap(): lax.ppermute(value, axis, [(s, s ^ mask) for s in range(lax.axis_size(axi...  36.4 us
    all_to_all x1, waiting for transfers between devices, body(): far = lax.all_to_all(far, 'head', 0, 0)  10 us
    ppermute x3, starting transfers between devices, shift(): lax.ppermute(value, axis, [(s, (s + step) % size) for s in range(size)])  9.43 us
    pallas_call x1, Pallas kernels, near_part(): pl.pallas_call(near_kernel, grid=(width // HEAD_DIM,), compiler_params=VM...  8.63 us
    ppermute x1, starting transfers between devices, body(): w_across = lax.ppermute(weights, 'z', [(z, across(z)) for z in range(ring)])  8.22 us
    all_to_all x1, starting transfers between devices, body(): near = lax.all_to_all(near, 'head', 0, 0)  7.27 us
    ppermute x6, waiting for transfers between devices, swap(): lax.ppermute(value, axis, [(s, s ^ mask) for s in range(lax.axis_size(axi...  5.79 us
    all_to_all x1, starting transfers between devices, body(): far = lax.all_to_all(far, 'head', 0, 0)  4.51 us
  transfers between devices with their start and end apart: 13, of which 4 were waited for; matrix products, arithmetic and copies ran while one was open for 0% of the time, Pallas kernels for 12%

profile of v5, /device:TPU:1, one launch (start us, length us, event | category | flops | bytes accessed | tf_op | source)
XLA Modules:
  0.0 106.3 jit_solution(11021997189236309970)
XLA Ops:
  0.0 0.0 copy-start.1
  0.0 0.0 copy-start.2
  0.0 0.0 copy-start.3
  0.0 1.5 %collective-permute-start = (bf16[16,512]{1,0:T(8,128)(2,1)}, bf16[16,512]{1,0:T(8,128)(2,1)S(1)}, u32[]{:S(2)}, u32[]{:S(2)}) collective-permute-start(bf16[16,512]{1,0:T(8,128)(2,1)} %bitcast.27), channel_id=1, source_target_pairs={{0,0},{1,128},{2,256},{3,384},{128,1},{129,129},{130,257},{131,385... | collective-permute-start | bytes 49160 | tf_op jit(solution)/shard_map/ppermute | solution.py:354
  1.5 2.8 %shard_map.46 = (bf16[2,128,512]{2,1,0:T(8,128)(2,1)S(1)}, bf16[2,64,512]{2,1,0:T(8,128)(2,1)S(1)}, bf16[2,32,512]{2,1,0:T(8,128)(2,1)S(1)}, bf16[2,16,512]{2,1,0:T(8,128)(2,1)S(1)}) custom-call(bf16[512,512]{1,0:T(8,128)(2,1)} %key_ref.3, bf16[512,512]{1,0:T(8,128)(2,1)} %value_ref.3), custom_call_target="tpu_custom_call" | custom-call | tf_op jit(solution)/shard_map/pallas_call | solution.py:211
  4.3 0.0 collective-permute-done
  4.3 9.6 %collective-permute-start.1 = (bf16[2,24,512]{2,1,0:T(8,128)(2,1)S(1)}, bf16[2,24,512]{2,1,0:T(8,128)(2,1)S(1)}, u32[]{:S(2)}, u32[]{:S(2)}) collective-permute-start(bf16[2,24,512]{2,1,0:T(8,128)(2,1)S(1)} %pad_maximum_fusion.5), channel_id=1, source_target_pairs={{0,32},{8,40},{16,48},{24,56},{32,0},{40,8},{48,16},{56,24},{64,96... | collective-permute-start | bytes 147464 | tf_op jit(solution)/shard_map/ppermute | solution.py:20
  14.0 1.5 %collective-permute-done.1.a_ref = bf16[2,24,512]{2,1,0:T(8,128)(2,1)S(1)} collective-permute-done((bf16[2,24,512]{2,1,0:T(8,128)(2,1)S(1)}, bf16[2,24,512]{2,1,0:T(8,128)(2,1)S(1)}, u32[]{:S(2)}, u32[]{:S(2)}) %collective-permute-start.1) | collective-permute-done | bytes 49184 | tf_op jit(solution)/shard_map/ppermute | solution.py:20
  15.5 6.1 %collective-permute-start.2 = (bf16[2,64,512]{2,1,0:T(8,128)(2,1)S(1)}, bf16[2,64,512]{2,1,0:T(8,128)(2,1)S(1)}, u32[]{:S(2)}, u32[]{:S(2)}) collective-permute-start(bf16[2,64,512]{2,1,0:T(8,128)(2,1)S(1)} %pad_maximum_fusion.3), channel_id=1, source_target_pairs={{0,16},{8,24},{16,0},{24,8},{32,48},{40,56},{48,32},{56,40},{64,80... | collective-permute-start | bytes 393224 | tf_op jit(solution)/shard_map/ppermute | solution.py:20
  21.5 0.0 copy-done.1
  21.5 0.0 copy-done.2
  21.6 0.0 copy-done.3
  21.6 8.6 %shard_map.47 = (bf16[4,528,512]{2,1,0:T(8,128)(2,1)}, bf16[512,512]{1,0:T(8,128)(2,1)S(1)}) custom-call(bf16[512,512]{1,0:T(8,128)(2,1)S(1)} %copy-done.3, bf16[512,512]{1,0:T(8,128)(2,1)S(1)} %copy-done.1, bf16[512,512]{1,0:T(8,128)(2,1)S(1)} %copy-done.2), custom_call_target="tpu_custom_call" | custom-call | tf_op jit(solution)/shard_map/pallas_call | solution.py:226
  30.2 0.0 copy-start.4
  30.2 0.8 copy-done.4
  31.0 7.3 %all-to-all-start = ((bf16[4,528,512]{2,1,0:T(8,128)(2,1)}), bf16[4,528,512]{2,1,0:T(8,128)(2,1)S(1)}, u32[]{:S(2)}, u32[]{:S(2)}) async-start(bf16[4,528,512]{2,1,0:T(8,128)(2,1)} %get-tuple-element.18), calls=%async_computation | async-start | bytes 4325376 | tf_op jit(solution)/shard_map/all_to_all | solution.py:361
  38.3 0.0 collective-permute-done.2.b_ref
  38.3 3.5 %collective-permute-start.3 = (bf16[2,160,512]{2,1,0:T(8,128)(2,1)S(1)}, bf16[2,160,512]{2,1,0:T(8,128)(2,1)S(1)}, u32[]{:S(2)}, u32[]{:S(2)}) collective-permute-start(bf16[2,160,512]{2,1,0:T(8,128)(2,1)S(1)} %pad_maximum_fusion.2), channel_id=1, source_target_pairs={{0,8},{8,0},{16,24},{24,16},{32,40},{40,32},{48,56},{56,48},{64,72... | collective-permute-start | bytes 983048 | tf_op jit(solution)/shard_map/ppermute | solution.py:20
  41.9 8.2 %collective-permute-start.4 = (bf16[64,512]{1,0:T(8,128)(2,1)S(1)}, bf16[64,512]{1,0:T(8,128)(2,1)S(1)}, u32[]{:S(2)}, u32[]{:S(2)}) collective-permute-start(bf16[64,512]{1,0:T(8,128)(2,1)S(1)} %pad_maximum_fusion.4), channel_id=1, source_target_pairs={{0,96},{8,104},{16,112},{24,120},{32,64},{40,72},{48,80},{56,88},{... | collective-permute-start | bytes 196616 | tf_op jit(solution)/shard_map/ppermute | solution.py:363
  50.1 3.3 %collective-permute-done.4 = bf16[64,512]{1,0:T(8,128)(2,1)S(1)} collective-permute-done((bf16[64,512]{1,0:T(8,128)(2,1)S(1)}, bf16[64,512]{1,0:T(8,128)(2,1)S(1)}, u32[]{:S(2)}, u32[]{:S(2)}) %collective-permute-start.4) | collective-permute-done | bytes 65568 | tf_op jit(solution)/shard_map/ppermute | solution.py:363
  53.4 1.9 %collective-permute-start.5 = (bf16[64,512]{1,0:T(8,128)(2,1)S(1)}, bf16[64,512]{1,0:T(8,128)(2,1)S(1)}, u32[]{:S(2)}, u32[]{:S(2)}) collective-permute-start(bf16[64,512]{1,0:T(8,128)(2,1)S(1)} %collective-permute-done.4), channel_id=1, source_target_pairs={{0,8},{8,0},{16,24},{24,16},{32,40},{40,32},{48,56},{56,48},{64,72... | collective-permute-start | bytes 196616 | tf_op jit(solution)/shard_map/ppermute | solution.py:20
  55.4 0.0 collective-permute-done.3.c_ref
  55.4 4.3 %collective-permute-done.5 = bf16[64,512]{1,0:T(8,128)(2,1)S(1)} collective-permute-done((bf16[64,512]{1,0:T(8,128)(2,1)S(1)}, bf16[64,512]{1,0:T(8,128)(2,1)S(1)}, u32[]{:S(2)}, u32[]{:S(2)}) %collective-permute-start.5) | collective-permute-done | bytes 65568 | tf_op jit(solution)/shard_map/ppermute | solution.py:20
  59.7 2.9 %collective-permute-start.6 = (bf16[256,512]{1,0:T(8,128)(2,1)S(1)}, bf16[256,512]{1,0:T(8,128)(2,1)S(1)}, u32[]{:S(2)}, u32[]{:S(2)}) collective-permute-start(bf16[256,512]{1,0:T(8,128)(2,1)S(1)} %constant_dynamic-update-slice_fusion), channel_id=1, source_target_pairs={{0,128},{128,256},{256,384},{384,0},{1,129},{129,257},{257,385},{3... | collective-permute-start | bytes 786440 | tf_op jit(solution)/shard_map/ppermute | solution.py:25
  62.7 3.6 %collective-permute-start.7 = (bf16[256,512]{1,0:T(8,128)(2,1)S(1)}, bf16[256,512]{1,0:T(8,128)(2,1)S(1)}, u32[]{:S(2)}, u32[]{:S(2)}) collective-permute-start(bf16[256,512]{1,0:T(8,128)(2,1)S(1)} %constant_dynamic-update-slice_fusion), channel_id=1, source_target_pairs={{0,384},{128,0},{256,128},{384,256},{1,385},{129,1},{257,129},{385... | collective-permute-start | bytes 786440 | tf_op jit(solution)/shard_map/ppermute | solution.py:25
  66.2 3.0 %collective-permute-start.8 = (bf16[256,512]{1,0:T(8,128)(2,1)S(1)}, bf16[256,512]{1,0:T(8,128)(2,1)S(1)}, u32[]{:S(2)}, u32[]{:S(2)}) collective-permute-start(bf16[256,512]{1,0:T(8,128)(2,1)S(1)} %constant_dynamic-update-slice_fusion), channel_id=1, source_target_pairs={{0,256},{128,384},{256,0},{384,128},{1,257},{129,385},{257,1},{385... | collective-permute-start | bytes 786440 | tf_op jit(solution)/shard_map/ppermute | solution.py:25
  69.3 0.0 copy-start.5
  69.3 9.0 %collective-permute-start.9 = (bf16[2,320,512]{2,1,0:T(8,128)(2,1)S(1)}, bf16[2,320,512]{2,1,0:T(8,128)(2,1)S(1)}, u32[]{:S(2)}, u32[]{:S(2)}) collective-permute-start(bf16[2,320,512]{2,1,0:T(8,128)(2,1)S(1)} %pad_maximum_fusion.1), channel_id=1, source_target_pairs={{0,4},{4,0},{1,5},{5,1},{2,6},{6,2},{3,7},{7,3},{8,12},{12,8},{9,1... | collective-permute-start | bytes 1966088 | tf_op jit(solution)/shard_map/ppermute | solution.py:20
  78.3 0.0 collective-permute-done.6
  78.3 0.0 collective-permute-done.7
  78.3 0.0 collective-permute-done.8
  78.3 0.1 pad_maximum_fusion.refs_0_
  78.5 6.3 %collective-permute-start.10 = (bf16[4,256,512]{2,1,0:T(8,128)(2,1)S(1)}, bf16[4,256,512]{2,1,0:T(8,128)(2,1)}, u32[]{:S(2)}, u32[]{:S(2)}) collective-permute-start(bf16[4,256,512]{2,1,0:T(8,128)(2,1)S(1)} %pad_maximum_fusion.refs_0_), channel_id=1, source_target_pairs={{0,4},{4,0},{1,5},{5,1},{2,6},{6,2},{3,7},{7,3},{8,12},{12,8},{9,1... | collective-permute-start | bytes 3145736 | tf_op jit(solution)/shard_map/ppermute | solution.py:20
  84.7 0.0 collective-permute-done.9.d_ref
  84.7 0.0 copy-done.5
  84.8 1.6 %shard_map.48 = bf16[4,144,512]{2,1,0:T(8,128)(2,1)S(1)} custom-call(bf16[512,512]{1,0:T(8,128)(2,1)S(1)} %copy-done.5, bf16[2,24,512]{2,1,0:T(8,128)(2,1)S(1)} %collective-permute-done.1.a_ref, bf16[2,64,512]{2,1,0:T(8,128)(2,1)S(1)} %collective-permute-done.2.b_ref, bf16[2,160,512]{2,1,0:T(8,128)(2,1)S(1)} %collective-permute-done.3.c_ref, ...), custom_call_target="tpu_custom_call" | custom-call | tf_op jit(solution)/shard_map/pallas_call | solution.py:248
  86.4 0.0 copy-start
  86.4 0.8 copy-done
  87.2 0.0 all-to-all-done.refs_1_
  87.2 4.5 %all-to-all-start.1 = ((bf16[4,144,512]{2,1,0:T(8,128)(2,1)}), bf16[4,144,512]{2,1,0:T(8,128)(2,1)}, u32[]{:S(2)}, u32[]{:S(2)}) async-start(bf16[4,144,512]{2,1,0:T(8,128)(2,1)} %copy-done), calls=%async_computation.1 | async-start | bytes 1179648 | tf_op jit(solution)/shard_map/all_to_all | solution.py:372
  91.7 0.1 pad_add_fusion.place_ref
  91.8 0.0 collective-permute-done.10.refs_3_
  91.8 10.0 %all-to-all-done.1.refs_2_ = bf16[4,144,512]{2,1,0:T(8,128)(2,1)} async-done(((bf16[4,144,512]{2,1,0:T(8,128)(2,1)}), bf16[4,144,512]{2,1,0:T(8,128)(2,1)}, u32[]{:S(2)}, u32[]{:S(2)}) %all-to-all-start.1) | async-done | bytes 589856 | tf_op jit(solution)/shard_map/all_to_all | solution.py:372
  101.8 4.5 %shard_map.49 = bf16[512,512]{1,0:T(8,128)(2,1)} custom-call(s32[3]{0:T(128)S(1)} %pad_add_fusion.place_ref, bf16[4,256,512]{2,1,0:T(8,128)(2,1)S(1)} %pad_maximum_fusion.refs_0_, bf16[4,528,512]{2,1,0:T(8,128)(2,1)S(1)} %all-to-all-done.refs_1_, bf16[4,144,512]{2,1,0:T(8,128)(2,1)} %all-to-all-done.1.refs_2_, ...), custom_call_target="tpu_custom_call" | custom-call | tf_op jit(solution)/shard_map/pallas_call | solution.py:330
  (18 shorter events, 0.2 us)
Async XLA Ops:
  0.0 21.5 %copy-start.1 = (bf16[512,512]{1,0:T(8,128)(2,1)S(1)}, bf16[512,512]{1,0:T(8,128)(2,1)}, u32[]{:S(2)}) copy-start(bf16[512,512]{1,0:T(8,128)(2,1)} %key_ref.3) | copy-start | bytes 1572868
  0.0 21.5 %copy-start.2 = (bf16[512,512]{1,0:T(8,128)(2,1)S(1)}, bf16[512,512]{1,0:T(8,128)(2,1)}, u32[]{:S(2)}) copy-start(bf16[512,512]{1,0:T(8,128)(2,1)} %value_ref.3) | copy-start | bytes 1572868
  0.0 21.6 %copy-start.3 = (bf16[512,512]{1,0:T(8,128)(2,1)S(1)}, bf16[512,512]{1,0:T(8,128)(2,1)}, u32[]{:S(2)}) copy-start(bf16[512,512]{1,0:T(8,128)(2,1)} %query_ref.1) | copy-start | bytes 1572868
  0.0 4.3 %collective-permute-start = (bf16[16,512]{1,0:T(8,128)(2,1)}, bf16[16,512]{1,0:T(8,128)(2,1)S(1)}, u32[]{:S(2)}, u32[]{:S(2)}) collective-permute-start(bf16[16,512]{1,0:T(8,128)(2,1)} %bitcast.27), channel_id=1, source_target_pairs={{0,0},{1,128},{2,256},{3,384},{128,1},{129,129},{130,257},{131,385... | collective-permute-start | bytes 49160 | tf_op jit(solution)/shard_map/ppermute | solution.py:354
  4.3 11.1 %collective-permute-start.1 = (bf16[2,24,512]{2,1,0:T(8,128)(2,1)S(1)}, bf16[2,24,512]{2,1,0:T(8,128)(2,1)S(1)}, u32[]{:S(2)}, u32[]{:S(2)}) collective-permute-start(bf16[2,24,512]{2,1,0:T(8,128)(2,1)S(1)} %pad_maximum_fusion.5), channel_id=1, source_target_pairs={{0,32},{8,40},{16,48},{24,56},{32,0},{40,8},{48,16},{56,24},{64,96... | collective-permute-start | bytes 147464 | tf_op jit(solution)/shard_map/ppermute | solution.py:20
  15.5 22.8 %collective-permute-start.2 = (bf16[2,64,512]{2,1,0:T(8,128)(2,1)S(1)}, bf16[2,64,512]{2,1,0:T(8,128)(2,1)S(1)}, u32[]{:S(2)}, u32[]{:S(2)}) collective-permute-start(bf16[2,64,512]{2,1,0:T(8,128)(2,1)S(1)} %pad_maximum_fusion.3), channel_id=1, source_target_pairs={{0,16},{8,24},{16,0},{24,8},{32,48},{40,56},{48,32},{56,40},{64,80... | collective-permute-start | bytes 393224 | tf_op jit(solution)/shard_map/ppermute | solution.py:20
  30.2 0.8 copy-start.4
  31.0 56.2 %all-to-all-start = ((bf16[4,528,512]{2,1,0:T(8,128)(2,1)}), bf16[4,528,512]{2,1,0:T(8,128)(2,1)S(1)}, u32[]{:S(2)}, u32[]{:S(2)}) async-start(bf16[4,528,512]{2,1,0:T(8,128)(2,1)} %get-tuple-element.18), calls=%async_computation | async-start | bytes 4325376 | tf_op jit(solution)/shard_map/all_to_all | solution.py:361
  38.3 17.0 %collective-permute-start.3 = (bf16[2,160,512]{2,1,0:T(8,128)(2,1)S(1)}, bf16[2,160,512]{2,1,0:T(8,128)(2,1)S(1)}, u32[]{:S(2)}, u32[]{:S(2)}) collective-permute-start(bf16[2,160,512]{2,1,0:T(8,128)(2,1)S(1)} %pad_maximum_fusion.2), channel_id=1, source_target_pairs={{0,8},{8,0},{16,24},{24,16},{32,40},{40,32},{48,56},{56,48},{64,72... | collective-permute-start | bytes 983048 | tf_op jit(solution)/shard_map/ppermute | solution.py:20
  41.9 11.5 %collective-permute-start.4 = (bf16[64,512]{1,0:T(8,128)(2,1)S(1)}, bf16[64,512]{1,0:T(8,128)(2,1)S(1)}, u32[]{:S(2)}, u32[]{:S(2)}) collective-permute-start(bf16[64,512]{1,0:T(8,128)(2,1)S(1)} %pad_maximum_fusion.4), channel_id=1, source_target_pairs={{0,96},{8,104},{16,112},{24,120},{32,64},{40,72},{48,80},{56,88},{... | collective-permute-start | bytes 196616 | tf_op jit(solution)/shard_map/ppermute | solution.py:363
  53.4 6.3 %collective-permute-start.5 = (bf16[64,512]{1,0:T(8,128)(2,1)S(1)}, bf16[64,512]{1,0:T(8,128)(2,1)S(1)}, u32[]{:S(2)}, u32[]{:S(2)}) collective-permute-start(bf16[64,512]{1,0:T(8,128)(2,1)S(1)} %collective-permute-done.4), channel_id=1, source_target_pairs={{0,8},{8,0},{16,24},{24,16},{32,40},{40,32},{48,56},{56,48},{64,72... | collective-permute-start | bytes 196616 | tf_op jit(solution)/shard_map/ppermute | solution.py:20
  59.7 18.6 %collective-permute-start.6 = (bf16[256,512]{1,0:T(8,128)(2,1)S(1)}, bf16[256,512]{1,0:T(8,128)(2,1)S(1)}, u32[]{:S(2)}, u32[]{:S(2)}) collective-permute-start(bf16[256,512]{1,0:T(8,128)(2,1)S(1)} %constant_dynamic-update-slice_fusion), channel_id=1, source_target_pairs={{0,128},{128,256},{256,384},{384,0},{1,129},{129,257},{257,385},{3... | collective-permute-start | bytes 786440 | tf_op jit(solution)/shard_map/ppermute | solution.py:25
  62.7 15.6 %collective-permute-start.7 = (bf16[256,512]{1,0:T(8,128)(2,1)S(1)}, bf16[256,512]{1,0:T(8,128)(2,1)S(1)}, u32[]{:S(2)}, u32[]{:S(2)}) collective-permute-start(bf16[256,512]{1,0:T(8,128)(2,1)S(1)} %constant_dynamic-update-slice_fusion), channel_id=1, source_target_pairs={{0,384},{128,0},{256,128},{384,256},{1,385},{129,1},{257,129},{385... | collective-permute-start | bytes 786440 | tf_op jit(solution)/shard_map/ppermute | solution.py:25
  66.2 12.1 %collective-permute-start.8 = (bf16[256,512]{1,0:T(8,128)(2,1)S(1)}, bf16[256,512]{1,0:T(8,128)(2,1)S(1)}, u32[]{:S(2)}, u32[]{:S(2)}) collective-permute-start(bf16[256,512]{1,0:T(8,128)(2,1)S(1)} %constant_dynamic-update-slice_fusion), channel_id=1, source_target_pairs={{0,256},{128,384},{256,0},{384,128},{1,257},{129,385},{257,1},{385... | collective-permute-start | bytes 786440 | tf_op jit(solution)/shard_map/ppermute | solution.py:25
  69.3 15.5 %copy-start.5 = (bf16[512,512]{1,0:T(8,128)(2,1)S(1)}, bf16[512,512]{1,0:T(8,128)(2,1)}, u32[]{:S(2)}) copy-start(bf16[512,512]{1,0:T(8,128)(2,1)} %copy-done.4) | copy-start | bytes 1572868
  69.3 15.4 %collective-permute-start.9 = (bf16[2,320,512]{2,1,0:T(8,128)(2,1)S(1)}, bf16[2,320,512]{2,1,0:T(8,128)(2,1)S(1)}, u32[]{:S(2)}, u32[]{:S(2)}) collective-permute-start(bf16[2,320,512]{2,1,0:T(8,128)(2,1)S(1)} %pad_maximum_fusion.1), channel_id=1, source_target_pairs={{0,4},{4,0},{1,5},{5,1},{2,6},{6,2},{3,7},{7,3},{8,12},{12,8},{9,1... | collective-permute-start | bytes 1966088 | tf_op jit(solution)/shard_map/ppermute | solution.py:20
  78.5 13.3 %collective-permute-start.10 = (bf16[4,256,512]{2,1,0:T(8,128)(2,1)S(1)}, bf16[4,256,512]{2,1,0:T(8,128)(2,1)}, u32[]{:S(2)}, u32[]{:S(2)}) collective-permute-start(bf16[4,256,512]{2,1,0:T(8,128)(2,1)S(1)} %pad_maximum_fusion.refs_0_), channel_id=1, source_target_pairs={{0,4},{4,0},{1,5},{5,1},{2,6},{6,2},{3,7},{7,3},{8,12},{12,8},{9,1... | collective-permute-start | bytes 3145736 | tf_op jit(solution)/shard_map/ppermute | solution.py:20
  86.4 0.8 copy-start
  87.2 14.6 %all-to-all-start.1 = ((bf16[4,144,512]{2,1,0:T(8,128)(2,1)}), bf16[4,144,512]{2,1,0:T(8,128)(2,1)}, u32[]{:S(2)}, u32[]{:S(2)}) async-start(bf16[4,144,512]{2,1,0:T(8,128)(2,1)} %copy-done), calls=%async_computation.1 | async-start | bytes 1179648 | tf_op jit(solution)/shard_map/all_to_all | solution.py:372

commit v6 on v5

--- a/solution.py
+++ b/solution.py
@@ -136,15 +136,23 @@
     )
 
 
-def near_kernel(query_ref, key_ref, value_ref, out_ref, coarse_ref):
+def near_kernel(query_ref, key_ref, value_ref, out_ref, coarse_ref, held_ref, sems):
     rows = query_ref.shape[0]
-    for start in range(0, query_ref.shape[1], HEAD_DIM):
-        lanes = slice(start, start + HEAD_DIM)
+    sends = []
+    for head in range(query_ref.shape[1] // HEAD_DIM):
+        lanes = slice(head * HEAD_DIM, (head + 1) * HEAD_DIM)
         mean, tile, coarse = near_head(query_ref[:, lanes], key_ref[:, lanes], value_ref[:, lanes])
         coarse_ref[:, lanes] = coarse
+        held_ref[:rows, lanes] = mean
+        held_ref[rows:, lanes] = tile
         for copy in range(out_ref.shape[0]):
-            out_ref[copy, :rows, lanes] = mean
-            out_ref[copy, rows:, lanes] = tile
+            send = pltpu.make_async_copy(
+                held_ref.at[:, lanes], out_ref.at[copy, :, lanes], sems.at[head, copy]
+            )
+            send.start()
+            sends.append(send)
+    for send in sends:
+        send.wait()
 
 
 def far_head(coarse, keys, values):
@@ -222,19 +230,17 @@
 
 def near_part(queries, keys, values, copies):
     rows, width = queries.shape
-    column = pl.BlockSpec((rows, HEAD_DIM), lambda h: (0, h))
     return pl.pallas_call(
         near_kernel,
-        grid=(width // HEAD_DIM,),
         compiler_params=VMEM_LIMIT,
-        in_specs=[column] * 3,
-        out_specs=[
-            pl.BlockSpec((copies, rows + 16, HEAD_DIM), lambda h: (0, 0, h)),
-            pl.BlockSpec((4 * BLOCK, HEAD_DIM), lambda h: (0, h)),
-        ],
+        out_specs=[pl.BlockSpec(memory_space=pl.ANY), pl.BlockSpec(memory_space=pltpu.VMEM)],
         out_shape=[
             pltpu.HBM((copies, rows + 16, width), jnp.bfloat16),
             shape((4 * BLOCK, width)),
+        ],
+        scratch_shapes=[
+            pltpu.VMEM((rows + 16, width), jnp.bfloat16),
+            pltpu.SemaphoreType.DMA((width // HEAD_DIM, copies)),
         ],
     )(queries, keys, values)
 
@@ -248,7 +254,7 @@
     return pl.pallas_call(
         far_kernel,
         compiler_params=VMEM_LIMIT,
-        out_shape=shape((copies, BLOCK + 16, width)),
+        out_shape=pltpu.HBM((copies, BLOCK + 16, width), jnp.bfloat16),
     )(in_vmem(coarse), *map(in_vmem, pieces))
 
 

time: 107 us -> 106 us (level)
  no operation moved by 1% of the time
where the time goes in v6:
time: 106 us; the launch traced here: 105 us
  starting transfers between devices  67.4 us (64%)
  waiting for transfers between devices  19.1 us (18%)
  Pallas kernels  17.2 us (16%)
    ppermute x6, starting transfers between devices, swap(): lax.ppermute(value, axis, [(s, s ^ mask) for s in range(lax.axis_size(axi...  36.4 us
    all_to_all x1, waiting for transfers between devices, body(): far = lax.all_to_all(far, 'head', 0, 0)  10 us
    ppermute x3, starting transfers between devices, shift(): lax.ppermute(value, axis, [(s, (s + step) % size) for s in range(size)])  9.43 us
    ppermute x1, starting transfers between devices, body(): w_across = lax.ppermute(weights, 'z', [(z, across(z)) for z in range(ring)])  8.22 us
    pallas_call x1, Pallas kernels, near_part(): pl.pallas_call(near_kernel, compiler_params=VMEM_LIMIT, out_specs=[pl.Blo...  7.51 us
    all_to_all x1, starting transfers between devices, body(): near = lax.all_to_all(near, 'head', 0, 0)  7.27 us
    ppermute x6, waiting for transfers between devices, swap(): lax.ppermute(value, axis, [(s, s ^ mask) for s in range(lax.axis_size(axi...  5.79 us
    all_to_all x1, starting transfers between devices, body(): far = lax.all_to_all(far, 'head', 0, 0)  4.51 us
  transfers between devices with their start and end apart: 13, of which 4 were waited for; matrix products, arithmetic and copies ran while one was open for 0% of the time, Pallas kernels for 12%

profile of v6, /device:TPU:1, one launch (start us, length us, event | category | flops | bytes accessed | tf_op | source)
XLA Modules:
  0.0 105.2 jit_solution(16604149419767793392)
XLA Ops:
  0.0 0.0 copy-start
  0.0 0.0 copy-start.1
  0.0 0.0 copy-start.2
  0.0 1.5 %collective-permute-start = (bf16[16,512]{1,0:T(8,128)(2,1)}, bf16[16,512]{1,0:T(8,128)(2,1)S(1)}, u32[]{:S(2)}, u32[]{:S(2)}) collective-permute-start(bf16[16,512]{1,0:T(8,128)(2,1)} %bitcast.27), channel_id=1, source_target_pairs={{0,0},{1,128},{2,256},{3,384},{128,1},{129,129},{130,257},{131,385... | collective-permute-start | bytes 49160 | tf_op jit(solution)/shard_map/ppermute | solution.py:360
  1.5 2.8 %shard_map.46 = (bf16[2,128,512]{2,1,0:T(8,128)(2,1)S(1)}, bf16[2,64,512]{2,1,0:T(8,128)(2,1)S(1)}, bf16[2,32,512]{2,1,0:T(8,128)(2,1)S(1)}, bf16[2,16,512]{2,1,0:T(8,128)(2,1)S(1)}) custom-call(bf16[512,512]{1,0:T(8,128)(2,1)} %key_ref.3, bf16[512,512]{1,0:T(8,128)(2,1)} %value_ref.3), custom_call_target="tpu_custom_call" | custom-call | tf_op jit(solution)/shard_map/pallas_call | solution.py:219
  4.3 0.0 collective-permute-done
  4.3 9.6 %collective-permute-start.1 = (bf16[2,24,512]{2,1,0:T(8,128)(2,1)S(1)}, bf16[2,24,512]{2,1,0:T(8,128)(2,1)S(1)}, u32[]{:S(2)}, u32[]{:S(2)}) collective-permute-start(bf16[2,24,512]{2,1,0:T(8,128)(2,1)S(1)} %pad_maximum_fusion.5), channel_id=1, source_target_pairs={{0,32},{8,40},{16,48},{24,56},{32,0},{40,8},{48,16},{56,24},{64,96... | collective-permute-start | bytes 147464 | tf_op jit(solution)/shard_map/ppermute | solution.py:20
  14.0 1.5 %collective-permute-done.1.a_ref = bf16[2,24,512]{2,1,0:T(8,128)(2,1)S(1)} collective-permute-done((bf16[2,24,512]{2,1,0:T(8,128)(2,1)S(1)}, bf16[2,24,512]{2,1,0:T(8,128)(2,1)S(1)}, u32[]{:S(2)}, u32[]{:S(2)}) %collective-permute-start.1) | collective-permute-done | bytes 49184 | tf_op jit(solution)/shard_map/ppermute | solution.py:20
  15.5 6.1 %collective-permute-start.2 = (bf16[2,64,512]{2,1,0:T(8,128)(2,1)S(1)}, bf16[2,64,512]{2,1,0:T(8,128)(2,1)S(1)}, u32[]{:S(2)}, u32[]{:S(2)}) collective-permute-start(bf16[2,64,512]{2,1,0:T(8,128)(2,1)S(1)} %pad_maximum_fusion.3), channel_id=1, source_target_pairs={{0,16},{8,24},{16,0},{24,8},{32,48},{40,56},{48,32},{56,40},{64,80... | collective-permute-start | bytes 393224 | tf_op jit(solution)/shard_map/ppermute | solution.py:20
  21.5 0.0 copy-done
  21.5 0.0 copy-done.1
  21.6 0.0 copy-done.2
  21.6 7.5 %shard_map.47 = (bf16[4,528,512]{2,1,0:T(8,128)(2,1)}, bf16[512,512]{1,0:T(8,128)(2,1)S(1)}) custom-call(bf16[512,512]{1,0:T(8,128)(2,1)S(1)} %copy-done.2, bf16[512,512]{1,0:T(8,128)(2,1)S(1)} %copy-done, bf16[512,512]{1,0:T(8,128)(2,1)S(1)} %copy-done.1), custom_call_target="tpu_custom_call" | custom-call | tf_op jit(solution)/shard_map/pallas_call | solution.py:233
  29.1 0.0 copy-start.3
  29.1 0.8 copy-done.3
  29.9 7.3 %all-to-all-start = ((bf16[4,528,512]{2,1,0:T(8,128)(2,1)}), bf16[4,528,512]{2,1,0:T(8,128)(2,1)S(1)}, u32[]{:S(2)}, u32[]{:S(2)}) async-start(bf16[4,528,512]{2,1,0:T(8,128)(2,1)} %get-tuple-element.18), calls=%async_computation | async-start | bytes 4325376 | tf_op jit(solution)/shard_map/all_to_all | solution.py:367
  37.1 0.0 collective-permute-done.2.b_ref
  37.2 3.5 %collective-permute-start.3 = (bf16[2,160,512]{2,1,0:T(8,128)(2,1)S(1)}, bf16[2,160,512]{2,1,0:T(8,128)(2,1)S(1)}, u32[]{:S(2)}, u32[]{:S(2)}) collective-permute-start(bf16[2,160,512]{2,1,0:T(8,128)(2,1)S(1)} %pad_maximum_fusion.2), channel_id=1, source_target_pairs={{0,8},{8,0},{16,24},{24,16},{32,40},{40,32},{48,56},{56,48},{64,72... | collective-permute-start | bytes 983048 | tf_op jit(solution)/shard_map/ppermute | solution.py:20
  40.8 8.2 %collective-permute-start.4 = (bf16[64,512]{1,0:T(8,128)(2,1)S(1)}, bf16[64,512]{1,0:T(8,128)(2,1)S(1)}, u32[]{:S(2)}, u32[]{:S(2)}) collective-permute-start(bf16[64,512]{1,0:T(8,128)(2,1)S(1)} %pad_maximum_fusion.4), channel_id=1, source_target_pairs={{0,96},{8,104},{16,112},{24,120},{32,64},{40,72},{48,80},{56,88},{... | collective-permute-start | bytes 196616 | tf_op jit(solution)/shard_map/ppermute | solution.py:369
  49.0 3.3 %collective-permute-done.4 = bf16[64,512]{1,0:T(8,128)(2,1)S(1)} collective-permute-done((bf16[64,512]{1,0:T(8,128)(2,1)S(1)}, bf16[64,512]{1,0:T(8,128)(2,1)S(1)}, u32[]{:S(2)}, u32[]{:S(2)}) %collective-permute-start.4) | collective-permute-done | bytes 65568 | tf_op jit(solution)/shard_map/ppermute | solution.py:369
  52.3 1.9 %collective-permute-start.5 = (bf16[64,512]{1,0:T(8,128)(2,1)S(1)}, bf16[64,512]{1,0:T(8,128)(2,1)S(1)}, u32[]{:S(2)}, u32[]{:S(2)}) collective-permute-start(bf16[64,512]{1,0:T(8,128)(2,1)S(1)} %collective-permute-done.4), channel_id=1, source_target_pairs={{0,8},{8,0},{16,24},{24,16},{32,40},{40,32},{48,56},{56,48},{64,72... | collective-permute-start | bytes 196616 | tf_op jit(solution)/shard_map/ppermute | solution.py:20
  54.3 0.0 collective-permute-done.3.c_ref
  54.3 4.3 %collective-permute-done.5 = bf16[64,512]{1,0:T(8,128)(2,1)S(1)} collective-permute-done((bf16[64,512]{1,0:T(8,128)(2,1)S(1)}, bf16[64,512]{1,0:T(8,128)(2,1)S(1)}, u32[]{:S(2)}, u32[]{:S(2)}) %collective-permute-start.5) | collective-permute-done | bytes 65568 | tf_op jit(solution)/shard_map/ppermute | solution.py:20
  58.6 2.9 %collective-permute-start.6 = (bf16[256,512]{1,0:T(8,128)(2,1)S(1)}, bf16[256,512]{1,0:T(8,128)(2,1)S(1)}, u32[]{:S(2)}, u32[]{:S(2)}) collective-permute-start(bf16[256,512]{1,0:T(8,128)(2,1)S(1)} %constant_dynamic-update-slice_fusion), channel_id=1, source_target_pairs={{0,128},{128,256},{256,384},{384,0},{1,129},{129,257},{257,385},{3... | collective-permute-start | bytes 786440 | tf_op jit(solution)/shard_map/ppermute | solution.py:25
  61.6 3.6 %collective-permute-start.7 = (bf16[256,512]{1,0:T(8,128)(2,1)S(1)}, bf16[256,512]{1,0:T(8,128)(2,1)S(1)}, u32[]{:S(2)}, u32[]{:S(2)}) collective-permute-start(bf16[256,512]{1,0:T(8,128)(2,1)S(1)} %constant_dynamic-update-slice_fusion), channel_id=1, source_target_pairs={{0,384},{128,0},{256,128},{384,256},{1,385},{129,1},{257,129},{385... | collective-permute-start | bytes 786440 | tf_op jit(solution)/shard_map/ppermute | solution.py:25
  65.1 3.0 %collective-permute-start.8 = (bf16[256,512]{1,0:T(8,128)(2,1)S(1)}, bf16[256,512]{1,0:T(8,128)(2,1)S(1)}, u32[]{:S(2)}, u32[]{:S(2)}) collective-permute-start(bf16[256,512]{1,0:T(8,128)(2,1)S(1)} %constant_dynamic-update-slice_fusion), channel_id=1, source_target_pairs={{0,256},{128,384},{256,0},{384,128},{1,257},{129,385},{257,1},{385... | collective-permute-start | bytes 786440 | tf_op jit(solution)/shard_map/ppermute | solution.py:25
  68.2 0.0 copy-start.4
  68.2 9.0 %collective-permute-start.9 = (bf16[2,320,512]{2,1,0:T(8,128)(2,1)S(1)}, bf16[2,320,512]{2,1,0:T(8,128)(2,1)S(1)}, u32[]{:S(2)}, u32[]{:S(2)}) collective-permute-start(bf16[2,320,512]{2,1,0:T(8,128)(2,1)S(1)} %pad_maximum_fusion.1), channel_id=1, source_target_pairs={{0,4},{4,0},{1,5},{5,1},{2,6},{6,2},{3,7},{7,3},{8,12},{12,8},{9,1... | collective-permute-start | bytes 1966088 | tf_op jit(solution)/shard_map/ppermute | solution.py:20
  77.2 0.0 collective-permute-done.6
  77.2 0.0 collective-permute-done.7
  77.2 0.0 collective-permute-done.8
  77.2 0.1 pad_maximum_fusion.refs_0_
  77.4 6.3 %collective-permute-start.10 = (bf16[4,256,512]{2,1,0:T(8,128)(2,1)S(1)}, bf16[4,256,512]{2,1,0:T(8,128)(2,1)}, u32[]{:S(2)}, u32[]{:S(2)}) collective-permute-start(bf16[4,256,512]{2,1,0:T(8,128)(2,1)S(1)} %pad_maximum_fusion.refs_0_), channel_id=1, source_target_pairs={{0,4},{4,0},{1,5},{5,1},{2,6},{6,2},{3,7},{7,3},{8,12},{12,8},{9,1... | collective-permute-start | bytes 3145736 | tf_op jit(solution)/shard_map/ppermute | solution.py:20
  83.6 0.0 collective-permute-done.9.d_ref
  83.6 0.0 copy-done.4
  83.6 2.4 %shard_map.48 = bf16[4,144,512]{2,1,0:T(8,128)(2,1)} custom-call(bf16[512,512]{1,0:T(8,128)(2,1)S(1)} %copy-done.4, bf16[2,24,512]{2,1,0:T(8,128)(2,1)S(1)} %collective-permute-done.1.a_ref, bf16[2,64,512]{2,1,0:T(8,128)(2,1)S(1)} %collective-permute-done.2.b_ref, bf16[2,160,512]{2,1,0:T(8,128)(2,1)S(1)} %collective-permute-done.3.c_ref, ...), custom_call_target="tpu_custom_call" | custom-call | tf_op jit(solution)/shard_map/pallas_call | solution.py:254
  86.1 0.0 all-to-all-done.refs_1_
  86.1 4.5 %all-to-all-start.1 = ((bf16[4,144,512]{2,1,0:T(8,128)(2,1)}), bf16[4,144,512]{2,1,0:T(8,128)(2,1)}, u32[]{:S(2)}, u32[]{:S(2)}) async-start(bf16[4,144,512]{2,1,0:T(8,128)(2,1)} %shard_map.48), calls=%async_computation.1 | async-start | bytes 1179648 | tf_op jit(solution)/shard_map/all_to_all | solution.py:378
  90.6 0.1 pad_add_fusion.place_ref
  90.7 0.0 collective-permute-done.10.refs_3_
  90.7 10.0 %all-to-all-done.1.refs_2_ = bf16[4,144,512]{2,1,0:T(8,128)(2,1)} async-done(((bf16[4,144,512]{2,1,0:T(8,128)(2,1)}), bf16[4,144,512]{2,1,0:T(8,128)(2,1)}, u32[]{:S(2)}, u32[]{:S(2)}) %all-to-all-start.1) | async-done | bytes 589856 | tf_op jit(solution)/shard_map/all_to_all | solution.py:378
  100.7 4.5 %shard_map.49 = bf16[512,512]{1,0:T(8,128)(2,1)} custom-call(s32[3]{0:T(128)S(1)} %pad_add_fusion.place_ref, bf16[4,256,512]{2,1,0:T(8,128)(2,1)S(1)} %pad_maximum_fusion.refs_0_, bf16[4,528,512]{2,1,0:T(8,128)(2,1)S(1)} %all-to-all-done.refs_1_, bf16[4,144,512]{2,1,0:T(8,128)(2,1)} %all-to-all-done.1.refs_2_, ...), custom_call_target="tpu_custom_call" | custom-call | tf_op jit(solution)/shard_map/pallas_call | solution.py:336
  (18 shorter events, 0.2 us)
Async XLA Ops:
  0.0 21.5 %copy-start = (bf16[512,512]{1,0:T(8,128)(2,1)S(1)}, bf16[512,512]{1,0:T(8,128)(2,1)}, u32[]{:S(2)}) copy-start(bf16[512,512]{1,0:T(8,128)(2,1)} %key_ref.3) | copy-start | bytes 1572868
  0.0 21.5 %copy-start.1 = (bf16[512,512]{1,0:T(8,128)(2,1)S(1)}, bf16[512,512]{1,0:T(8,128)(2,1)}, u32[]{:S(2)}) copy-start(bf16[512,512]{1,0:T(8,128)(2,1)} %value_ref.3) | copy-start | bytes 1572868
  0.0 21.6 %copy-start.2 = (bf16[512,512]{1,0:T(8,128)(2,1)S(1)}, bf16[512,512]{1,0:T(8,128)(2,1)}, u32[]{:S(2)}) copy-start(bf16[512,512]{1,0:T(8,128)(2,1)} %query_ref.1) | copy-start | bytes 1572868
  0.0 4.3 %collective-permute-start = (bf16[16,512]{1,0:T(8,128)(2,1)}, bf16[16,512]{1,0:T(8,128)(2,1)S(1)}, u32[]{:S(2)}, u32[]{:S(2)}) collective-permute-start(bf16[16,512]{1,0:T(8,128)(2,1)} %bitcast.27), channel_id=1, source_target_pairs={{0,0},{1,128},{2,256},{3,384},{128,1},{129,129},{130,257},{131,385... | collective-permute-start | bytes 49160 | tf_op jit(solution)/shard_map/ppermute | solution.py:360
  4.3 11.1 %collective-permute-start.1 = (bf16[2,24,512]{2,1,0:T(8,128)(2,1)S(1)}, bf16[2,24,512]{2,1,0:T(8,128)(2,1)S(1)}, u32[]{:S(2)}, u32[]{:S(2)}) collective-permute-start(bf16[2,24,512]{2,1,0:T(8,128)(2,1)S(1)} %pad_maximum_fusion.5), channel_id=1, source_target_pairs={{0,32},{8,40},{16,48},{24,56},{32,0},{40,8},{48,16},{56,24},{64,96... | collective-permute-start | bytes 147464 | tf_op jit(solution)/shard_map/ppermute | solution.py:20
  15.5 21.7 %collective-permute-start.2 = (bf16[2,64,512]{2,1,0:T(8,128)(2,1)S(1)}, bf16[2,64,512]{2,1,0:T(8,128)(2,1)S(1)}, u32[]{:S(2)}, u32[]{:S(2)}) collective-permute-start(bf16[2,64,512]{2,1,0:T(8,128)(2,1)S(1)} %pad_maximum_fusion.3), channel_id=1, source_target_pairs={{0,16},{8,24},{16,0},{24,8},{32,48},{40,56},{48,32},{56,40},{64,80... | collective-permute-start | bytes 393224 | tf_op jit(solution)/shard_map/ppermute | solution.py:20
  29.1 0.8 copy-start.3
  29.9 56.2 %all-to-all-start = ((bf16[4,528,512]{2,1,0:T(8,128)(2,1)}), bf16[4,528,512]{2,1,0:T(8,128)(2,1)S(1)}, u32[]{:S(2)}, u32[]{:S(2)}) async-start(bf16[4,528,512]{2,1,0:T(8,128)(2,1)} %get-tuple-element.18), calls=%async_computation | async-start | bytes 4325376 | tf_op jit(solution)/shard_map/all_to_all | solution.py:367
  37.2 17.0 %collective-permute-start.3 = (bf16[2,160,512]{2,1,0:T(8,128)(2,1)S(1)}, bf16[2,160,512]{2,1,0:T(8,128)(2,1)S(1)}, u32[]{:S(2)}, u32[]{:S(2)}) collective-permute-start(bf16[2,160,512]{2,1,0:T(8,128)(2,1)S(1)} %pad_maximum_fusion.2), channel_id=1, source_target_pairs={{0,8},{8,0},{16,24},{24,16},{32,40},{40,32},{48,56},{56,48},{64,72... | collective-permute-start | bytes 983048 | tf_op jit(solution)/shard_map/ppermute | solution.py:20
  40.8 11.5 %collective-permute-start.4 = (bf16[64,512]{1,0:T(8,128)(2,1)S(1)}, bf16[64,512]{1,0:T(8,128)(2,1)S(1)}, u32[]{:S(2)}, u32[]{:S(2)}) collective-permute-start(bf16[64,512]{1,0:T(8,128)(2,1)S(1)} %pad_maximum_fusion.4), channel_id=1, source_target_pairs={{0,96},{8,104},{16,112},{24,120},{32,64},{40,72},{48,80},{56,88},{... | collective-permute-start | bytes 196616 | tf_op jit(solution)/shard_map/ppermute | solution.py:369
  52.3 6.3 %collective-permute-start.5 = (bf16[64,512]{1,0:T(8,128)(2,1)S(1)}, bf16[64,512]{1,0:T(8,128)(2,1)S(1)}, u32[]{:S(2)}, u32[]{:S(2)}) collective-permute-start(bf16[64,512]{1,0:T(8,128)(2,1)S(1)} %collective-permute-done.4), channel_id=1, source_target_pairs={{0,8},{8,0},{16,24},{24,16},{32,40},{40,32},{48,56},{56,48},{64,72... | collective-permute-start | bytes 196616 | tf_op jit(solution)/shard_map/ppermute | solution.py:20
  58.6 18.6 %collective-permute-start.6 = (bf16[256,512]{1,0:T(8,128)(2,1)S(1)}, bf16[256,512]{1,0:T(8,128)(2,1)S(1)}, u32[]{:S(2)}, u32[]{:S(2)}) collective-permute-start(bf16[256,512]{1,0:T(8,128)(2,1)S(1)} %constant_dynamic-update-slice_fusion), channel_id=1, source_target_pairs={{0,128},{128,256},{256,384},{384,0},{1,129},{129,257},{257,385},{3... | collective-permute-start | bytes 786440 | tf_op jit(solution)/shard_map/ppermute | solution.py:25
  61.6 15.6 %collective-permute-start.7 = (bf16[256,512]{1,0:T(8,128)(2,1)S(1)}, bf16[256,512]{1,0:T(8,128)(2,1)S(1)}, u32[]{:S(2)}, u32[]{:S(2)}) collective-permute-start(bf16[256,512]{1,0:T(8,128)(2,1)S(1)} %constant_dynamic-update-slice_fusion), channel_id=1, source_target_pairs={{0,384},{128,0},{256,128},{384,256},{1,385},{129,1},{257,129},{385... | collective-permute-start | bytes 786440 | tf_op jit(solution)/shard_map/ppermute | solution.py:25
  65.1 12.1 %collective-permute-start.8 = (bf16[256,512]{1,0:T(8,128)(2,1)S(1)}, bf16[256,512]{1,0:T(8,128)(2,1)S(1)}, u32[]{:S(2)}, u32[]{:S(2)}) collective-permute-start(bf16[256,512]{1,0:T(8,128)(2,1)S(1)} %constant_dynamic-update-slice_fusion), channel_id=1, source_target_pairs={{0,256},{128,384},{256,0},{384,128},{1,257},{129,385},{257,1},{385... | collective-permute-start | bytes 786440 | tf_op jit(solution)/shard_map/ppermute | solution.py:25
  68.2 15.5 %copy-start.4 = (bf16[512,512]{1,0:T(8,128)(2,1)S(1)}, bf16[512,512]{1,0:T(8,128)(2,1)}, u32[]{:S(2)}) copy-start(bf16[512,512]{1,0:T(8,128)(2,1)} %copy-done.3) | copy-start | bytes 1572868
  68.2 15.4 %collective-permute-start.9 = (bf16[2,320,512]{2,1,0:T(8,128)(2,1)S(1)}, bf16[2,320,512]{2,1,0:T(8,128)(2,1)S(1)}, u32[]{:S(2)}, u32[]{:S(2)}) collective-permute-start(bf16[2,320,512]{2,1,0:T(8,128)(2,1)S(1)} %pad_maximum_fusion.1), channel_id=1, source_target_pairs={{0,4},{4,0},{1,5},{5,1},{2,6},{6,2},{3,7},{7,3},{8,12},{12,8},{9,1... | collective-permute-start | bytes 1966088 | tf_op jit(solution)/shard_map/ppermute | solution.py:20
  77.4 13.3 %collective-permute-start.10 = (bf16[4,256,512]{2,1,0:T(8,128)(2,1)S(1)}, bf16[4,256,512]{2,1,0:T(8,128)(2,1)}, u32[]{:S(2)}, u32[]{:S(2)}) collective-permute-start(bf16[4,256,512]{2,1,0:T(8,128)(2,1)S(1)} %pad_maximum_fusion.refs_0_), channel_id=1, source_target_pairs={{0,4},{4,0},{1,5},{5,1},{2,6},{6,2},{3,7},{7,3},{8,12},{12,8},{9,1... | collective-permute-start | bytes 3145736 | tf_op jit(solution)/shard_map/ppermute | solution.py:20
  86.1 14.6 %all-to-all-start.1 = ((bf16[4,144,512]{2,1,0:T(8,128)(2,1)}), bf16[4,144,512]{2,1,0:T(8,128)(2,1)}, u32[]{:S(2)}, u32[]{:S(2)}) async-start(bf16[4,144,512]{2,1,0:T(8,128)(2,1)} %shard_map.48), calls=%async_computation.1 | async-start | bytes 1179648 | tf_op jit(solution)/shard_map/all_to_all | solution.py:378

commit v7 on v6

--- a/solution.py
+++ b/solution.py
@@ -106,9 +106,11 @@
     return jnp.dot(choice, value, preferred_element_type=jnp.float32).astype(jnp.bfloat16)
 
 
-def near_head(queries, keys, values):
+def near_head(fetch, keys, values):
     half = 2 * BLOCK
-    q1, k1, v1 = pool(queries, 0.5), pool(keys, 0.5), pool(values, 1.0)
+    k1, v1 = pool(keys, 0.5), pool(values, 1.0)
+    queries = fetch()
+    q1 = pool(queries, 0.5)
     level = pool(q1, 0.5)
     coarse = [level]
     for factor in (2, 4, 8):
@@ -136,12 +138,29 @@
     )
 
 
-def near_kernel(query_ref, key_ref, value_ref, out_ref, coarse_ref, held_ref, sems):
+def near_kernel(
+    query_ref, key_ref, value_ref, out_ref, coarse_ref, held_ref, sems, query_held, query_sems
+):
     rows = query_ref.shape[0]
+    columns = [
+        slice(start, start + HEAD_DIM) for start in range(0, query_ref.shape[1], HEAD_DIM)
+    ]
+    loads = [
+        pltpu.make_async_copy(
+            query_ref.at[:, lanes], query_held.at[:, lanes], query_sems.at[head]
+        )
+        for head, lanes in enumerate(columns)
+    ]
+    for load in loads:
+        load.start()
     sends = []
-    for head in range(query_ref.shape[1] // HEAD_DIM):
-        lanes = slice(head * HEAD_DIM, (head + 1) * HEAD_DIM)
-        mean, tile, coarse = near_head(query_ref[:, lanes], key_ref[:, lanes], value_ref[:, lanes])
+    for head, lanes in enumerate(columns):
+
+        def fetch():
+            loads[head].wait()
+            return query_held[:, lanes]
+
+        mean, tile, coarse = near_head(fetch, key_ref[:, lanes], value_ref[:, lanes])
         coarse_ref[:, lanes] = coarse
         held_ref[:rows, lanes] = mean
         held_ref[rows:, lanes] = tile
@@ -233,6 +252,7 @@
     return pl.pallas_call(
         near_kernel,
         compiler_params=VMEM_LIMIT,
+        in_specs=[pl.BlockSpec(memory_space=pl.ANY)] + [pl.BlockSpec(memory_space=pltpu.VMEM)] * 2,
         out_specs=[pl.BlockSpec(memory_space=pl.ANY), pl.BlockSpec(memory_space=pltpu.VMEM)],
         out_shape=[
             pltpu.HBM((copies, rows + 16, width), jnp.bfloat16),
@@ -241,8 +261,10 @@
         scratch_shapes=[
             pltpu.VMEM((rows + 16, width), jnp.bfloat16),
             pltpu.SemaphoreType.DMA((width // HEAD_DIM, copies)),
+            pltpu.VMEM((rows, width), jnp.bfloat16),
+            pltpu.SemaphoreType.DMA((width // HEAD_DIM,)),
         ],
-    )(queries, keys, values)
+    )(pltpu.with_memory_space_constraint(queries, pltpu.HBM), keys, values)
 
 
 def in_vmem(value):
@@ -283,12 +305,10 @@
     return jnp.dot(total.astype(jnp.bfloat16), choice, preferred_element_type=jnp.float32)
 
 
-def mix_kernel(place_ref, *refs):
-    own_ref, near_ref, far_ref, other_ref, out_ref, attended_ref = refs
-    groups = own_ref.shape[0]
-    z, core, y = (place_ref[i] for i in range(3))
-    width = near_ref.shape[2]
-    rows, coarse_rows = out_ref.shape[0], BLOCK
+def blend_kernel(place_ref, near_ref, far_ref, attended_ref):
+    groups, width = near_ref.shape[0], near_ref.shape[2]
+    y = place_ref[2]
+    rows, coarse_rows = attended_ref.shape[0], BLOCK
     tiles, ratio = rows // BLOCK, rows // coarse_rows
     heads = width // HEAD_DIM
     depth = BLOCK // ratio
@@ -322,24 +342,25 @@
                 attended_ref[at, start : start + piece] = (far + share * (near - far)).astype(
                     jnp.bfloat16
                 )
+
+
+def mix_kernel(place_ref, attended_ref, own_ref, other_ref, out_ref):
     weights = [
-        jnp.concatenate([own_ref[i], other_ref[i]], axis=0) for i in range(groups)
+        jnp.concatenate([own_ref[i], other_ref[i]], axis=0) for i in range(own_ref.shape[0])
     ]
     total = times(attended_ref[...], jnp.concatenate(weights, axis=1))
-    out_ref[...] = placed(total, z, core).astype(jnp.bfloat16)
-
-
-def mix_part(place, own, near, far, other):
-    groups, rows, width = near.shape
-    rows = rows - 16
+    out_ref[...] = placed(total, place_ref[0], place_ref[1]).astype(jnp.bfloat16)
+
+
+def on_chip(kernel, out_shape, place, *operands):
     vmem = pl.BlockSpec(memory_space=pltpu.VMEM)
     return pl.pallas_call(
-        mix_kernel,
+        kernel,
         compiler_params=VMEM_LIMIT,
-        in_specs=[pl.BlockSpec(memory_space=pltpu.SMEM)] + [vmem] * 4,
-        out_shape=shape((rows, 2 * own.shape[1])),
-        scratch_shapes=[pltpu.VMEM((rows, groups * width), jnp.bfloat16)],
-    )(place, *map(in_vmem, (own, near, far, other)))
+        in_specs=[pl.BlockSpec(memory_space=pltpu.SMEM)] + [vmem] * len(operands),
+        out_specs=vmem,
+        out_shape=out_shape,
+    )(place, *map(in_vmem, operands))
 
 
 def body(queries, key_vectors, values, out_weight):
@@ -379,7 +400,11 @@
     own = jnp.stack(own)
     other = swap(own, "core", 1)
     place = jnp.stack([lax.axis_index(name) for name in ("z", "core", "y")]).astype(jnp.int32)
-    return mix_part(place, own, near, far, other)
+    groups, rows, width = near.shape
+    attended = pltpu.VMEM((rows - 16, groups * width), jnp.bfloat16)
+    attended = on_chip(blend_kernel, attended, place, near, far)
+    mixed = shape((rows - 16, 2 * own.shape[1]))
+    return on_chip(mix_kernel, mixed, place, attended, own, other)
 
 
 def solution(mesh):

time: 106 us -> 110 us (1.038)
  Pallas kernels: 17.2 us -> 20.6 us
    pallas_call x2 -> x3, Pallas kernels: 12 us -> 15.4 us  [the longest x1 9.22 us: near_part(): pl.pallas_call(near_kernel, compiler_params=VMEM_LIMIT, in_specs=[pl.Bloc...]
  transfers between devices with their start and end apart: 13 -> 13, of which waited for: 4 -> 4; matrix products, arithmetic and copies ran while one was open for 0% -> 0% of each run, Pallas kernels for 12% -> 16%
where the time goes in v7:
time: 110 us; the launch traced here: 109 us
  starting transfers between devices  67.8 us (62%)
  Pallas kernels  20.6 us (19%)
  waiting for transfers between devices  19.1 us (17%)
    ppermute x6, starting transfers between devices, swap(): lax.ppermute(value, axis, [(s, s ^ mask) for s in range(lax.axis_size(axi...  36.9 us
    all_to_all x1, waiting for transfers between devices, body(): far = lax.all_to_all(far, 'head', 0, 0)  10 us
    ppermute x3, starting transfers between devices, shift(): lax.ppermute(value, axis, [(s, (s + step) % size) for s in range(size)])  9.43 us
    pallas_call x1, Pallas kernels, near_part(): pl.pallas_call(near_kernel, compiler_params=VMEM_LIMIT, in_specs=[pl.Bloc...  9.22 us
    ppermute x1, starting transfers between devices, body(): w_across = lax.ppermute(weights, 'z', [(z, across(z)) for z in range(ring)])  8.22 us
    all_to_all x1, starting transfers between devices, body(): near = lax.all_to_all(near, 'head', 0, 0)  7.26 us
    pallas_call x2, Pallas kernels, on_chip(): pl.pallas_call(kernel, compiler_params=VMEM_LIMIT, in_specs=[pl.BlockSpec...  6.18 us
    ppermute x6, waiting for transfers between devices, swap(): lax.ppermute(value, axis, [(s, s ^ mask) for s in range(lax.axis_size(axi...  5.8 us
  transfers between devices with their start and end apart: 13, of which 4 were waited for; matrix products, arithmetic and copies ran while one was open for 0% of the time, Pallas kernels for 16%

profile of v7, /device:TPU:1, one launch (start us, length us, event | category | flops | bytes accessed | tf_op | source)
XLA Modules:
  0.0 109.0 jit_solution(11676441764210389474)
XLA Ops:
  0.0 0.0 copy-start
  0.0 0.0 copy-start.1
  0.0 1.5 %collective-permute-start = (bf16[16,512]{1,0:T(8,128)(2,1)}, bf16[16,512]{1,0:T(8,128)(2,1)S(1)}, u32[]{:S(2)}, u32[]{:S(2)}) collective-permute-start(bf16[16,512]{1,0:T(8,128)(2,1)} %bitcast.27), channel_id=1, source_target_pairs={{0,0},{1,128},{2,256},{3,384},{128,1},{129,129},{130,257},{131,385... | collective-permute-start | bytes 49160 | tf_op jit(solution)/shard_map/ppermute | solution.py:381
  1.5 2.8 %shard_map.47 = (bf16[2,128,512]{2,1,0:T(8,128)(2,1)S(1)}, bf16[2,64,512]{2,1,0:T(8,128)(2,1)S(1)}, bf16[2,32,512]{2,1,0:T(8,128)(2,1)S(1)}, bf16[2,16,512]{2,1,0:T(8,128)(2,1)S(1)}) custom-call(bf16[512,512]{1,0:T(8,128)(2,1)} %key_ref.3, bf16[512,512]{1,0:T(8,128)(2,1)} %value_ref.3), custom_call_target="tpu_custom_call" | custom-call | tf_op jit(solution)/shard_map/pallas_call | solution.py:238
  4.3 0.0 collective-permute-done
  4.3 9.6 %collective-permute-start.1 = (bf16[2,24,512]{2,1,0:T(8,128)(2,1)S(1)}, bf16[2,24,512]{2,1,0:T(8,128)(2,1)S(1)}, u32[]{:S(2)}, u32[]{:S(2)}) collective-permute-start(bf16[2,24,512]{2,1,0:T(8,128)(2,1)S(1)} %pad_maximum_fusion.5), channel_id=1, source_target_pairs={{0,32},{8,40},{16,48},{24,56},{32,0},{40,8},{48,16},{56,24},{64,96... | collective-permute-start | bytes 147464 | tf_op jit(solution)/shard_map/ppermute | solution.py:20
  13.9 1.5 %collective-permute-done.1.a_ref = bf16[2,24,512]{2,1,0:T(8,128)(2,1)S(1)} collective-permute-done((bf16[2,24,512]{2,1,0:T(8,128)(2,1)S(1)}, bf16[2,24,512]{2,1,0:T(8,128)(2,1)S(1)}, u32[]{:S(2)}, u32[]{:S(2)}) %collective-permute-start.1) | collective-permute-done | bytes 49184 | tf_op jit(solution)/shard_map/ppermute | solution.py:20
  15.4 6.1 %collective-permute-start.2 = (bf16[2,64,512]{2,1,0:T(8,128)(2,1)S(1)}, bf16[2,64,512]{2,1,0:T(8,128)(2,1)S(1)}, u32[]{:S(2)}, u32[]{:S(2)}) collective-permute-start(bf16[2,64,512]{2,1,0:T(8,128)(2,1)S(1)} %pad_maximum_fusion.3), channel_id=1, source_target_pairs={{0,16},{8,24},{16,0},{24,8},{32,48},{40,56},{48,32},{56,40},{64,80... | collective-permute-start | bytes 393224 | tf_op jit(solution)/shard_map/ppermute | solution.py:20
  21.5 0.0 copy-done
  21.5 0.0 copy-done.1
  21.5 9.2 %shard_map.46 = (bf16[4,528,512]{2,1,0:T(8,128)(2,1)}, bf16[512,512]{1,0:T(8,128)(2,1)S(1)}) custom-call(bf16[512,512]{1,0:T(8,128)(2,1)} %query_ref.1, bf16[512,512]{1,0:T(8,128)(2,1)S(1)} %copy-done, bf16[512,512]{1,0:T(8,128)(2,1)S(1)} %copy-done.1), custom_call_target="tpu_custom_call" | custom-call | tf_op jit(solution)/shard_map/pallas_call | solution.py:252
  30.8 0.0 copy-start.2
  30.8 0.8 copy-done.2
  31.6 7.3 %all-to-all-start = ((bf16[4,528,512]{2,1,0:T(8,128)(2,1)}), bf16[4,528,512]{2,1,0:T(8,128)(2,1)S(1)}, u32[]{:S(2)}, u32[]{:S(2)}) async-start(bf16[4,528,512]{2,1,0:T(8,128)(2,1)} %get-tuple-element.18), calls=%async_computation | async-start | bytes 4325376 | tf_op jit(solution)/shard_map/all_to_all | solution.py:388
  38.8 0.0 collective-permute-done.2.b_ref
  38.9 3.6 %collective-permute-start.3 = (bf16[2,160,512]{2,1,0:T(8,128)(2,1)S(1)}, bf16[2,160,512]{2,1,0:T(8,128)(2,1)S(1)}, u32[]{:S(2)}, u32[]{:S(2)}) collective-permute-start(bf16[2,160,512]{2,1,0:T(8,128)(2,1)S(1)} %pad_maximum_fusion.2), channel_id=1, source_target_pairs={{0,8},{8,0},{16,24},{24,16},{32,40},{40,32},{48,56},{56,48},{64,72... | collective-permute-start | bytes 983048 | tf_op jit(solution)/shard_map/ppermute | solution.py:20
  42.5 8.2 %collective-permute-start.5 = (bf16[64,512]{1,0:T(8,128)(2,1)S(1)}, bf16[64,512]{1,0:T(8,128)(2,1)S(1)}, u32[]{:S(2)}, u32[]{:S(2)}) collective-permute-start(bf16[64,512]{1,0:T(8,128)(2,1)S(1)} %pad_maximum_fusion.4), channel_id=1, source_target_pairs={{0,96},{8,104},{16,112},{24,120},{32,64},{40,72},{48,80},{56,88},{... | collective-permute-start | bytes 196616 | tf_op jit(solution)/shard_map/ppermute | solution.py:390
  50.7 3.3 %collective-permute-done.5 = bf16[64,512]{1,0:T(8,128)(2,1)S(1)} collective-permute-done((bf16[64,512]{1,0:T(8,128)(2,1)S(1)}, bf16[64,512]{1,0:T(8,128)(2,1)S(1)}, u32[]{:S(2)}, u32[]{:S(2)}) %collective-permute-start.5) | collective-permute-done | bytes 65568 | tf_op jit(solution)/shard_map/ppermute | solution.py:390
  54.0 1.9 %collective-permute-start.6 = (bf16[64,512]{1,0:T(8,128)(2,1)S(1)}, bf16[64,512]{1,0:T(8,128)(2,1)S(1)}, u32[]{:S(2)}, u32[]{:S(2)}) collective-permute-start(bf16[64,512]{1,0:T(8,128)(2,1)S(1)} %collective-permute-done.5), channel_id=1, source_target_pairs={{0,8},{8,0},{16,24},{24,16},{32,40},{40,32},{48,56},{56,48},{64,72... | collective-permute-start | bytes 196616 | tf_op jit(solution)/shard_map/ppermute | solution.py:20
  55.9 0.0 collective-permute-done.3.c_ref
  56.0 4.3 %collective-permute-done.6 = bf16[64,512]{1,0:T(8,128)(2,1)S(1)} collective-permute-done((bf16[64,512]{1,0:T(8,128)(2,1)S(1)}, bf16[64,512]{1,0:T(8,128)(2,1)S(1)}, u32[]{:S(2)}, u32[]{:S(2)}) %collective-permute-start.6) | collective-permute-done | bytes 65568 | tf_op jit(solution)/shard_map/ppermute | solution.py:20
  60.3 4.2 %collective-permute-start.9 = (bf16[256,512]{1,0:T(8,128)(2,1)S(1)}, bf16[256,512]{1,0:T(8,128)(2,1)S(1)}, u32[]{:S(2)}, u32[]{:S(2)}) collective-permute-start(bf16[256,512]{1,0:T(8,128)(2,1)S(1)} %constant_dynamic-update-slice_fusion), channel_id=1, source_target_pairs={{0,256},{128,384},{256,0},{384,128},{1,257},{129,385},{257,1},{385... | collective-permute-start | bytes 786440 | tf_op jit(solution)/shard_map/ppermute | solution.py:25
  64.5 3.1 %collective-permute-start.8 = (bf16[256,512]{1,0:T(8,128)(2,1)S(1)}, bf16[256,512]{1,0:T(8,128)(2,1)S(1)}, u32[]{:S(2)}, u32[]{:S(2)}) collective-permute-start(bf16[256,512]{1,0:T(8,128)(2,1)S(1)} %constant_dynamic-update-slice_fusion), channel_id=1, source_target_pairs={{0,384},{128,0},{256,128},{384,256},{1,385},{129,1},{257,129},{385... | collective-permute-start | bytes 786440 | tf_op jit(solution)/shard_map/ppermute | solution.py:25
  67.6 2.2 %collective-permute-start.7 = (bf16[256,512]{1,0:T(8,128)(2,1)S(1)}, bf16[256,512]{1,0:T(8,128)(2,1)S(1)}, u32[]{:S(2)}, u32[]{:S(2)}) collective-permute-start(bf16[256,512]{1,0:T(8,128)(2,1)S(1)} %constant_dynamic-update-slice_fusion), channel_id=1, source_target_pairs={{0,128},{128,256},{256,384},{384,0},{1,129},{129,257},{257,385},{3... | collective-permute-start | bytes 786440 | tf_op jit(solution)/shard_map/ppermute | solution.py:25
  69.8 0.0 copy-start.3
  69.9 9.0 %collective-permute-start.4 = (bf16[2,320,512]{2,1,0:T(8,128)(2,1)S(1)}, bf16[2,320,512]{2,1,0:T(8,128)(2,1)S(1)}, u32[]{:S(2)}, u32[]{:S(2)}) collective-permute-start(bf16[2,320,512]{2,1,0:T(8,128)(2,1)S(1)} %pad_maximum_fusion.1), channel_id=1, source_target_pairs={{0,4},{4,0},{1,5},{5,1},{2,6},{6,2},{3,7},{7,3},{8,12},{12,8},{9,1... | collective-permute-start | bytes 1966088 | tf_op jit(solution)/shard_map/ppermute | solution.py:20
  78.9 0.0 collective-permute-done.9
  78.9 0.0 collective-permute-done.8
  78.9 0.0 collective-permute-done.7
  78.9 0.1 pad_maximum_fusion.own_ref
  79.0 6.7 %collective-permute-start.10 = (bf16[4,256,512]{2,1,0:T(8,128)(2,1)S(1)}, bf16[4,256,512]{2,1,0:T(8,128)(2,1)}, u32[]{:S(2)}, u32[]{:S(2)}) collective-permute-start(bf16[4,256,512]{2,1,0:T(8,128)(2,1)S(1)} %pad_maximum_fusion.own_ref), channel_id=1, source_target_pairs={{0,4},{4,0},{1,5},{5,1},{2,6},{6,2},{3,7},{7,3},{8,12},{12,8},{9,1... | collective-permute-start | bytes 3145736 | tf_op jit(solution)/shard_map/ppermute | solution.py:20
  85.8 0.0 collective-permute-done.4.d_ref
  85.8 0.0 copy-done.3
  85.8 2.5 %shard_map.48 = bf16[4,144,512]{2,1,0:T(8,128)(2,1)} custom-call(bf16[512,512]{1,0:T(8,128)(2,1)S(1)} %copy-done.3, bf16[2,24,512]{2,1,0:T(8,128)(2,1)S(1)} %collective-permute-done.1.a_ref, bf16[2,64,512]{2,1,0:T(8,128)(2,1)S(1)} %collective-permute-done.2.b_ref, bf16[2,160,512]{2,1,0:T(8,128)(2,1)S(1)} %collective-permute-done.3.c_ref, ...), custom_call_target="tpu_custom_call" | custom-call | tf_op jit(solution)/shard_map/pallas_call | solution.py:276
  88.2 0.0 all-to-all-done.near_ref
  88.2 4.5 %all-to-all-start.1 = ((bf16[4,144,512]{2,1,0:T(8,128)(2,1)}), bf16[4,144,512]{2,1,0:T(8,128)(2,1)}, u32[]{:S(2)}, u32[]{:S(2)}) async-start(bf16[4,144,512]{2,1,0:T(8,128)(2,1)} %shard_map.48), calls=%async_computation.1 | async-start | bytes 1179648 | tf_op jit(solution)/shard_map/all_to_all | solution.py:399
  92.7 0.1 pad_add_fusion.place_ref
  92.8 10.0 %all-to-all-done.1.far_ref = bf16[4,144,512]{2,1,0:T(8,128)(2,1)} async-done(((bf16[4,144,512]{2,1,0:T(8,128)(2,1)}), bf16[4,144,512]{2,1,0:T(8,128)(2,1)}, u32[]{:S(2)}, u32[]{:S(2)}) %all-to-all-start.1) | async-done | bytes 589856 | tf_op jit(solution)/shard_map/all_to_all | solution.py:399
  102.8 2.5 %shard_map.49.attended_ref = bf16[512,2048]{1,0:T(8,128)(2,1)S(1)} custom-call(s32[3]{0:T(128)S(1)} %pad_add_fusion.place_ref, bf16[4,528,512]{2,1,0:T(8,128)(2,1)S(1)} %all-to-all-done.near_ref, bf16[4,144,512]{2,1,0:T(8,128)(2,1)} %all-to-all-done.1.far_ref), custom_call_target="tpu_custom_call" | custom-call | tf_op jit(solution)/shard_map/pallas_call | solution.py:357
  105.4 0.0 collective-permute-done.10.other_ref
  105.4 3.6 %shard_map.50 = bf16[512,512]{1,0:T(8,128)(2,1)} custom-call(s32[3]{0:T(128)S(1)} %pad_add_fusion.place_ref, bf16[512,2048]{1,0:T(8,128)(2,1)S(1)} %shard_map.49.attended_ref, bf16[4,256,512]{2,1,0:T(8,128)(2,1)S(1)} %pad_maximum_fusion.own_ref, bf16[4,256,512]{2,1,0:T(8,128)(2,1)} %collective-permute-done.10.other_ref), custom_call_target="tpu_custom_call" | custom-call | tf_op jit(solution)/shard_map/pallas_call | solution.py:357
  (18 shorter events, 0.2 us)
Async XLA Ops:
  0.0 21.5 %copy-start = (bf16[512,512]{1,0:T(8,128)(2,1)S(1)}, bf16[512,512]{1,0:T(8,128)(2,1)}, u32[]{:S(2)}) copy-start(bf16[512,512]{1,0:T(8,128)(2,1)} %key_ref.3) | copy-start | bytes 1572868
  0.0 21.5 %copy-start.1 = (bf16[512,512]{1,0:T(8,128)(2,1)S(1)}, bf16[512,512]{1,0:T(8,128)(2,1)}, u32[]{:S(2)}) copy-start(bf16[512,512]{1,0:T(8,128)(2,1)} %value_ref.3) | copy-start | bytes 1572868
  0.0 4.3 %collective-permute-start = (bf16[16,512]{1,0:T(8,128)(2,1)}, bf16[16,512]{1,0:T(8,128)(2,1)S(1)}, u32[]{:S(2)}, u32[]{:S(2)}) collective-permute-start(bf16[16,512]{1,0:T(8,128)(2,1)} %bitcast.27), channel_id=1, source_target_pairs={{0,0},{1,128},{2,256},{3,384},{128,1},{129,129},{130,257},{131,385... | collective-permute-start | bytes 49160 | tf_op jit(solution)/shard_map/ppermute | solution.py:381
  4.3 11.1 %collective-permute-start.1 = (bf16[2,24,512]{2,1,0:T(8,128)(2,1)S(1)}, bf16[2,24,512]{2,1,0:T(8,128)(2,1)S(1)}, u32[]{:S(2)}, u32[]{:S(2)}) collective-permute-start(bf16[2,24,512]{2,1,0:T(8,128)(2,1)S(1)} %pad_maximum_fusion.5), channel_id=1, source_target_pairs={{0,32},{8,40},{16,48},{24,56},{32,0},{40,8},{48,16},{56,24},{64,96... | collective-permute-start | bytes 147464 | tf_op jit(solution)/shard_map/ppermute | solution.py:20
  15.4 23.4 %collective-permute-start.2 = (bf16[2,64,512]{2,1,0:T(8,128)(2,1)S(1)}, bf16[2,64,512]{2,1,0:T(8,128)(2,1)S(1)}, u32[]{:S(2)}, u32[]{:S(2)}) collective-permute-start(bf16[2,64,512]{2,1,0:T(8,128)(2,1)S(1)} %pad_maximum_fusion.3), channel_id=1, source_target_pairs={{0,16},{8,24},{16,0},{24,8},{32,48},{40,56},{48,32},{56,40},{64,80... | collective-permute-start | bytes 393224 | tf_op jit(solution)/shard_map/ppermute | solution.py:20
  30.8 0.8 copy-start.2
  31.6 56.7 %all-to-all-start = ((bf16[4,528,512]{2,1,0:T(8,128)(2,1)}), bf16[4,528,512]{2,1,0:T(8,128)(2,1)S(1)}, u32[]{:S(2)}, u32[]{:S(2)}) async-start(bf16[4,528,512]{2,1,0:T(8,128)(2,1)} %get-tuple-element.18), calls=%async_computation | async-start | bytes 4325376 | tf_op jit(solution)/shard_map/all_to_all | solution.py:388
  38.9 17.0 %collective-permute-start.3 = (bf16[2,160,512]{2,1,0:T(8,128)(2,1)S(1)}, bf16[2,160,512]{2,1,0:T(8,128)(2,1)S(1)}, u32[]{:S(2)}, u32[]{:S(2)}) collective-permute-start(bf16[2,160,512]{2,1,0:T(8,128)(2,1)S(1)} %pad_maximum_fusion.2), channel_id=1, source_target_pairs={{0,8},{8,0},{16,24},{24,16},{32,40},{40,32},{48,56},{56,48},{64,72... | collective-permute-start | bytes 983048 | tf_op jit(solution)/shard_map/ppermute | solution.py:20
  42.5 11.5 %collective-permute-start.5 = (bf16[64,512]{1,0:T(8,128)(2,1)S(1)}, bf16[64,512]{1,0:T(8,128)(2,1)S(1)}, u32[]{:S(2)}, u32[]{:S(2)}) collective-permute-start(bf16[64,512]{1,0:T(8,128)(2,1)S(1)} %pad_maximum_fusion.4), channel_id=1, source_target_pairs={{0,96},{8,104},{16,112},{24,120},{32,64},{40,72},{48,80},{56,88},{... | collective-permute-start | bytes 196616 | tf_op jit(solution)/shard_map/ppermute | solution.py:390
  54.0 6.3 %collective-permute-start.6 = (bf16[64,512]{1,0:T(8,128)(2,1)S(1)}, bf16[64,512]{1,0:T(8,128)(2,1)S(1)}, u32[]{:S(2)}, u32[]{:S(2)}) collective-permute-start(bf16[64,512]{1,0:T(8,128)(2,1)S(1)} %collective-permute-done.5), channel_id=1, source_target_pairs={{0,8},{8,0},{16,24},{24,16},{32,40},{40,32},{48,56},{56,48},{64,72... | collective-permute-start | bytes 196616 | tf_op jit(solution)/shard_map/ppermute | solution.py:20
  60.3 18.6 %collective-permute-start.9 = (bf16[256,512]{1,0:T(8,128)(2,1)S(1)}, bf16[256,512]{1,0:T(8,128)(2,1)S(1)}, u32[]{:S(2)}, u32[]{:S(2)}) collective-permute-start(bf16[256,512]{1,0:T(8,128)(2,1)S(1)} %constant_dynamic-update-slice_fusion), channel_id=1, source_target_pairs={{0,256},{128,384},{256,0},{384,128},{1,257},{129,385},{257,1},{385... | collective-permute-start | bytes 786440 | tf_op jit(solution)/shard_map/ppermute | solution.py:25
  64.5 14.4 %collective-permute-start.8 = (bf16[256,512]{1,0:T(8,128)(2,1)S(1)}, bf16[256,512]{1,0:T(8,128)(2,1)S(1)}, u32[]{:S(2)}, u32[]{:S(2)}) collective-permute-start(bf16[256,512]{1,0:T(8,128)(2,1)S(1)} %constant_dynamic-update-slice_fusion), channel_id=1, source_target_pairs={{0,384},{128,0},{256,128},{384,256},{1,385},{129,1},{257,129},{385... | collective-permute-start | bytes 786440 | tf_op jit(solution)/shard_map/ppermute | solution.py:25
  67.6 11.3 %collective-permute-start.7 = (bf16[256,512]{1,0:T(8,128)(2,1)S(1)}, bf16[256,512]{1,0:T(8,128)(2,1)S(1)}, u32[]{:S(2)}, u32[]{:S(2)}) collective-permute-start(bf16[256,512]{1,0:T(8,128)(2,1)S(1)} %constant_dynamic-update-slice_fusion), channel_id=1, source_target_pairs={{0,128},{128,256},{256,384},{384,0},{1,129},{129,257},{257,385},{3... | collective-permute-start | bytes 786440 | tf_op jit(solution)/shard_map/ppermute | solution.py:25
  69.8 15.9 %copy-start.3 = (bf16[512,512]{1,0:T(8,128)(2,1)S(1)}, bf16[512,512]{1,0:T(8,128)(2,1)}, u32[]{:S(2)}) copy-start(bf16[512,512]{1,0:T(8,128)(2,1)} %copy-done.2) | copy-start | bytes 1572868
  69.9 15.9 %collective-permute-start.4 = (bf16[2,320,512]{2,1,0:T(8,128)(2,1)S(1)}, bf16[2,320,512]{2,1,0:T(8,128)(2,1)S(1)}, u32[]{:S(2)}, u32[]{:S(2)}) collective-permute-start(bf16[2,320,512]{2,1,0:T(8,128)(2,1)S(1)} %pad_maximum_fusion.1), channel_id=1, source_target_pairs={{0,4},{4,0},{1,5},{5,1},{2,6},{6,2},{3,7},{7,3},{8,12},{12,8},{9,1... | collective-permute-start | bytes 1966088 | tf_op jit(solution)/shard_map/ppermute | solution.py:20
  79.0 26.3 %collective-permute-start.10 = (bf16[4,256,512]{2,1,0:T(8,128)(2,1)S(1)}, bf16[4,256,512]{2,1,0:T(8,128)(2,1)}, u32[]{:S(2)}, u32[]{:S(2)}) collective-permute-start(bf16[4,256,512]{2,1,0:T(8,128)(2,1)S(1)} %pad_maximum_fusion.own_ref), channel_id=1, source_target_pairs={{0,4},{4,0},{1,5},{5,1},{2,6},{6,2},{3,7},{7,3},{8,12},{12,8},{9,1... | collective-permute-start | bytes 3145736 | tf_op jit(solution)/shard_map/ppermute | solution.py:20
  88.2 14.6 %all-to-all-start.1 = ((bf16[4,144,512]{2,1,0:T(8,128)(2,1)}), bf16[4,144,512]{2,1,0:T(8,128)(2,1)}, u32[]{:S(2)}, u32[]{:S(2)}) async-start(bf16[4,144,512]{2,1,0:T(8,128)(2,1)} %shard_map.48), calls=%async_computation.1 | async-start | bytes 1179648 | tf_op jit(solution)/shard_map/all_to_all | solution.py:399

commit v8 on v6

--- a/solution.py
+++ b/solution.py
@@ -145,12 +145,10 @@
         coarse_ref[:, lanes] = coarse
         held_ref[:rows, lanes] = mean
         held_ref[rows:, lanes] = tile
-        for copy in range(out_ref.shape[0]):
-            send = pltpu.make_async_copy(
-                held_ref.at[:, lanes], out_ref.at[copy, :, lanes], sems.at[head, copy]
-            )
-            send.start()
-            sends.append(send)
+    for copy in range(out_ref.shape[0]):
+        send = pltpu.make_async_copy(held_ref, out_ref.at[copy], sems.at[copy])
+        send.start()
+        sends.append(send)
     for send in sends:
         send.wait()
 
@@ -240,7 +238,7 @@
         ],
         scratch_shapes=[
             pltpu.VMEM((rows + 16, width), jnp.bfloat16),
-            pltpu.SemaphoreType.DMA((width // HEAD_DIM, copies)),
+            pltpu.SemaphoreType.DMA((copies,)),
         ],
     )(queries, keys, values)
 

time: 106 us -> 106 us (level)
  no operation moved by 1% of the time
where the time goes in v8:
time: 106 us
  starting transfers between devices  67.4 us (64%)
  waiting for transfers between devices  19.1 us (18%)
  Pallas kernels  17.6 us (17%)
    ppermute x6, starting transfers between devices, swap(): lax.ppermute(value, axis, [(s, s ^ mask) for s in range(lax.axis_size(axi...  36.4 us
    all_to_all x1, waiting for transfers between devices, body(): far = lax.all_to_all(far, 'head', 0, 0)  10 us
    ppermute x3, starting transfers between devices, shift(): lax.ppermute(value, axis, [(s, (s + step) % size) for s in range(size)])  9.43 us
    ppermute x1, starting transfers between devices, body(): w_across = lax.ppermute(weights, 'z', [(z, across(z)) for z in range(ring)])  8.22 us
    pallas_call x1, Pallas kernels, near_part(): pl.pallas_call(near_kernel, compiler_params=VMEM_LIMIT, out_specs=[pl.Blo...  7.89 us
    all_to_all x1, starting transfers between devices, body(): near = lax.all_to_all(near, 'head', 0, 0)  7.27 us
    ppermute x6, waiting for transfers between devices, swap(): lax.ppermute(value, axis, [(s, s ^ mask) for s in range(lax.axis_size(axi...  5.79 us
    all_to_all x1, starting transfers between devices, body(): far = lax.all_to_all(far, 'head', 0, 0)  4.51 us
  transfers between devices with their start and end apart: 13, of which 4 were waited for; matrix products, arithmetic and copies ran while one was open for 0% of the time, Pallas kernels for 12%

profile of v8, /device:TPU:1, one launch (start us, length us, event | category | flops | bytes accessed | tf_op | source)
XLA Modules:
  0.0 105.5 jit_solution(1035137924627367707)
XLA Ops:
  0.0 0.0 copy-start
  0.0 0.0 copy-start.1
  0.0 0.0 copy-start.2
  0.0 1.5 %collective-permute-start = (bf16[16,512]{1,0:T(8,128)(2,1)}, bf16[16,512]{1,0:T(8,128)(2,1)S(1)}, u32[]{:S(2)}, u32[]{:S(2)}) collective-permute-start(bf16[16,512]{1,0:T(8,128)(2,1)} %bitcast.27), channel_id=1, source_target_pairs={{0,0},{1,128},{2,256},{3,384},{128,1},{129,129},{130,257},{131,385... | collective-permute-start | bytes 49160 | tf_op jit(solution)/shard_map/ppermute | solution.py:358
  1.5 2.8 %shard_map.46 = (bf16[2,128,512]{2,1,0:T(8,128)(2,1)S(1)}, bf16[2,64,512]{2,1,0:T(8,128)(2,1)S(1)}, bf16[2,32,512]{2,1,0:T(8,128)(2,1)S(1)}, bf16[2,16,512]{2,1,0:T(8,128)(2,1)S(1)}) custom-call(bf16[512,512]{1,0:T(8,128)(2,1)} %key_ref.3, bf16[512,512]{1,0:T(8,128)(2,1)} %value_ref.3), custom_call_target="tpu_custom_call" | custom-call | tf_op jit(solution)/shard_map/pallas_call | solution.py:217
  4.3 0.0 collective-permute-done
  4.3 9.6 %collective-permute-start.1 = (bf16[2,24,512]{2,1,0:T(8,128)(2,1)S(1)}, bf16[2,24,512]{2,1,0:T(8,128)(2,1)S(1)}, u32[]{:S(2)}, u32[]{:S(2)}) collective-permute-start(bf16[2,24,512]{2,1,0:T(8,128)(2,1)S(1)} %pad_maximum_fusion.5), channel_id=1, source_target_pairs={{0,32},{8,40},{16,48},{24,56},{32,0},{40,8},{48,16},{56,24},{64,96... | collective-permute-start | bytes 147464 | tf_op jit(solution)/shard_map/ppermute | solution.py:20
  14.0 1.5 %collective-permute-done.1.a_ref = bf16[2,24,512]{2,1,0:T(8,128)(2,1)S(1)} collective-permute-done((bf16[2,24,512]{2,1,0:T(8,128)(2,1)S(1)}, bf16[2,24,512]{2,1,0:T(8,128)(2,1)S(1)}, u32[]{:S(2)}, u32[]{:S(2)}) %collective-permute-start.1) | collective-permute-done | bytes 49184 | tf_op jit(solution)/shard_map/ppermute | solution.py:20
  15.5 6.1 %collective-permute-start.2 = (bf16[2,64,512]{2,1,0:T(8,128)(2,1)S(1)}, bf16[2,64,512]{2,1,0:T(8,128)(2,1)S(1)}, u32[]{:S(2)}, u32[]{:S(2)}) collective-permute-start(bf16[2,64,512]{2,1,0:T(8,128)(2,1)S(1)} %pad_maximum_fusion.3), channel_id=1, source_target_pairs={{0,16},{8,24},{16,0},{24,8},{32,48},{40,56},{48,32},{56,40},{64,80... | collective-permute-start | bytes 393224 | tf_op jit(solution)/shard_map/ppermute | solution.py:20
  21.5 0.0 copy-done
  21.5 0.0 copy-done.1
  21.6 0.0 copy-done.2
  21.6 7.9 %shard_map.47 = (bf16[4,528,512]{2,1,0:T(8,128)(2,1)}, bf16[512,512]{1,0:T(8,128)(2,1)S(1)}) custom-call(bf16[512,512]{1,0:T(8,128)(2,1)S(1)} %copy-done.2, bf16[512,512]{1,0:T(8,128)(2,1)S(1)} %copy-done, bf16[512,512]{1,0:T(8,128)(2,1)S(1)} %copy-done.1), custom_call_target="tpu_custom_call" | custom-call | tf_op jit(solution)/shard_map/pallas_call | solution.py:231
  29.5 0.0 copy-start.3
  29.5 0.8 copy-done.3
  30.3 7.3 %all-to-all-start = ((bf16[4,528,512]{2,1,0:T(8,128)(2,1)}), bf16[4,528,512]{2,1,0:T(8,128)(2,1)S(1)}, u32[]{:S(2)}, u32[]{:S(2)}) async-start(bf16[4,528,512]{2,1,0:T(8,128)(2,1)} %get-tuple-element.18), calls=%async_computation | async-start | bytes 4325376 | tf_op jit(solution)/shard_map/all_to_all | solution.py:365
  37.5 0.0 collective-permute-done.2.b_ref
  37.6 3.5 %collective-permute-start.3 = (bf16[2,160,512]{2,1,0:T(8,128)(2,1)S(1)}, bf16[2,160,512]{2,1,0:T(8,128)(2,1)S(1)}, u32[]{:S(2)}, u32[]{:S(2)}) collective-permute-start(bf16[2,160,512]{2,1,0:T(8,128)(2,1)S(1)} %pad_maximum_fusion.2), channel_id=1, source_target_pairs={{0,8},{8,0},{16,24},{24,16},{32,40},{40,32},{48,56},{56,48},{64,72... | collective-permute-start | bytes 983048 | tf_op jit(solution)/shard_map/ppermute | solution.py:20
  41.2 8.2 %collective-permute-start.4 = (bf16[64,512]{1,0:T(8,128)(2,1)S(1)}, bf16[64,512]{1,0:T(8,128)(2,1)S(1)}, u32[]{:S(2)}, u32[]{:S(2)}) collective-permute-start(bf16[64,512]{1,0:T(8,128)(2,1)S(1)} %pad_maximum_fusion.4), channel_id=1, source_target_pairs={{0,96},{8,104},{16,112},{24,120},{32,64},{40,72},{48,80},{56,88},{... | collective-permute-start | bytes 196616 | tf_op jit(solution)/shard_map/ppermute | solution.py:367
  49.4 3.3 %collective-permute-done.4 = bf16[64,512]{1,0:T(8,128)(2,1)S(1)} collective-permute-done((bf16[64,512]{1,0:T(8,128)(2,1)S(1)}, bf16[64,512]{1,0:T(8,128)(2,1)S(1)}, u32[]{:S(2)}, u32[]{:S(2)}) %collective-permute-start.4) | collective-permute-done | bytes 65568 | tf_op jit(solution)/shard_map/ppermute | solution.py:367
  52.7 1.9 %collective-permute-start.5 = (bf16[64,512]{1,0:T(8,128)(2,1)S(1)}, bf16[64,512]{1,0:T(8,128)(2,1)S(1)}, u32[]{:S(2)}, u32[]{:S(2)}) collective-permute-start(bf16[64,512]{1,0:T(8,128)(2,1)S(1)} %collective-permute-done.4), channel_id=1, source_target_pairs={{0,8},{8,0},{16,24},{24,16},{32,40},{40,32},{48,56},{56,48},{64,72... | collective-permute-start | bytes 196616 | tf_op jit(solution)/shard_map/ppermute | solution.py:20
  54.6 0.0 collective-permute-done.3.c_ref
  54.7 4.3 %collective-permute-done.5 = bf16[64,512]{1,0:T(8,128)(2,1)S(1)} collective-permute-done((bf16[64,512]{1,0:T(8,128)(2,1)S(1)}, bf16[64,512]{1,0:T(8,128)(2,1)S(1)}, u32[]{:S(2)}, u32[]{:S(2)}) %collective-permute-start.5) | collective-permute-done | bytes 65568 | tf_op jit(solution)/shard_map/ppermute | solution.py:20
  59.0 2.9 %collective-permute-start.6 = (bf16[256,512]{1,0:T(8,128)(2,1)S(1)}, bf16[256,512]{1,0:T(8,128)(2,1)S(1)}, u32[]{:S(2)}, u32[]{:S(2)}) collective-permute-start(bf16[256,512]{1,0:T(8,128)(2,1)S(1)} %constant_dynamic-update-slice_fusion), channel_id=1, source_target_pairs={{0,128},{128,256},{256,384},{384,0},{1,129},{129,257},{257,385},{3... | collective-permute-start | bytes 786440 | tf_op jit(solution)/shard_map/ppermute | solution.py:25
  61.9 3.6 %collective-permute-start.7 = (bf16[256,512]{1,0:T(8,128)(2,1)S(1)}, bf16[256,512]{1,0:T(8,128)(2,1)S(1)}, u32[]{:S(2)}, u32[]{:S(2)}) collective-permute-start(bf16[256,512]{1,0:T(8,128)(2,1)S(1)} %constant_dynamic-update-slice_fusion), channel_id=1, source_target_pairs={{0,384},{128,0},{256,128},{384,256},{1,385},{129,1},{257,129},{385... | collective-permute-start | bytes 786440 | tf_op jit(solution)/shard_map/ppermute | solution.py:25
  65.5 3.0 %collective-permute-start.8 = (bf16[256,512]{1,0:T(8,128)(2,1)S(1)}, bf16[256,512]{1,0:T(8,128)(2,1)S(1)}, u32[]{:S(2)}, u32[]{:S(2)}) collective-permute-start(bf16[256,512]{1,0:T(8,128)(2,1)S(1)} %constant_dynamic-update-slice_fusion), channel_id=1, source_target_pairs={{0,256},{128,384},{256,0},{384,128},{1,257},{129,385},{257,1},{385... | collective-permute-start | bytes 786440 | tf_op jit(solution)/shard_map/ppermute | solution.py:25
  68.5 0.0 copy-start.4
  68.6 9.0 %collective-permute-start.9 = (bf16[2,320,512]{2,1,0:T(8,128)(2,1)S(1)}, bf16[2,320,512]{2,1,0:T(8,128)(2,1)S(1)}, u32[]{:S(2)}, u32[]{:S(2)}) collective-permute-start(bf16[2,320,512]{2,1,0:T(8,128)(2,1)S(1)} %pad_maximum_fusion.1), channel_id=1, source_target_pairs={{0,4},{4,0},{1,5},{5,1},{2,6},{6,2},{3,7},{7,3},{8,12},{12,8},{9,1... | collective-permute-start | bytes 1966088 | tf_op jit(solution)/shard_map/ppermute | solution.py:20
  77.6 0.0 collective-permute-done.6
  77.6 0.0 collective-permute-done.7
  77.6 0.0 collective-permute-done.8
  77.6 0.1 pad_maximum_fusion.refs_0_
  77.7 6.3 %collective-permute-start.10 = (bf16[4,256,512]{2,1,0:T(8,128)(2,1)S(1)}, bf16[4,256,512]{2,1,0:T(8,128)(2,1)}, u32[]{:S(2)}, u32[]{:S(2)}) collective-permute-start(bf16[4,256,512]{2,1,0:T(8,128)(2,1)S(1)} %pad_maximum_fusion.refs_0_), channel_id=1, source_target_pairs={{0,4},{4,0},{1,5},{5,1},{2,6},{6,2},{3,7},{7,3},{8,12},{12,8},{9,1... | collective-permute-start | bytes 3145736 | tf_op jit(solution)/shard_map/ppermute | solution.py:20
  84.0 0.0 collective-permute-done.9.d_ref
  84.0 0.0 copy-done.4
  84.0 2.4 %shard_map.48 = bf16[4,144,512]{2,1,0:T(8,128)(2,1)} custom-call(bf16[512,512]{1,0:T(8,128)(2,1)S(1)} %copy-done.4, bf16[2,24,512]{2,1,0:T(8,128)(2,1)S(1)} %collective-permute-done.1.a_ref, bf16[2,64,512]{2,1,0:T(8,128)(2,1)S(1)} %collective-permute-done.2.b_ref, bf16[2,160,512]{2,1,0:T(8,128)(2,1)S(1)} %collective-permute-done.3.c_ref, ...), custom_call_target="tpu_custom_call" | custom-call | tf_op jit(solution)/shard_map/pallas_call | solution.py:252
  86.5 0.0 all-to-all-done.refs_1_
  86.5 4.5 %all-to-all-start.1 = ((bf16[4,144,512]{2,1,0:T(8,128)(2,1)}), bf16[4,144,512]{2,1,0:T(8,128)(2,1)}, u32[]{:S(2)}, u32[]{:S(2)}) async-start(bf16[4,144,512]{2,1,0:T(8,128)(2,1)} %shard_map.48), calls=%async_computation.1 | async-start | bytes 1179648 | tf_op jit(solution)/shard_map/all_to_all | solution.py:376
  91.0 0.1 pad_add_fusion.place_ref
  91.1 0.0 collective-permute-done.10.refs_3_
  91.1 10.0 %all-to-all-done.1.refs_2_ = bf16[4,144,512]{2,1,0:T(8,128)(2,1)} async-done(((bf16[4,144,512]{2,1,0:T(8,128)(2,1)}), bf16[4,144,512]{2,1,0:T(8,128)(2,1)}, u32[]{:S(2)}, u32[]{:S(2)}) %all-to-all-start.1) | async-done | bytes 589856 | tf_op jit(solution)/shard_map/all_to_all | solution.py:376
  101.1 4.5 %shard_map.49 = bf16[512,512]{1,0:T(8,128)(2,1)} custom-call(s32[3]{0:T(128)S(1)} %pad_add_fusion.place_ref, bf16[4,256,512]{2,1,0:T(8,128)(2,1)S(1)} %pad_maximum_fusion.refs_0_, bf16[4,528,512]{2,1,0:T(8,128)(2,1)S(1)} %all-to-all-done.refs_1_, bf16[4,144,512]{2,1,0:T(8,128)(2,1)} %all-to-all-done.1.refs_2_, ...), custom_call_target="tpu_custom_call" | custom-call | tf_op jit(solution)/shard_map/pallas_call | solution.py:334
  (18 shorter events, 0.2 us)
Async XLA Ops:
  0.0 21.5 %copy-start = (bf16[512,512]{1,0:T(8,128)(2,1)S(1)}, bf16[512,512]{1,0:T(8,128)(2,1)}, u32[]{:S(2)}) copy-start(bf16[512,512]{1,0:T(8,128)(2,1)} %key_ref.3) | copy-start | bytes 1572868
  0.0 21.5 %copy-start.1 = (bf16[512,512]{1,0:T(8,128)(2,1)S(1)}, bf16[512,512]{1,0:T(8,128)(2,1)}, u32[]{:S(2)}) copy-start(bf16[512,512]{1,0:T(8,128)(2,1)} %value_ref.3) | copy-start | bytes 1572868
  0.0 21.6 %copy-start.2 = (bf16[512,512]{1,0:T(8,128)(2,1)S(1)}, bf16[512,512]{1,0:T(8,128)(2,1)}, u32[]{:S(2)}) copy-start(bf16[512,512]{1,0:T(8,128)(2,1)} %query_ref.1) | copy-start | bytes 1572868
  0.0 4.3 %collective-permute-start = (bf16[16,512]{1,0:T(8,128)(2,1)}, bf16[16,512]{1,0:T(8,128)(2,1)S(1)}, u32[]{:S(2)}, u32[]{:S(2)}) collective-permute-start(bf16[16,512]{1,0:T(8,128)(2,1)} %bitcast.27), channel_id=1, source_target_pairs={{0,0},{1,128},{2,256},{3,384},{128,1},{129,129},{130,257},{131,385... | collective-permute-start | bytes 49160 | tf_op jit(solution)/shard_map/ppermute | solution.py:358
  4.3 11.1 %collective-permute-start.1 = (bf16[2,24,512]{2,1,0:T(8,128)(2,1)S(1)}, bf16[2,24,512]{2,1,0:T(8,128)(2,1)S(1)}, u32[]{:S(2)}, u32[]{:S(2)}) collective-permute-start(bf16[2,24,512]{2,1,0:T(8,128)(2,1)S(1)} %pad_maximum_fusion.5), channel_id=1, source_target_pairs={{0,32},{8,40},{16,48},{24,56},{32,0},{40,8},{48,16},{56,24},{64,96... | collective-permute-start | bytes 147464 | tf_op jit(solution)/shard_map/ppermute | solution.py:20
  15.5 22.1 %collective-permute-start.2 = (bf16[2,64,512]{2,1,0:T(8,128)(2,1)S(1)}, bf16[2,64,512]{2,1,0:T(8,128)(2,1)S(1)}, u32[]{:S(2)}, u32[]{:S(2)}) collective-permute-start(bf16[2,64,512]{2,1,0:T(8,128)(2,1)S(1)} %pad_maximum_fusion.3), channel_id=1, source_target_pairs={{0,16},{8,24},{16,0},{24,8},{32,48},{40,56},{48,32},{56,40},{64,80... | collective-permute-start | bytes 393224 | tf_op jit(solution)/shard_map/ppermute | solution.py:20
  29.5 0.8 copy-start.3
  30.3 56.2 %all-to-all-start = ((bf16[4,528,512]{2,1,0:T(8,128)(2,1)}), bf16[4,528,512]{2,1,0:T(8,128)(2,1)S(1)}, u32[]{:S(2)}, u32[]{:S(2)}) async-start(bf16[4,528,512]{2,1,0:T(8,128)(2,1)} %get-tuple-element.18), calls=%async_computation | async-start | bytes 4325376 | tf_op jit(solution)/shard_map/all_to_all | solution.py:365
  37.6 17.0 %collective-permute-start.3 = (bf16[2,160,512]{2,1,0:T(8,128)(2,1)S(1)}, bf16[2,160,512]{2,1,0:T(8,128)(2,1)S(1)}, u32[]{:S(2)}, u32[]{:S(2)}) collective-permute-start(bf16[2,160,512]{2,1,0:T(8,128)(2,1)S(1)} %pad_maximum_fusion.2), channel_id=1, source_target_pairs={{0,8},{8,0},{16,24},{24,16},{32,40},{40,32},{48,56},{56,48},{64,72... | collective-permute-start | bytes 983048 | tf_op jit(solution)/shard_map/ppermute | solution.py:20
  41.2 11.5 %collective-permute-start.4 = (bf16[64,512]{1,0:T(8,128)(2,1)S(1)}, bf16[64,512]{1,0:T(8,128)(2,1)S(1)}, u32[]{:S(2)}, u32[]{:S(2)}) collective-permute-start(bf16[64,512]{1,0:T(8,128)(2,1)S(1)} %pad_maximum_fusion.4), channel_id=1, source_target_pairs={{0,96},{8,104},{16,112},{24,120},{32,64},{40,72},{48,80},{56,88},{... | collective-permute-start | bytes 196616 | tf_op jit(solution)/shard_map/ppermute | solution.py:367
  52.7 6.3 %collective-permute-start.5 = (bf16[64,512]{1,0:T(8,128)(2,1)S(1)}, bf16[64,512]{1,0:T(8,128)(2,1)S(1)}, u32[]{:S(2)}, u32[]{:S(2)}) collective-permute-start(bf16[64,512]{1,0:T(8,128)(2,1)S(1)} %collective-permute-done.4), channel_id=1, source_target_pairs={{0,8},{8,0},{16,24},{24,16},{32,40},{40,32},{48,56},{56,48},{64,72... | collective-permute-start | bytes 196616 | tf_op jit(solution)/shard_map/ppermute | solution.py:20
  59.0 18.6 %collective-permute-start.6 = (bf16[256,512]{1,0:T(8,128)(2,1)S(1)}, bf16[256,512]{1,0:T(8,128)(2,1)S(1)}, u32[]{:S(2)}, u32[]{:S(2)}) collective-permute-start(bf16[256,512]{1,0:T(8,128)(2,1)S(1)} %constant_dynamic-update-slice_fusion), channel_id=1, source_target_pairs={{0,128},{128,256},{256,384},{384,0},{1,129},{129,257},{257,385},{3... | collective-permute-start | bytes 786440 | tf_op jit(solution)/shard_map/ppermute | solution.py:25
  61.9 15.6 %collective-permute-start.7 = (bf16[256,512]{1,0:T(8,128)(2,1)S(1)}, bf16[256,512]{1,0:T(8,128)(2,1)S(1)}, u32[]{:S(2)}, u32[]{:S(2)}) collective-permute-start(bf16[256,512]{1,0:T(8,128)(2,1)S(1)} %constant_dynamic-update-slice_fusion), channel_id=1, source_target_pairs={{0,384},{128,0},{256,128},{384,256},{1,385},{129,1},{257,129},{385... | collective-permute-start | bytes 786440 | tf_op jit(solution)/shard_map/ppermute | solution.py:25
  65.5 12.1 %collective-permute-start.8 = (bf16[256,512]{1,0:T(8,128)(2,1)S(1)}, bf16[256,512]{1,0:T(8,128)(2,1)S(1)}, u32[]{:S(2)}, u32[]{:S(2)}) collective-permute-start(bf16[256,512]{1,0:T(8,128)(2,1)S(1)} %constant_dynamic-update-slice_fusion), channel_id=1, source_target_pairs={{0,256},{128,384},{256,0},{384,128},{1,257},{129,385},{257,1},{385... | collective-permute-start | bytes 786440 | tf_op jit(solution)/shard_map/ppermute | solution.py:25
  68.5 15.5 %copy-start.4 = (bf16[512,512]{1,0:T(8,128)(2,1)S(1)}, bf16[512,512]{1,0:T(8,128)(2,1)}, u32[]{:S(2)}) copy-start(bf16[512,512]{1,0:T(8,128)(2,1)} %copy-done.3) | copy-start | bytes 1572868
  68.6 15.4 %collective-permute-start.9 = (bf16[2,320,512]{2,1,0:T(8,128)(2,1)S(1)}, bf16[2,320,512]{2,1,0:T(8,128)(2,1)S(1)}, u32[]{:S(2)}, u32[]{:S(2)}) collective-permute-start(bf16[2,320,512]{2,1,0:T(8,128)(2,1)S(1)} %pad_maximum_fusion.1), channel_id=1, source_target_pairs={{0,4},{4,0},{1,5},{5,1},{2,6},{6,2},{3,7},{7,3},{8,12},{12,8},{9,1... | collective-permute-start | bytes 1966088 | tf_op jit(solution)/shard_map/ppermute | solution.py:20
  77.7 13.3 %collective-permute-start.10 = (bf16[4,256,512]{2,1,0:T(8,128)(2,1)S(1)}, bf16[4,256,512]{2,1,0:T(8,128)(2,1)}, u32[]{:S(2)}, u32[]{:S(2)}) collective-permute-start(bf16[4,256,512]{2,1,0:T(8,128)(2,1)S(1)} %pad_maximum_fusion.refs_0_), channel_id=1, source_target_pairs={{0,4},{4,0},{1,5},{5,1},{2,6},{6,2},{3,7},{7,3},{8,12},{12,8},{9,1... | collective-permute-start | bytes 3145736 | tf_op jit(solution)/shard_map/ppermute | solution.py:20
  86.5 14.6 %all-to-all-start.1 = ((bf16[4,144,512]{2,1,0:T(8,128)(2,1)}), bf16[4,144,512]{2,1,0:T(8,128)(2,1)}, u32[]{:S(2)}, u32[]{:S(2)}) async-start(bf16[4,144,512]{2,1,0:T(8,128)(2,1)} %shard_map.48), calls=%async_computation.1 | async-start | bytes 1179648 | tf_op jit(solution)/shard_map/all_to_all | solution.py:376
